TPU v7x, 256 devices: a whole 4x4x8 slice. The times are simulated.
256 devices in a mesh: grp: 2 (over z_lo), tok: 64 (over y, x, z_hi), sub: 2 (over core).
Axes of the slice: x: 4, y: 4, z: 8 (z_hi: 4, z_lo: 2; z = z_hi * 2 + z_lo), core: 2. Of those that a mesh axis runs over, the one named last changes fastest.
Arguments:
- patches: bfloat16 [32768, 1408], P(('grp', 'tok')), may hold values from -6 to 6
- image_sizes: int32 [128, 4], P(('grp', 'tok')), may hold values from 1 to 32, 64 in all within a row
- vision_inproj: bfloat16 [1408, 2, 3, 704], P('tok', 'sub'), may hold values from -0.15625 to 0.15625
- vision_outproj: bfloat16 [1408, 1408], P('sub', 'tok'), may hold values from -0.625 to 0.625
- merger_weight: bfloat16 [5632, 1408], P('tok', 'sub'), may hold values from -0.078125 to 0.078125
- text_embed: bfloat16 [16384, 1408], P(('grp', 'tok')), may hold values from -6 to 6
- image_positions: int32 [2, 4096], P('grp', 'tok'), may hold values from 0 to 8191, as said below
- prompt_lengths: int32 [2, 2], P('grp'), may hold values from 1 to 8064, 8192 in all within a row
- decoder_inproj: bfloat16 [1408, 2, 3, 704], P(('grp', 'tok'), 'sub'), may hold values from -0.15625 to 0.15625
- decoder_outproj: bfloat16 [1408, 1408], P('sub', ('grp', 'tok')), may hold values from -0.625 to 0.625
Outputs:
- text_update: bfloat16 [16384, 1408], P(('grp', 'tok', 'sub'))
Inputs may be any that keep to these rules, and one draw needn't show every extreme that they name: `image_positions`: within each half the positions are distinct. Of the 64 merged tokens of one piece, at most 2 go to positions of any one block of 128 positions, and some reach that number. `image_sizes`: each row sums to 64. `prompt_lengths`: each row sums to 8192.
All inputs are finite; a program needn't handle non-finite values.
Results may differ from a plain program's by a relative error of at most 0.03.
Values may be sent and summed in bfloat16 or wider, within the bound.
No kernel may reach another device: no remote copies, remote signals or barrier semaphores. Data moves between devices by JAX's collectives and lax.ppermute only.
A program may use at most 128 MiB of HBM per device.

v0:
```python
import math

import jax
import jax.numpy as jnp
from jax import lax
from jax.sharding import PartitionSpec as P

HD = 88
REACH = 3


norm_eps = 1e-06


def passed_along(block, axis, distance):
    devices = range(lax.axis_size(axis))
    route = [(i - distance, i) for i in devices if i - distance in devices]
    return lax.ppermute(block, axis, route)


def layer_norm(values):
    center = values - jnp.mean(values, axis=-1, keepdims=True)
    spread = jnp.mean(center * center, axis=-1, keepdims=True)
    return center * lax.rsqrt(spread + norm_eps)


def softmax_heads(queries, keys_all, values_all, allowed):
    scores = jnp.einsum("qhe,khe->hqk", queries, keys_all, preferred_element_type=jnp.float32) * (
        1.0 / math.sqrt(HD)
    )
    weights_raw = jnp.exp(scores) * allowed[None]
    weights = (weights_raw / jnp.sum(weights_raw, axis=-1, keepdims=True)).astype(jnp.bfloat16)
    mixture = jnp.einsum("hqk,khe->qhe", weights, values_all, preferred_element_type=jnp.float32)
    return mixture.astype(jnp.bfloat16)


def attend_blocks(queries, keys_all, values_all, allowed):
    row_total, head_count, head_size = queries.shape
    block_rows = min(row_total, 512)
    block_count = row_total // block_rows
    query_blocks = queries.reshape(block_count, block_rows, head_count, head_size)
    allow_blocks = allowed.reshape(block_count, block_rows, allowed.shape[1])
    outputs = lax.map(
        lambda block_pair: softmax_heads(block_pair[0], keys_all, values_all, block_pair[1]),
        (query_blocks, allow_blocks),
    )
    return outputs.reshape(row_total, head_count * head_size)


def shards(
    patches,
    image_sizes,
    vision_inproj,
    vision_outproj,
    merger_weight,
    text_embed,
    image_positions,
    prompt_lengths,
    decoder_inproj,
    decoder_outproj,
):
    inproj_full, outproj_full, merger_full = (
        lax.all_gather(vision_inproj, "tok", axis=0, tiled=True),
        lax.all_gather(vision_outproj, "tok", axis=1, tiled=True),
        lax.all_gather(merger_weight, "tok", axis=0, tiled=True),
    )
    patch_count, width = patches.shape
    half_width = inproj_full.shape[3]
    head_local = half_width // HD
    patch_rows = patches.astype(jnp.float32)
    normed = layer_norm(patch_rows).astype(jnp.bfloat16)
    projected = jnp.dot(
        normed, inproj_full.reshape(width, 3 * half_width), preferred_element_type=jnp.float32
    )
    triple = projected.astype(jnp.bfloat16).reshape(patch_count, 3, head_local, HD)
    image_ends = jnp.cumsum(image_sizes[0])
    group_ids = jnp.arange(patch_count, dtype=jnp.int32) // 4
    image_ids = jnp.sum((group_ids[:, None] >= image_ends[None, :]).astype(jnp.int32), axis=1)
    same_image = (image_ids[:, None] == image_ids[None, :]).astype(jnp.float32)
    heads_out = attend_blocks(triple[:, 0], triple[:, 1], triple[:, 2], same_image)
    partial_value = jnp.dot(heads_out, outproj_full, preferred_element_type=jnp.float32)
    hidden = patch_rows + lax.psum(partial_value.astype(jnp.bfloat16), "sub").astype(jnp.float32)
    merged = layer_norm(hidden).astype(jnp.bfloat16).reshape(patch_count // 4, 4 * width)
    piece_count = lax.axis_size("tok")
    capacity = patch_count // (2 * piece_count)
    piece_rows = text_embed.shape[0]
    targets = image_positions[0]
    target_chip = targets // piece_rows
    target_row = targets % piece_rows
    chip_hits = (target_chip[:, None] == jnp.arange(piece_count, dtype=jnp.int32)[None, :]).astype(
        jnp.int32
    )
    slot_index = jnp.sum((jnp.cumsum(chip_hits, axis=0) - chip_hits) * chip_hits, axis=1)
    row_buffer = (
        jnp.full((piece_count, capacity), piece_rows, jnp.int32)
        .at[target_chip, slot_index]
        .set(target_row)
    )
    embedded = jnp.dot(merged, merger_full, preferred_element_type=jnp.float32).astype(jnp.bfloat16)
    narrow_rows = lax.all_to_all(
        jnp.zeros((piece_count, capacity, embedded.shape[1]), embedded.dtype)
        .at[target_chip, slot_index]
        .set(embedded),
        "tok",
        split_axis=0,
        concat_axis=0,
        tiled=True,
    )
    arrived_rows = lax.all_to_all(row_buffer, "tok", split_axis=0, concat_axis=0, tiled=True)
    image_half = narrow_rows.reshape(piece_count * capacity, half_width)
    image_full = lax.all_gather(image_half, "sub", axis=1, tiled=True)
    decoder_input = text_embed.at[arrived_rows.reshape(-1)].set(image_full, mode="drop")
    text_inproj, text_outproj = (
        lax.all_gather(decoder_inproj, ("grp", "tok"), axis=0, tiled=True),
        lax.all_gather(decoder_outproj, ("grp", "tok"), axis=1, tiled=True),
    )
    normed_text = layer_norm(decoder_input.astype(jnp.float32)).astype(jnp.bfloat16)
    text_proj = jnp.dot(
        normed_text, text_inproj.reshape(width, 3 * half_width), preferred_element_type=jnp.float32
    )
    text_triple = text_proj.astype(jnp.bfloat16).reshape(piece_rows, 3, head_local, HD)
    own_pair = text_triple[:, 1:].reshape(piece_rows, 2 * half_width)
    earlier = [own_pair]
    carried = own_pair
    for step_back in range(REACH):
        carried = passed_along(carried, "tok", 1)
        earlier.append(carried)
    window = jnp.concatenate(earlier[::-1], axis=0).reshape(
        (REACH + 1) * piece_rows, 2, head_local, HD
    )
    piece_id = lax.axis_index("tok")
    query_pos = piece_id * piece_rows + jnp.arange(piece_rows, dtype=jnp.int32)
    key_pos = (piece_id - REACH) * piece_rows + jnp.arange(
        (REACH + 1) * piece_rows, dtype=jnp.int32
    )
    lengths = prompt_lengths[0]
    starts = jnp.cumsum(lengths) - lengths
    query_start = jnp.max(
        jnp.where(starts[None, :] <= query_pos[:, None], starts[None, :], 0), axis=1
    )
    allowed = (
        (key_pos[None, :] <= query_pos[:, None]) & (key_pos[None, :] >= query_start[:, None])
    ).astype(jnp.float32)
    text_heads = attend_blocks(text_triple[:, 0], window[:, 0], window[:, 1], allowed)
    text_partial = jnp.dot(text_heads, text_outproj, preferred_element_type=jnp.float32)
    return lax.psum_scatter(
        text_partial.astype(jnp.bfloat16), "sub", scatter_dimension=0, tiled=True
    )


def solution(mesh):
    placed = (
        P(("grp", "tok"), None),
        P(("grp", "tok"), None),
        P("tok", "sub", None, None),
        P("sub", "tok"),
        P("tok", "sub"),
        P(("grp", "tok"), None),
        P("grp", "tok"),
        P("grp", None),
        P(("grp", "tok"), "sub", None, None),
        P("sub", ("grp", "tok")),
    )
    return jax.shard_map(
        shards,
        mesh=mesh,
        in_specs=placed,
        out_specs=P(("grp", "tok", "sub"), None),
        check_vma=False,
    )
```

profile of v0, /device:TPU:1, one launch (start us, length us, event | category | flops | bytes accessed | tf_op | source)
XLA Modules:
  0.0 1940.3 jit_solution(17972249292921718679)
XLA Ops:
  7.3 1.6 copy.25
  9.9 1.3 convert_reduce_fusion
  11.7 80.6 %all-gather.14.cloned.1.call-done = bf16[64,22,704]{2,1,0:T(8,128)(2,1)} async-done(((bf16[1,22,704]{2,1,0:T(8,128)(2,1)}), bf16[64,22,704]{2,1,0:T(8,128)(2,1)}) %all-gather.14.cloned.1.call-update) | async-done | bytes 1982480 | tf_op jit(solution)/shard_map/all_gather | solution.py:64
  92.2 2.9 reshape.303
  95.2 108.4 %all-gather.8.cloned.1.call-done = bf16[1408,1,3,704]{3,2,1,0:T(4,128)(2,1)} async-done(((bf16[22,1,3,704]{3,2,1,0:T(4,128)(2,1)}), bf16[1408,1,3,704]{3,2,1,0:T(4,128)(2,1)}) %all-gather.8.cloned.1.call-update) | async-done | bytes 5947408 | tf_op jit(solution)/shard_map/all_gather | solution.py:63
  203.6 14.1 copy.26
  217.7 4.7 convolution_convert_fusion
  223.6 1.7 convolution_convert_fusion.2
  227.0 3.5 scatter_fusion
  231.2 17.0 all-to-all-start
  248.8 13.0 all-reduce.2.cloned.1.call-done
  261.8 1.5 fusion.7
  263.3 1.5 multiply_reduce_fusion
  265.6 109.0 %all-gather.10.cloned.1.call-done = bf16[5632,704]{1,0:T(8,128)(2,1)} async-done(((bf16[88,704]{1,0:T(8,128)(2,1)}), bf16[5632,704]{1,0:T(8,128)(2,1)}) %all-gather.10.cloned.1.call-update) | async-done | bytes 7929872 | tf_op jit(solution)/shard_map/all_gather | solution.py:65
  374.6 5.1 convolution_convert_fusion.6
  380.5 8.6 scatter_fusion.1
  389.0 17.0 all-to-all-start.1
  407.7 558.9 %all-gather.12.cloned.1.call-done = bf16[1408,1,3,704]{3,2,1,0:T(4,128)(2,1)} async-done(((bf16[11,1,3,704]{3,2,1,0:T(4,128)(2,1)}), bf16[1408,1,3,704]{3,2,1,0:T(4,128)(2,1)}) %all-gather.12.cloned.1.call-update) | async-done | bytes 5947408 | tf_op jit(solution)/shard_map/all_gather | solution.py:114
  966.6 14.1 copy.30
  981.0 89.4 %all_gather.21 = bf16[128,1408]{0,1:T(8,128)(2,1)S(1)} all-gather(bf16[128,704]{0,1:T(8,128)(2,1)S(1)} %copy.28), channel_id=1, replica_groups=mesh['grp'=2,'tok'=64,'sub'=2] {'sub'}, dimensions={1}, use_global_device_ids=true | all-gather | bytes 540672 | tf_op jit(solution)/shard_map/all_gather | solution.py:111
  1070.6 1.4 scatter_fusion.2
  1072.4 4.5 convolution_convert_fusion.1
  1076.9 1.9 collective-permute-start
  1078.8 7.5 collective-permute-done
  1086.3 5.7 collective-permute-start.1
  1092.2 5.3 collective-permute-done.1
  1097.5 6.0 collective-permute-start.2
  1103.7 621.7 %all-gather.16.cloned.1.call-done = bf16[128,11,704]{2,1,0:T(8,128)(2,1)} async-done(((bf16[1,11,704]{2,1,0:T(8,128)(2,1)}), bf16[128,11,704]{2,1,0:T(8,128)(2,1)}) %all-gather.16.cloned.1.call-update) | async-done | bytes 1982480 | tf_op jit(solution)/shard_map/all_gather | solution.py:115
  1725.4 3.3 reshape.305
  1728.7 1.4 pad_maximum_fusion
  1731.5 1.6 convolution_convert_fusion.3
  1733.1 200.4 %reduce-scatter.2.cloned.1.call-done = bf16[64,1408]{1,0:T(8,128)(2,1)} async-done(((bf16[128,1408]{1,0:T(8,128)(2,1)}), bf16[64,1408]{1,0:T(8,128)(2,1)}) %reduce-scatter.2.cloned.1.call-update) | async-done | bytes 180240 | tf_op jit(solution)/shard_map/reduce_scatter | solution.py:146
  (70 shorter events, 12.2 us)
Async XLA Ops:
  6.5 4.7 copy-start.1
  6.5 85.7 %all-gather.14.cloned.1.call-start = ((), (), s32[]{:S(2)}) async-start(), calls=%async_computation.8 | async-start | bytes 2396160 | tf_op jit(solution)/shard_map/all_gather | solution.py:64
  7.3 196.3 %all-gather.8.cloned.1.call-start = ((), (), s32[]{:S(2)}) async-start(), calls=%async_computation.3 | async-start | bytes 8785920 | tf_op jit(solution)/shard_map/all_gather | solution.py:63
  8.9 252.9 %all-reduce.2.cloned.1.call-start = ((), (), s32[]{:S(2)}) async-start(), calls=%async_computation.4 | async-start | bytes 1441792 | tf_op jit(solution)/shard_map/psum | solution.py:82
  223.6 2.9 copy-start.4
  225.4 149.3 %all-gather.10.cloned.1.call-start = ((), (), s32[]{:S(2)}) async-start(), calls=%async_computation.5 | async-start | bytes 8785920 | tf_op jit(solution)/shard_map/all_gather | solution.py:65
  226.0 740.6 %all-gather.12.cloned.1.call-start = ((), (), s32[]{:S(2)}) async-start(), calls=%async_computation.6 | async-start | bytes 8718336 | tf_op jit(solution)/shard_map/all_gather | solution.py:114
  231.2 157.9 %all-to-all-start = ((s32[64,1,2]{2,1,0:T(1,128)}), s32[64,1,2]{2,1,0:T(1,128)S(1)}, u32[]{:S(2)}, u32[]{:S(2)}) async-start(s32[64,1,2]{2,1,0:T(1,128)} %copy.24), calls=%async_computation | async-start | bytes 65536 | tf_op jit(solution)/shard_map/all_to_all | solution.py:109
  248.2 1477.2 %all-gather.16.cloned.1.call-start = ((), (), s32[]{:S(2)}) async-start(), calls=%async_computation.9 | async-start | bytes 3170304 | tf_op jit(solution)/shard_map/all_gather | solution.py:115
  261.8 3.0 copy-start.2
  389.0 591.7 %all-to-all-start.1 = ((bf16[64,2,704]{2,1,0:T(2,128)(2,1)}), bf16[64,2,704]{2,1,0:T(2,128)(2,1)S(1)}, u32[]{:S(2)}, u32[]{:S(2)}) async-start(bf16[64,2,704]{2,1,0:T(2,128)(2,1)} %scatter_fusion.1), calls=%async_computation.1 | async-start | bytes 393216 | tf_op jit(solution)/shard_map/all_to_all | solution.py:100
  406.1 1527.4 %reduce-scatter.2.cloned.1.call-start = ((), (), s32[]{:S(2)}) async-start(), calls=%async_computation.7 | async-start | bytes 540672 | tf_op jit(solution)/shard_map/reduce_scatter | solution.py:146
  980.7 89.9 %copy-start = (bf16[128,1408]{1,0:T(8,128)(2,1)S(1)}, bf16[128,1408]{1,0:T(8,128)(2,1)}, u32[]{:S(2)}) copy-start(bf16[128,1408]{1,0:T(8,128)(2,1)} %param.15) | copy-start | bytes 1081348
  1072.4 19.7 %copy-start.5 = (s32[1,2]{1,0:T(1,128)S(1)}, s32[1,2]{1,0:T(1,128)}, u32[]{:S(2)}) copy-start(s32[1,2]{1,0:T(1,128)} %param.17) | copy-start | bytes 28
  1076.9 9.4 collective-permute-start
  1086.3 17.4 copy-start.3
  1086.3 11.2 collective-permute-start.1
  1097.5 631.2 %collective-permute-start.2 = (bf16[128,1408]{0,1:T(8,128)(2,1)}, bf16[128,1408]{0,1:T(8,128)(2,1)}, u32[]{:S(2)}, u32[]{:S(2)}) collective-permute-start(bf16[128,1408]{0,1:T(8,128)(2,1)} %collective-permute-done.1), channel_id=1, source_target_pairs={{0,2},{2,4},{4,6},{6,8},{8,10},{10,12},{12,14},{14,16},{16,18},{18... | collective-permute-start | bytes 1081352 | tf_op jit(solution)/shard_map/ppermute | solution.py:18
Sparse Core Ops, SparseCore 0:
  10.6 81.5 all-gather.13
  95.5 108.0 all-gather.7
  225.5 36.2 all-reduce.1
  265.4 109.1 all-gather.9
  376.4 590.1 all-gather.11
  968.4 756.9 all-gather.15
  1733.2 200.1 reduce-scatter.1
where the time goes:
time: 1940 us
  waiting for transfers between devices  1710 us (88%)
  blocking collectives  89.4 us (5%)
  local copies, waits for them, and re-layouts  52.7 us (3%)
  starting transfers between devices  48.1 us (2%)
  matrix products  20.2 us (1%)
    all_gather x1, waiting for transfers between devices, shards(): lax.all_gather(decoder_outproj, ('grp', 'tok'), axis=1, tiled=True)  622 us
    all_gather x1, waiting for transfers between devices, shards(): lax.all_gather(decoder_inproj, ('grp', 'tok'), axis=0, tiled=True)  559 us
    reduce_scatter x1, waiting for transfers between devices, shards(): lax.psum_scatter(text_partial.astype(jnp.bfloat16), 'sub', scatter_dimens...  200 us
    all_gather x1, waiting for transfers between devices, shards(): lax.all_gather(merger_weight, 'tok', axis=0, tiled=True)  109 us
    all_gather x1, waiting for transfers between devices, shards(): lax.all_gather(vision_inproj, 'tok', axis=0, tiled=True)  108 us
    all_gather x1, blocking collectives, shards(): image_full = lax.all_gather(image_half, 'sub', axis=1, tiled=True)  89.4 us
    all_gather x1, waiting for transfers between devices, shards(): lax.all_gather(vision_outproj, 'tok', axis=1, tiled=True)  80.6 us
  transfers between devices with their start and end apart: 12, of which 9 were waited for; matrix products, arithmetic and copies ran while one was open for 3% of the time, Pallas kernels for 0%

commit v1 on v0

v1 whole, which is shorter than its diff:
```python
import math

import jax
import jax.numpy as jnp
from jax import lax
from jax.sharding import Mesh
from jax.sharding import PartitionSpec as P

HD = 88
REACH = 3
EPS = 1e-06
TOK = ("y", "x", "zh")
PLANE = ("y", "x")
BF = jnp.bfloat16
F32 = jnp.float32


def layer_norm(values):
    center = values - jnp.mean(values, axis=-1, keepdims=True)
    spread = jnp.mean(center * center, axis=-1, keepdims=True)
    return center * lax.rsqrt(spread + EPS)


def softmax_weights(scores, allowed):
    raw = jnp.exp(scores * (1.0 / math.sqrt(HD))) * allowed
    return (raw / jnp.sum(raw, axis=-1, keepdims=True)).astype(BF)


def after(value, *others):
    return lax.optimization_barrier((value, *others))[0]


def swap_sub(value):
    return lax.ppermute(value, "sub", [(0, 1), (1, 0)])


def dot(a, b):
    return jnp.dot(a, b, preferred_element_type=F32)


def to_all(value, axes):
    count = lax.axis_size(axes)
    spread = jnp.broadcast_to(value[None], (count,) + value.shape)
    return lax.all_to_all(spread, axes, split_axis=0, concat_axis=0, tiled=True)


def shards(
    patches,
    image_sizes,
    vision_inproj,
    vision_outproj,
    merger_weight,
    text_embed,
    image_positions,
    prompt_lengths,
    decoder_inproj,
    decoder_outproj,
):
    lines = lax.axis_size("zh")
    planes = lax.axis_size(PLANE)
    pieces = lax.axis_size(TOK)
    rows_v, width = patches.shape
    half = vision_inproj.shape[3]
    quarter = half // lines
    heads_line = quarter // HD
    krows = vision_inproj.shape[0]
    mrows = merger_weight.shape[0]

    vin = vision_inproj.reshape(krows, 3, lines, quarter).transpose(2, 0, 1, 3)
    vin = vin.reshape(lines, krows, 3 * quarter)
    vin = jnp.pad(vin, ((0, 0), (0, 0), (0, half - 3 * quarter)))
    rest = jnp.concatenate([vision_outproj.T, merger_weight], axis=0)
    rest = jnp.broadcast_to(rest[None], (lines,) + rest.shape)
    line_v = lax.all_to_all(
        jnp.concatenate([vin, rest], axis=1), "zh", split_axis=0, concat_axis=0, tiled=True
    )
    line_v = jnp.concatenate(
        [
            line_v[:, :krows].reshape(lines * krows, half),
            line_v[:, krows : 2 * krows].reshape(lines * krows, half),
            line_v[:, 2 * krows :].reshape(lines * mrows, half),
        ],
        axis=0,
    )
    full_v = lax.all_gather(line_v, PLANE, axis=0, tiled=False)
    kline = lines * krows
    w_in = full_v[:, :kline].reshape(width, half)
    w_out = full_v[:, kline : 2 * kline].reshape(width, half)
    w_merge = full_v[:, 2 * kline :].reshape(planes * lines * mrows, half)

    drows = decoder_inproj.shape[0]
    dec = jnp.concatenate([decoder_inproj.reshape(drows, 3 * half), decoder_outproj.T], axis=1)
    dec = after(dec, line_v)
    line_d = to_all(dec, ("grp", "zh")).reshape(-1, 4 * half)
    full_d = lax.all_gather(line_d, PLANE, axis=0, tiled=True)
    fan = lines * drows
    order = jnp.arange(width, dtype=jnp.int32)
    natural = (
        (order // fan) % 2 * (width // 2) + order // (2 * fan) * fan + order % fan
    )
    reorder = (natural[None, :] == order[:, None]).astype(BF)

    piece_rows = text_embed.shape[0]
    reach = REACH + 1
    cap = rows_v // (2 * pieces)
    slots = reach * cap
    targets = image_positions[0]
    target_piece = targets // piece_rows
    target_row = targets % piece_rows
    hits = (target_piece[:, None] == jnp.arange(pieces, dtype=jnp.int32)[None, :]).astype(jnp.int32)
    slot = jnp.sum((jnp.cumsum(hits, axis=0) - hits) * hits, axis=1)
    dest = jnp.arange(pieces * slots, dtype=jnp.int32)
    back = dest // cap % reach
    wanted = (dest // slots)[:, None] - back[:, None] == target_piece[None, :]
    wanted = wanted & ((dest % cap)[:, None] == slot[None, :])
    window_row = (REACH - back)[:, None] * piece_rows + target_row[None, :]
    window_rows = reach * piece_rows
    row_list = jnp.min(jnp.where(wanted, window_row, window_rows), axis=1)
    row_list = after(row_list.reshape(pieces, slots), line_d)
    arrived = lax.all_to_all(row_list, TOK, split_axis=0, concat_axis=0, tiled=True).reshape(-1)
    place = jnp.arange(window_rows, dtype=jnp.int32)[:, None] == arrived[None, :]

    patch_rows = patches.astype(F32)
    ends = jnp.cumsum(image_sizes[0]).astype(BF)
    mark = jnp.zeros((16, width), BF).at[0, : ends.shape[0]].set(ends)
    own = jnp.concatenate([layer_norm(patch_rows).astype(BF), mark], axis=0)
    own = after(own, arrived)
    moved = [
        lax.ppermute(own, "zh", [(i, (i + s) % lines) for i in range(lines)])
        for s in range(1, lines)
    ]
    text = after(text_embed, moved[0])
    earlier = [
        lax.ppermute(text, TOK, [(i, i + s) for i in range(pieces - s)])
        for s in range(REACH, 0, -1)
    ]
    window_text = jnp.concatenate(earlier + [text_embed], axis=0)

    both = jnp.stack([own] + moved)
    normed = both[:, :rows_v].reshape(lines * rows_v, width)
    ends_all = both[:, rows_v, : ends.shape[0]].astype(jnp.int32)
    group_ids = jnp.arange(rows_v, dtype=jnp.int32) // 4
    image_ids = jnp.sum(
        (group_ids[None, :, None] >= ends_all[:, None, :]).astype(jnp.int32), axis=2
    )
    same = (image_ids[:, :, None] == image_ids[:, None, :]).astype(F32)
    projected = dot(normed, w_in)[:, : 3 * quarter].astype(BF)
    triple = projected.reshape(lines, rows_v, 3, heads_line, HD)
    scores = jnp.einsum(
        "pqhe,pkhe->phqk", triple[:, :, 0], triple[:, :, 1], preferred_element_type=F32
    )
    weights = softmax_weights(scores, same[:, None])
    heads = jnp.einsum("phqk,pkhe->pqhe", weights, triple[:, :, 2], preferred_element_type=F32)
    heads = heads.astype(BF).reshape(lines, rows_v, quarter)
    me = lax.axis_index("zh")
    heads = jnp.roll(heads[::-1], me + 1, axis=0)
    heads = lax.all_to_all(heads, "zh", split_axis=0, concat_axis=0, tiled=True)
    heads = heads.transpose(1, 0, 2).reshape(rows_v, half)
    partial = lax.dot_general(heads, w_out, (((1,), (1,)), ((), ())), preferred_element_type=F32)
    partial = partial.astype(BF)
    hidden = patch_rows + (partial.astype(F32) + swap_sub(partial).astype(F32))
    merged = layer_norm(hidden).astype(BF).reshape(rows_v // 4, 4 * width)
    embedded = dot(merged, w_merge).astype(BF)

    sent = dot(wanted.astype(BF), embedded).astype(BF).reshape(pieces, slots, half)
    got = lax.all_to_all(sent, TOK, split_axis=0, concat_axis=0, tiled=True)
    got = got.reshape(pieces * slots, half)
    other = swap_sub(got)
    first = lax.axis_index("sub") == 0
    image_full = jnp.concatenate(
        [jnp.where(first, got, other), jnp.where(first, other, got)], axis=1
    )
    placed = dot(place.astype(BF), image_full)
    filled = jnp.any(place, axis=1)
    decoder_input = jnp.where(filled[:, None], placed, window_text.astype(F32))
    normed_text = layer_norm(decoder_input).astype(BF)
    normed_text = dot(normed_text, reorder).astype(BF)
    head_local = half // HD
    query = dot(normed_text[REACH * piece_rows :], full_d[:, :half]).astype(BF)
    pair = dot(normed_text, full_d[:, half : 3 * half]).astype(BF)
    query = query.reshape(piece_rows, head_local, HD)
    pair = pair.reshape(window_rows, 2, head_local, HD)

    piece_id = lax.axis_index(TOK)
    query_pos = piece_id * piece_rows + jnp.arange(piece_rows, dtype=jnp.int32)
    key_pos = (piece_id - REACH) * piece_rows + jnp.arange(window_rows, dtype=jnp.int32)
    lengths = prompt_lengths[0]
    starts = jnp.cumsum(lengths) - lengths
    query_start = jnp.max(
        jnp.where(starts[None, :] <= query_pos[:, None], starts[None, :], 0), axis=1
    )
    allowed = (
        (key_pos[None, :] <= query_pos[:, None]) & (key_pos[None, :] >= query_start[:, None])
    ).astype(F32)
    scores = jnp.einsum("qhe,khe->hqk", query, pair[:, 0], preferred_element_type=F32)
    weights = softmax_weights(scores, allowed[None])
    text_heads = jnp.einsum("hqk,khe->qhe", weights, pair[:, 1], preferred_element_type=F32)
    text_heads = text_heads.astype(BF).reshape(piece_rows, half)
    partial = lax.dot_general(
        text_heads, full_d[:, 3 * half :], (((1,), (1,)), ((), ())), preferred_element_type=F32
    ).astype(BF)
    sub = lax.axis_index("sub")
    keep_rows = piece_rows // 2
    give = lax.dynamic_slice_in_dim(partial, (1 - sub) * keep_rows, keep_rows, 0)
    keep = lax.dynamic_slice_in_dim(partial, sub * keep_rows, keep_rows, 0)
    total = (keep.astype(F32) + swap_sub(give).astype(F32)).astype(BF)
    return lax.dot_general(
        total, reorder, (((1,), (1,)), ((), ())), preferred_element_type=F32
    ).astype(BF)


def solution(mesh):
    grp, tok, sub = mesh.devices.shape
    lined = Mesh(mesh.devices.reshape(grp, 4, 4, tok // 16, sub), ("grp", "y", "x", "zh", "sub"))
    whole = ("grp",) + TOK
    placed = (
        P(whole, None),
        P(whole, None),
        P(TOK, "sub", None, None),
        P("sub", TOK),
        P(TOK, "sub"),
        P(whole, None),
        P("grp", TOK),
        P("grp", None),
        P(whole, "sub", None, None),
        P("sub", whole),
    )
    return jax.shard_map(
        shards,
        mesh=lined,
        in_specs=placed,
        out_specs=P(whole + ("sub",), None),
        check_vma=False,
    )
```

time: 1940 us -> 308 us (0.16)
  the two profiles are of different devices: /device:TPU:1 before, /device:TPU:57 now
where the time goes in v1:
time: 308 us
  waiting for transfers between devices  117 us (38%)
  blocking collectives  67.4 us (22%)
  starting transfers between devices  44.8 us (15%)
  matrix products  31.1 us (10%)
  local copies, waits for them, and re-layouts  23.4 us (8%)
  between operations  13.9 us (5%)
  other arithmetic  10.5 us (3%)
    ppermute x3, waiting for transfers between devices, shards(): lax.ppermute(own, 'zh', [(i, (i + s) % lines) for i in range(lines)])  64.3 us
    ppermute x3, waiting for transfers between devices, shards(): lax.ppermute(text, TOK, [(i, i + s) for i in range(pieces - s)])  31.2 us
    all_to_all x1, blocking collectives, shards(): lax.all_to_all(jnp.concatenate([vin, rest], axis=1), 'zh', split_axis=0,...  28.9 us
    all_to_all x1, blocking collectives, to_all(): return lax.all_to_all(spread, axes, split_axis=0, concat_axis=0, tiled=True)  22.1 us
    dot_general x6, matrix products, dot(): return jnp.dot(a, b, preferred_element_type=F32)  20.9 us
    all_to_all x1, waiting for transfers between devices, shards(): got = lax.all_to_all(sent, TOK, split_axis=0, concat_axis=0, tiled=True)  20 us
    all_to_all x1, blocking collectives, shards(): heads = lax.all_to_all(heads, 'zh', split_axis=0, concat_axis=0, tiled=True)  16.3 us
    ppermute x3, starting transfers between devices, shards(): lax.ppermute(text, TOK, [(i, i + s) for i in range(pieces - s)])  14.3 us
  transfers between devices with their start and end apart: 13, of which 7 were waited for; matrix products, arithmetic and copies ran while one was open for 14% of the time, Pallas kernels for 0%

profile of v1, /device:TPU:57, one launch (start us, length us, event | category | flops | bytes accessed | tf_op | source)
XLA Modules:
  0.0 307.7 jit_solution(3915825929419191379)
XLA Ops:
  9.1 28.9 %all_to_all.29 = bf16[4,132,704]{2,1,0:T(8,128)(2,1)S(1)} all-to-all(bf16[4,132,704]{2,1,0:T(8,128)(2,1)S(1)} %fusion.31), channel_id=1, replica_groups=mesh['grp'=2,'y'=4,'x'=4,'zh'=4,'sub'=2] {'zh'}, dimensions={0} | all-to-all | bytes 1486848 | tf_op jit(solution)/shard_map/all_to_all | solution.py:74
  39.7 22.1 %all_to_all.30 = bf16[8,11,2816]{2,1,0:T(8,128)(2,1)S(1)} all-to-all(bf16[8,11,2816]{2,1,0:T(8,128)(2,1)S(1)} %broadcast_in_dim.20), channel_id=1, replica_groups=mesh['grp'=2,'y'=4,'x'=4,'zh'=4,'sub'=2] {'grp','zh'}, dimensions={0} | all-to-all | bytes 991232 | tf_op jit(solution)/shard_map/all_to_all | solution.py:44
  64.0 1.5 collective-permute-start
  65.5 1.5 collective-permute-start.1
  67.0 3.2 %collective-permute-start.2 = (bf16[272,1408]{1,0:T(8,128)(2,1)S(1)}, bf16[272,1408]{1,0:T(8,128)(2,1)}, u32[]{:S(2)}, u32[]{:S(2)}) collective-permute-start(bf16[272,1408]{1,0:T(8,128)(2,1)S(1)} %fusion.32), channel_id=1, source_target_pairs={{0,6},{2,0},{4,2},{6,4},{1,7},{3,1},{5,3},{7,5},{8,14},{10,8},{12,... | collective-permute-start | bytes 2297864 | tf_op jit(solution)/shard_map/ppermute | solution.py:129
  70.2 63.5 %collective-permute-done = bf16[272,1408]{1,0:T(8,128)(2,1)S(1)} collective-permute-done((bf16[272,1408]{1,0:T(8,128)(2,1)S(1)}, bf16[272,1408]{1,0:T(8,128)(2,1)S(1)}, u32[]{:S(2)}, u32[]{:S(2)}) %collective-permute-start) | collective-permute-done | bytes 765984 | tf_op jit(solution)/shard_map/ppermute | solution.py:129
  134.5 1.5 pad_maximum_fusion
  136.0 1.6 copy-done.1
  138.4 1.2 compare_convert_fusion
  139.5 4.0 %fusion.76 = (bf16[16,88,704]{2,1,0:T(8,128)(2,1)}, bf16[16,88,704]{2,1,0:T(8,128)(2,1)S(1)}) fusion(bf16[16,528,704]{2,1,0:T(8,128)(2,1)} %bitcast.85), kind=kLoop, calls=%fused_computation.164 | loop fusion | bytes 7929856 | tf_op jit(solution)/shard_map/slice | solution.py:88
  143.6 2.5 fusion.80
  149.6 16.3 %all_to_all.31 = bf16[4,256,176]{1,2,0:T(8,128)(2,1)S(1)} all-to-all(bf16[4,256,176]{1,2,0:T(8,128)(2,1)S(1)} %fusion.36), channel_id=1, replica_groups=mesh['grp'=2,'y'=4,'x'=4,'zh'=4,'sub'=2] {'zh'}, dimensions={0} | all-to-all | bytes 720896 | tf_op jit(solution)/shard_map/all_to_all | solution.py:157
  166.0 2.4 convolution_convert_fusion
  168.4 3.2 %collective-permute-start.3 = (bf16[256,1408]{1,0:T(8,128)(2,1)S(1)}, bf16[256,1408]{1,0:T(8,128)(2,1)S(1)}, u32[]{:S(2)}, u32[]{:S(2)}) collective-permute-start(bf16[256,1408]{1,0:T(8,128)(2,1)S(1)} %convolution_convert_fusion), channel_id=1, source_target_pairs={{0,1},{1,0},{2,3},{3,2},{4,5},{5,4},{6,7},{7,6},{8,9},{9,8},{10,11... | collective-permute-start | bytes 2162696 | tf_op jit(solution)/shard_map/ppermute | solution.py:34
  172.0 7.5 %slice.99 = bf16[16,352,704]{2,1,0:T(8,128)(2,1)} slice(bf16[16,528,704]{2,1,0:T(8,128)(2,1)} %bitcast.86), slice={[0:16], [176:528], [0:704]} | slice | bytes 15859712 | tf_op jit(solution)/shard_map/slice | solution.py:89
  181.2 5.8 %convolution_convert_fusion.2 = bf16[512,704]{0,1:T(8,128)(2,1)S(1)} fusion(bf16[64,5632]{1,0:T(8,128)(2,1)S(1)} %reshape.369, bf16[5632,704]{1,0:T(8,128)(2,1)} %bitcast.84, s32[512]{0:T(512)S(1)} %get-tuple-element.40, s32[512]{0:T(512)S(1)} %get-tuple-element.41, s32[64]{0:T(128)S(1)} %select_reduce_fusion.1, s32[64]{0:T(128)S(1)} %get-tuple-element.33), kind=kOutput, calls=%fused_computation.44 | convolution fusion | flops 554151936 | bytes 9376256 | tf_op jit(solution)/shard_map/dot_general | solution.py:38
  188.2 8.0 %all-to-all-start.4 = ((bf16[64,8,704]{2,1,0:T(8,128)(2,1)}), bf16[64,8,704]{2,1,0:T(8,128)(2,1)S(1)}, u32[]{:S(2)}, u32[]{:S(2)}) async-start(bf16[64,8,704]{2,1,0:T(8,128)(2,1)} %bitcast.26), calls=%async_computation.4 | async-start | bytes 1572864 | tf_op jit(solution)/shard_map/all_to_all | solution.py:166
  196.5 20.0 %all-to-all-done.4 = bf16[64,8,704]{2,1,0:T(8,128)(2,1)S(1)} async-done(((bf16[64,8,704]{2,1,0:T(8,128)(2,1)}), bf16[64,8,704]{2,1,0:T(8,128)(2,1)S(1)}, u32[]{:S(2)}, u32[]{:S(2)}) %all-to-all-start.4) | async-done | bytes 720928 | tf_op jit(solution)/shard_map/all_to_all | solution.py:166
  216.8 1.7 collective-permute-start.4
  219.4 10.3 %all-to-all-start.2 = ((s32[64,1,8]{2,1,0:T(1,128)}), s32[64,1,8]{2,1,0:T(1,128)S(1)}, u32[]{:S(2)}, u32[]{:S(2)}) async-start(s32[64,1,8]{2,1,0:T(1,128)} %bitcast.8), calls=%async_computation.2 | async-start | bytes 65536 | tf_op jit(solution)/shard_map/all_to_all | solution.py:120
  229.8 5.2 %collective-permute-start.5 = (bf16[128,1408]{1,0:T(8,128)(2,1)S(1)}, bf16[128,1408]{1,0:T(8,128)(2,1)S(1)}, u32[]{:S(2)}, u32[]{:S(2)}) collective-permute-start(bf16[128,1408]{1,0:T(8,128)(2,1)S(1)} %copy-done.5), channel_id=1, source_target_pairs={{0,6},{2,8},{4,10},{6,12},{8,14},{10,16},{12,18},{14,20},{16,22},{... | collective-permute-start | bytes 1081352 | tf_op jit(solution)/shard_map/ppermute | solution.py:134
  235.0 4.9 %collective-permute-start.6 = (bf16[128,1408]{1,0:T(8,128)(2,1)S(1)}, bf16[128,1408]{1,0:T(8,128)(2,1)}, u32[]{:S(2)}, u32[]{:S(2)}) collective-permute-start(bf16[128,1408]{1,0:T(8,128)(2,1)S(1)} %copy-done.5), channel_id=1, source_target_pairs={{0,4},{2,6},{4,8},{6,10},{8,12},{10,14},{12,16},{14,18},{16,20},{1... | collective-permute-start | bytes 1081352 | tf_op jit(solution)/shard_map/ppermute | solution.py:134
  239.9 4.2 %collective-permute-start.7 = (bf16[128,1408]{1,0:T(8,128)(2,1)S(1)}, bf16[128,1408]{1,0:T(8,128)(2,1)}, u32[]{:S(2)}, u32[]{:S(2)}) collective-permute-start(bf16[128,1408]{1,0:T(8,128)(2,1)S(1)} %copy-done.5), channel_id=1, source_target_pairs={{0,2},{2,4},{4,6},{6,8},{8,10},{10,12},{12,14},{14,16},{16,18},{18... | collective-permute-start | bytes 1081352 | tf_op jit(solution)/shard_map/ppermute | solution.py:134
  246.1 1.8 collective-permute-done.5
  247.9 24.0 %collective-permute-done.6 = bf16[128,1408]{1,0:T(8,128)(2,1)} collective-permute-done((bf16[128,1408]{1,0:T(8,128)(2,1)S(1)}, bf16[128,1408]{1,0:T(8,128)(2,1)}, u32[]{:S(2)}, u32[]{:S(2)}) %collective-permute-start.6) | collective-permute-done | bytes 360480 | tf_op jit(solution)/shard_map/ppermute | solution.py:134
  271.9 5.4 %collective-permute-done.7 = bf16[128,1408]{1,0:T(8,128)(2,1)} collective-permute-done((bf16[128,1408]{1,0:T(8,128)(2,1)S(1)}, bf16[128,1408]{1,0:T(8,128)(2,1)}, u32[]{:S(2)}, u32[]{:S(2)}) %collective-permute-start.7) | collective-permute-done | bytes 360480 | tf_op jit(solution)/shard_map/ppermute | solution.py:134
  277.3 2.3 fusion.79
  280.0 2.7 fusion.9
  283.8 4.9 %fusion.6 = bf16[512,1408]{1,0:T(8,128)(2,1)S(1)} fusion(bf16[512,1408]{1,0:T(8,128)(2,1)S(1)} %fusion.9, bf16[1408,2816]{1,0:T(8,128)(2,1)} %all-gather.4.cloned.1.call-done), kind=kOutput, calls=%fused_computation.9 | convolution fusion | flops 2030764032 | bytes 6848512 | tf_op jit(solution)/shard_map/dot_general | solution.py:38
  289.4 2.7 fusion.27
  293.6 2.8 convolution_convert_fusion.1
  298.5 2.3 fusion.10
  (105 shorter events, 23.7 us)
Async XLA Ops:
  6.5 133.0 %all-gather.6.cloned.1.call-start = ((), (), s32[]{:S(2)}) async-start(), calls=%async_computation.6 | async-start | bytes 13787136 | tf_op jit(solution)/shard_map/all_gather | solution.py:85
  38.0 1.3 copy-start.3
  38.1 1.5 copy-start.4
  39.3 243.4 %all-gather.4.cloned.1.call-start = ((), (), s32[]{:S(2)}) async-start(), calls=%async_computation.5 | async-start | bytes 8425472 | tf_op jit(solution)/shard_map/all_gather | solution.py:95
  39.5 23.3 %copy-start.6 = (s32[1,4]{1,0:T(1,128)S(1)}, s32[1,4]{1,0:T(1,128)}, u32[]{:S(2)}) copy-start(s32[1,4]{1,0:T(1,128)} %param.13) | copy-start | bytes 52
  39.5 23.5 %copy-start = (bf16[256,1408]{1,0:T(8,128)(2,1)S(1)}, bf16[256,1408]{1,0:T(8,128)(2,1)}, u32[]{:S(2)}) copy-start(bf16[256,1408]{1,0:T(8,128)(2,1)} %param.12) | copy-start | bytes 2162692
  64.0 69.7 %collective-permute-start = (bf16[272,1408]{1,0:T(8,128)(2,1)S(1)}, bf16[272,1408]{1,0:T(8,128)(2,1)S(1)}, u32[]{:S(2)}, u32[]{:S(2)}) collective-permute-start(bf16[272,1408]{1,0:T(8,128)(2,1)S(1)} %fusion.32), channel_id=1, source_target_pairs={{0,2},{2,4},{4,6},{6,0},{1,3},{3,5},{5,7},{7,1},{8,10},{10,12},{12... | collective-permute-start | bytes 2297864 | tf_op jit(solution)/shard_map/ppermute | solution.py:129
  65.5 68.2 %collective-permute-start.1 = (bf16[272,1408]{1,0:T(8,128)(2,1)S(1)}, bf16[272,1408]{1,0:T(8,128)(2,1)S(1)}, u32[]{:S(2)}, u32[]{:S(2)}) collective-permute-start(bf16[272,1408]{1,0:T(8,128)(2,1)S(1)} %fusion.32), channel_id=1, source_target_pairs={{0,4},{2,6},{4,0},{6,2},{1,5},{3,7},{5,1},{7,3},{8,12},{10,14},{12... | collective-permute-start | bytes 2297864 | tf_op jit(solution)/shard_map/ppermute | solution.py:129
  67.0 67.5 %collective-permute-start.2 = (bf16[272,1408]{1,0:T(8,128)(2,1)S(1)}, bf16[272,1408]{1,0:T(8,128)(2,1)}, u32[]{:S(2)}, u32[]{:S(2)}) collective-permute-start(bf16[272,1408]{1,0:T(8,128)(2,1)S(1)} %fusion.32), channel_id=1, source_target_pairs={{0,6},{2,0},{4,2},{6,4},{1,7},{3,1},{5,3},{7,5},{8,14},{10,8},{12,... | collective-permute-start | bytes 2297864 | tf_op jit(solution)/shard_map/ppermute | solution.py:129
  136.0 1.6 copy-start.1
  139.5 4.0 %slice-start = ((bf16[4,272,1408]{2,1,0:T(8,128)(2,1)}), bf16[4,256,1408]{2,1,0:T(8,128)(2,1)S(1)}, s32[]{:S(2)}) async-start(bf16[4,272,1408]{2,1,0:T(8,128)(2,1)} %copy-done.1), calls=%async_computation.7 | async-start | bytes 5767168 | tf_op jit(solution)/shard_map/slice | solution.py:140
  147.0 1.2 copy-start.2
  149.6 22.0 %copy-start.7 = (s32[1,64]{1,0:T(1,128)S(1)}, s32[1,64]{1,0:T(1,128)}, u32[]{:S(2)}) copy-start(s32[1,64]{1,0:T(1,128)} %param.18) | copy-start | bytes 772
  168.4 11.1 %collective-permute-start.3 = (bf16[256,1408]{1,0:T(8,128)(2,1)S(1)}, bf16[256,1408]{1,0:T(8,128)(2,1)S(1)}, u32[]{:S(2)}, u32[]{:S(2)}) collective-permute-start(bf16[256,1408]{1,0:T(8,128)(2,1)S(1)} %convolution_convert_fusion), channel_id=1, source_target_pairs={{0,1},{1,0},{2,3},{3,2},{4,5},{5,4},{6,7},{7,6},{8,9},{9,8},{10,11... | collective-permute-start | bytes 2162696 | tf_op jit(solution)/shard_map/ppermute | solution.py:34
  187.0 9.2 %copy-start.8 = (s32[1,2]{1,0:T(1,128)S(1)}, s32[1,2]{1,0:T(1,128)}, u32[]{:S(2)}) copy-start(s32[1,2]{1,0:T(1,128)} %param.19) | copy-start | bytes 28
  188.2 41.5 %copy-start.5 = (bf16[128,1408]{1,0:T(8,128)(2,1)S(1)}, bf16[128,1408]{1,0:T(8,128)(2,1)}, u32[]{:S(2)}) copy-start(bf16[128,1408]{1,0:T(8,128)(2,1)} %param.17) | copy-start | bytes 1081348
  188.2 28.3 %all-to-all-start.4 = ((bf16[64,8,704]{2,1,0:T(8,128)(2,1)}), bf16[64,8,704]{2,1,0:T(8,128)(2,1)S(1)}, u32[]{:S(2)}, u32[]{:S(2)}) async-start(bf16[64,8,704]{2,1,0:T(8,128)(2,1)} %bitcast.26), calls=%async_computation.4 | async-start | bytes 1572864 | tf_op jit(solution)/shard_map/all_to_all | solution.py:166
  216.8 28.9 %collective-permute-start.4 = (bf16[512,704]{0,1:T(8,128)(2,1)S(1)}, bf16[512,704]{0,1:T(8,128)(2,1)S(1)}, u32[]{:S(2)}, u32[]{:S(2)}) collective-permute-start(bf16[512,704]{0,1:T(8,128)(2,1)S(1)} %copy.45), channel_id=1, source_target_pairs={{0,1},{1,0},{2,3},{3,2},{4,5},{5,4},{6,7},{7,6},{8,9},{9,8},{10,11... | collective-permute-start | bytes 2162696 | tf_op jit(solution)/shard_map/ppermute | solution.py:34
  219.4 24.7 %all-to-all-start.2 = ((s32[64,1,8]{2,1,0:T(1,128)}), s32[64,1,8]{2,1,0:T(1,128)S(1)}, u32[]{:S(2)}, u32[]{:S(2)}) async-start(s32[64,1,8]{2,1,0:T(1,128)} %bitcast.8), calls=%async_computation.2 | async-start | bytes 65536 | tf_op jit(solution)/shard_map/all_to_all | solution.py:120
  229.8 18.2 %collective-permute-start.5 = (bf16[128,1408]{1,0:T(8,128)(2,1)S(1)}, bf16[128,1408]{1,0:T(8,128)(2,1)S(1)}, u32[]{:S(2)}, u32[]{:S(2)}) collective-permute-start(bf16[128,1408]{1,0:T(8,128)(2,1)S(1)} %copy-done.5), channel_id=1, source_target_pairs={{0,6},{2,8},{4,10},{6,12},{8,14},{10,16},{12,18},{14,20},{16,22},{... | collective-permute-start | bytes 1081352 | tf_op jit(solution)/shard_map/ppermute | solution.py:134
  235.0 36.9 %collective-permute-start.6 = (bf16[128,1408]{1,0:T(8,128)(2,1)S(1)}, bf16[128,1408]{1,0:T(8,128)(2,1)}, u32[]{:S(2)}, u32[]{:S(2)}) collective-permute-start(bf16[128,1408]{1,0:T(8,128)(2,1)S(1)} %copy-done.5), channel_id=1, source_target_pairs={{0,4},{2,6},{4,8},{6,10},{8,12},{10,14},{12,16},{14,18},{16,20},{1... | collective-permute-start | bytes 1081352 | tf_op jit(solution)/shard_map/ppermute | solution.py:134
  239.9 37.4 %collective-permute-start.7 = (bf16[128,1408]{1,0:T(8,128)(2,1)S(1)}, bf16[128,1408]{1,0:T(8,128)(2,1)}, u32[]{:S(2)}, u32[]{:S(2)}) collective-permute-start(bf16[128,1408]{1,0:T(8,128)(2,1)S(1)} %copy-done.5), channel_id=1, source_target_pairs={{0,2},{2,4},{4,6},{6,8},{8,10},{10,12},{12,14},{14,16},{16,18},{18... | collective-permute-start | bytes 1081352 | tf_op jit(solution)/shard_map/ppermute | solution.py:134
  282.7 1.1 copy-start.9
  296.4 2.1 collective-permute-start.8
Sparse Core Ops, SparseCore 0:
  39.4 96.0 all-gather.5
  138.0 82.0 all-gather.3

commit v2 on v1

--- a/solution.py
+++ b/solution.py
@@ -24,10 +24,6 @@
 def softmax_weights(scores, allowed):
     raw = jnp.exp(scores * (1.0 / math.sqrt(HD))) * allowed
     return (raw / jnp.sum(raw, axis=-1, keepdims=True)).astype(BF)
-
-
-def after(value, *others):
-    return lax.optimization_barrier((value, *others))[0]
 
 
 def swap_sub(value):
@@ -66,37 +62,41 @@
     krows = vision_inproj.shape[0]
     mrows = merger_weight.shape[0]
 
+    line_m = to_all(merger_weight, "zh").reshape(lines * mrows, half)
+
     vin = vision_inproj.reshape(krows, 3, lines, quarter).transpose(2, 0, 1, 3)
     vin = vin.reshape(lines, krows, 3 * quarter)
     vin = jnp.pad(vin, ((0, 0), (0, 0), (0, half - 3 * quarter)))
-    rest = jnp.concatenate([vision_outproj.T, merger_weight], axis=0)
+    drows = decoder_inproj.shape[0]
+    dec = jnp.concatenate(
+        [decoder_inproj.reshape(drows, 3, half).transpose(1, 0, 2), decoder_outproj.T[None]], axis=0
+    )
+    dec_other = lax.ppermute(dec, "grp", [(0, 1), (1, 0)])
+    low = lax.axis_index("grp") == 0
+    dec = jnp.stack([jnp.where(low, dec, dec_other), jnp.where(low, dec_other, dec)], axis=1)
+    rest = jnp.concatenate([vision_outproj.T, dec.reshape(8 * drows, half)], axis=0)
     rest = jnp.broadcast_to(rest[None], (lines,) + rest.shape)
-    line_v = lax.all_to_all(
-        jnp.concatenate([vin, rest], axis=1), "zh", split_axis=0, concat_axis=0, tiled=True
-    )
+    line = jnp.concatenate([vin, rest], axis=1)
+    line, line_m = lax.optimization_barrier((line, line_m))
+    w_merge = lax.all_gather(line_m, PLANE, axis=0, tiled=True)
+    line = lax.all_to_all(line, "zh", split_axis=0, concat_axis=0, tiled=True)
+    kline = lines * krows
     line_v = jnp.concatenate(
         [
-            line_v[:, :krows].reshape(lines * krows, half),
-            line_v[:, krows : 2 * krows].reshape(lines * krows, half),
-            line_v[:, 2 * krows :].reshape(lines * mrows, half),
+            line[:, :krows, : 3 * quarter].reshape(kline, 3 * quarter),
+            line[:, krows : 2 * krows].reshape(kline, half),
         ],
-        axis=0,
-    )
-    full_v = lax.all_gather(line_v, PLANE, axis=0, tiled=False)
-    kline = lines * krows
-    w_in = full_v[:, :kline].reshape(width, half)
-    w_out = full_v[:, kline : 2 * kline].reshape(width, half)
-    w_merge = full_v[:, 2 * kline :].reshape(planes * lines * mrows, half)
-
-    drows = decoder_inproj.shape[0]
-    dec = jnp.concatenate([decoder_inproj.reshape(drows, 3 * half), decoder_outproj.T], axis=1)
-    dec = after(dec, line_v)
-    line_d = to_all(dec, ("grp", "zh")).reshape(-1, 4 * half)
+        axis=1,
+    )
+    line_d = line[:, 2 * krows :].reshape(lines, 4, 2 * drows, half).transpose(0, 2, 1, 3)
+    line_d = line_d.reshape(lines * 2 * drows, 4 * half)
     full_d = lax.all_gather(line_d, PLANE, axis=0, tiled=True)
-    fan = lines * drows
+    full_v = to_all(line_v, PLANE).reshape(width, 3 * quarter + half)
+    w_in = full_v[:, : 3 * quarter]
+    w_out = full_v[:, 3 * quarter :]
     order = jnp.arange(width, dtype=jnp.int32)
     natural = (
-        (order // fan) % 2 * (width // 2) + order // (2 * fan) * fan + order % fan
+        order // drows % 2 * (width // 2) + order // (2 * drows) * drows + order % drows
     )
     reorder = (natural[None, :] == order[:, None]).astype(BF)
 
@@ -113,38 +113,41 @@
     back = dest // cap % reach
     wanted = (dest // slots)[:, None] - back[:, None] == target_piece[None, :]
     wanted = wanted & ((dest % cap)[:, None] == slot[None, :])
-    window_row = (REACH - back)[:, None] * piece_rows + target_row[None, :]
     window_rows = reach * piece_rows
-    row_list = jnp.min(jnp.where(wanted, window_row, window_rows), axis=1)
-    row_list = after(row_list.reshape(pieces, slots), line_d)
-    arrived = lax.all_to_all(row_list, TOK, split_axis=0, concat_axis=0, tiled=True).reshape(-1)
-    place = jnp.arange(window_rows, dtype=jnp.int32)[:, None] == arrived[None, :]
 
     patch_rows = patches.astype(F32)
+    first = lax.axis_index("sub") == 0
     ends = jnp.cumsum(image_sizes[0]).astype(BF)
     mark = jnp.zeros((16, width), BF).at[0, : ends.shape[0]].set(ends)
-    own = jnp.concatenate([layer_norm(patch_rows).astype(BF), mark], axis=0)
-    own = after(own, arrived)
+    normed = layer_norm(patch_rows).astype(BF)
+    side = rows_v // 2
+    top, bottom = normed[:side], normed[side:]
+    mine = jnp.concatenate([jnp.where(first, top, bottom), mark], axis=0)
     moved = [
-        lax.ppermute(own, "zh", [(i, (i + s) % lines) for i in range(lines)])
+        lax.ppermute(mine, "zh", [(i, (i + s) % lines) for i in range(lines)])
         for s in range(1, lines)
     ]
-    text = after(text_embed, moved[0])
+    moved = jnp.stack(moved)
+    traded = swap_sub(moved[:, :side])
+    kept = moved[:, :side]
+    others = jnp.concatenate(
+        [jnp.where(first, kept, traded), jnp.where(first, traded, kept)], axis=1
+    )
+    text, others = lax.optimization_barrier((text_embed, others))
     earlier = [
         lax.ppermute(text, TOK, [(i, i + s) for i in range(pieces - s)])
         for s in range(REACH, 0, -1)
     ]
-    window_text = jnp.concatenate(earlier + [text_embed], axis=0)
-
-    both = jnp.stack([own] + moved)
-    normed = both[:, :rows_v].reshape(lines * rows_v, width)
-    ends_all = both[:, rows_v, : ends.shape[0]].astype(jnp.int32)
+    window_text = jnp.concatenate(earlier + [text], axis=0)
+
+    normed = jnp.concatenate([normed[None], others]).reshape(lines * rows_v, width)
+    ends_all = jnp.concatenate([ends[None], moved[:, side, : ends.shape[0]]]).astype(jnp.int32)
     group_ids = jnp.arange(rows_v, dtype=jnp.int32) // 4
     image_ids = jnp.sum(
         (group_ids[None, :, None] >= ends_all[:, None, :]).astype(jnp.int32), axis=2
     )
     same = (image_ids[:, :, None] == image_ids[:, None, :]).astype(F32)
-    projected = dot(normed, w_in)[:, : 3 * quarter].astype(BF)
+    projected = dot(normed, w_in).astype(BF)
     triple = projected.reshape(lines, rows_v, 3, heads_line, HD)
     scores = jnp.einsum(
         "pqhe,pkhe->phqk", triple[:, :, 0], triple[:, :, 1], preferred_element_type=F32
@@ -154,6 +157,7 @@
     heads = heads.astype(BF).reshape(lines, rows_v, quarter)
     me = lax.axis_index("zh")
     heads = jnp.roll(heads[::-1], me + 1, axis=0)
+    heads, window_text = lax.optimization_barrier((heads, window_text))
     heads = lax.all_to_all(heads, "zh", split_axis=0, concat_axis=0, tiled=True)
     heads = heads.transpose(1, 0, 2).reshape(rows_v, half)
     partial = lax.dot_general(heads, w_out, (((1,), (1,)), ((), ())), preferred_element_type=F32)
@@ -162,11 +166,18 @@
     merged = layer_norm(hidden).astype(BF).reshape(rows_v // 4, 4 * width)
     embedded = dot(merged, w_merge).astype(BF)
 
-    sent = dot(wanted.astype(BF), embedded).astype(BF).reshape(pieces, slots, half)
-    got = lax.all_to_all(sent, TOK, split_axis=0, concat_axis=0, tiled=True)
-    got = got.reshape(pieces * slots, half)
+    note = jnp.stack([target_row, jnp.ones_like(target_row)], axis=1).astype(BF)
+    note = jnp.pad(note, ((0, 0), (0, 62)))
+    sent = dot(wanted.astype(BF), jnp.concatenate([embedded, note], axis=1)).astype(BF)
+    got = lax.all_to_all(
+        sent.reshape(pieces, slots, half + 64), TOK, split_axis=0, concat_axis=0, tiled=True
+    ).reshape(pieces * slots, half + 64)
+    note = got[:, half : half + 2].astype(jnp.int32)
+    arrived = jnp.arange(pieces * slots, dtype=jnp.int32) // cap % reach
+    arrived = jnp.where(note[:, 1] > 0, (REACH - arrived) * piece_rows + note[:, 0], window_rows)
+    place = jnp.arange(window_rows, dtype=jnp.int32)[:, None] == arrived[None, :]
+    got = got[:, :half]
     other = swap_sub(got)
-    first = lax.axis_index("sub") == 0
     image_full = jnp.concatenate(
         [jnp.where(first, got, other), jnp.where(first, other, got)], axis=1
     )

time: 308 us -> 284 us (0.922)
  the two profiles are of different devices: /device:TPU:57 before, /device:TPU:1 now
where the time goes in v2:
time: 284 us; the launch traced here: 283 us
  waiting for transfers between devices  146 us (51%)
  starting transfers between devices  55.1 us (19%)
  matrix products  37.6 us (13%)
  local copies, waits for them, and re-layouts  17.6 us (6%)
  between operations  14 us (5%)
  other arithmetic  13.1 us (5%)
    ppermute x3, waiting for transfers between devices, shards(): lax.ppermute(text, TOK, [(i, i + s) for i in range(pieces - s)])  31.7 us
    dot_general x7, matrix products, dot(): return jnp.dot(a, b, preferred_element_type=F32)  26.8 us
    all_to_all x1, waiting for transfers between devices, shards(): lax.all_to_all(sent.reshape(pieces, slots, half + 64), TOK, split_axis=0,...  24.5 us
    all_to_all x2, waiting for transfers between devices, to_all(): return lax.all_to_all(spread, axes, split_axis=0, concat_axis=0, tiled=True)  23.5 us
    all_to_all x1, waiting for transfers between devices, shards(): line = lax.all_to_all(line, 'zh', split_axis=0, concat_axis=0, tiled=True)  21.4 us
    ppermute x3, waiting for transfers between devices, shards(): lax.ppermute(mine, 'zh', [(i, (i + s) % lines) for i in range(lines)])  19 us
    all_to_all x2, starting transfers between devices, to_all(): return lax.all_to_all(spread, axes, split_axis=0, concat_axis=0, tiled=True)  15.8 us
    ppermute x3, starting transfers between devices, shards(): lax.ppermute(text, TOK, [(i, i + s) for i in range(pieces - s)])  12.5 us
  transfers between devices with their start and end apart: 18, of which 14 were waited for; matrix products, arithmetic and copies ran while one was open for 16% of the time, Pallas kernels for 0%

profile of v2, /device:TPU:1, one launch (start us, length us, event | category | flops | bytes accessed | tf_op | source)
XLA Modules:
  0.0 282.9 jit_solution(12278683149256310386)
XLA Ops:
  8.3 9.0 %all-to-all-start = ((bf16[4,88,704]{2,1,0:T(8,128)(2,1)}), bf16[4,88,704]{2,1,0:T(8,128)(2,1)S(1)}, u32[]{:S(2)}, u32[]{:S(2)}) async-start(bf16[4,88,704]{2,1,0:T(8,128)(2,1)} %broadcast_in_dim.27), calls=%async_computation | async-start | bytes 1081344 | tf_op jit(solution)/shard_map/all_to_all | solution.py:40
  21.2 10.3 %collective-permute-done.4 = bf16[4,11,704]{2,0,1:T(4,128)(2,1)S(1)} collective-permute-done((bf16[4,11,704]{2,0,1:T(4,128)(2,1)S(1)}, bf16[4,11,704]{2,0,1:T(4,128)(2,1)S(1)}, u32[]{:S(2)}, u32[]{:S(2)}) %collective-permute-start.4) | collective-permute-done | bytes 61984 | tf_op jit(solution)/shard_map/ppermute | solution.py:74
  33.9 5.2 %all-to-all-start.1 = ((bf16[4,132,704]{2,1,0:T(8,128)(2,1)}), bf16[4,132,704]{2,1,0:T(8,128)(2,1)S(1)}, u32[]{:S(2)}, u32[]{:S(2)}) async-start(bf16[4,132,704]{2,1,0:T(8,128)(2,1)} %fusion.37), calls=%async_computation.1 | async-start | bytes 1671168 | tf_op jit(solution)/shard_map/all_to_all | solution.py:82
  39.3 21.4 %all-to-all-done.1 = bf16[4,132,704]{2,1,0:T(8,128)(2,1)S(1)} async-done(((bf16[4,132,704]{2,1,0:T(8,128)(2,1)}), bf16[4,132,704]{2,1,0:T(8,128)(2,1)S(1)}, u32[]{:S(2)}, u32[]{:S(2)}) %all-to-all-start.1) | async-done | bytes 743456 | tf_op jit(solution)/shard_map/all_to_all | solution.py:82
  63.6 3.0 %collective-permute-start = (bf16[144,1408]{1,0:T(8,128)(2,1)S(1)}, bf16[144,1408]{1,0:T(8,128)(2,1)S(1)}, u32[]{:S(2)}, u32[]{:S(2)}) collective-permute-start(bf16[144,1408]{1,0:T(8,128)(2,1)S(1)} %fusion.41), channel_id=1, source_target_pairs={{0,2},{2,4},{4,6},{6,0},{1,3},{3,5},{5,7},{7,1},{8,10},{10,12},{12... | collective-permute-start | bytes 1216520 | tf_op jit(solution)/shard_map/ppermute | solution.py:127
  66.8 3.4 %collective-permute-start.2 = (bf16[144,1408]{1,0:T(8,128)(2,1)S(1)}, bf16[144,1408]{1,0:T(8,128)(2,1)S(1)}, u32[]{:S(2)}, u32[]{:S(2)}) collective-permute-start(bf16[144,1408]{1,0:T(8,128)(2,1)S(1)} %fusion.41), channel_id=1, source_target_pairs={{0,6},{2,0},{4,2},{6,4},{1,7},{3,1},{5,3},{7,5},{8,14},{10,8},{12,... | collective-permute-start | bytes 1216520 | tf_op jit(solution)/shard_map/ppermute | solution.py:127
  72.6 6.8 %all-to-all-start.2 = ((bf16[16,88,1232]{2,1,0:T(8,128)(2,1)}), bf16[16,88,1232]{2,1,0:T(8,128)(2,1)}, u32[]{:S(2)}, u32[]{:S(2)}) async-start(bf16[16,88,1232]{2,1,0:T(8,128)(2,1)} %broadcast_in_dim.28), calls=%async_computation.2 | async-start | bytes 7208960 | tf_op jit(solution)/shard_map/all_to_all | solution.py:40
  79.4 10.4 %collective-permute-done.1 = bf16[144,1408]{1,0:T(8,128)(2,1)S(1)} collective-permute-done((bf16[144,1408]{1,0:T(8,128)(2,1)S(1)}, bf16[144,1408]{1,0:T(8,128)(2,1)S(1)}, u32[]{:S(2)}, u32[]{:S(2)}) %collective-permute-start.1) | collective-permute-done | bytes 405536 | tf_op jit(solution)/shard_map/ppermute | solution.py:127
  89.8 8.7 %collective-permute-done.2 = bf16[144,1408]{1,0:T(8,128)(2,1)S(1)} collective-permute-done((bf16[144,1408]{1,0:T(8,128)(2,1)S(1)}, bf16[144,1408]{1,0:T(8,128)(2,1)S(1)}, u32[]{:S(2)}, u32[]{:S(2)}) %collective-permute-start.2) | collective-permute-done | bytes 405536 | tf_op jit(solution)/shard_map/ppermute | solution.py:127
  100.5 2.2 collective-permute-done.3
  105.2 5.4 %collective-permute-start.5 = (bf16[128,1408]{1,0:T(8,128)(2,1)S(1)}, bf16[128,1408]{1,0:T(8,128)(2,1)S(1)}, u32[]{:S(2)}, u32[]{:S(2)}) collective-permute-start(bf16[128,1408]{1,0:T(8,128)(2,1)S(1)} %copy-done.2), channel_id=1, source_target_pairs={{0,6},{2,8},{4,10},{6,12},{8,14},{10,16},{12,18},{14,20},{16,22},{... | collective-permute-start | bytes 1081352 | tf_op jit(solution)/shard_map/ppermute | solution.py:138
  110.6 5.6 %collective-permute-start.6 = (bf16[128,1408]{1,0:T(8,128)(2,1)S(1)}, bf16[128,1408]{1,0:T(8,128)(2,1)S(1)}, u32[]{:S(2)}, u32[]{:S(2)}) collective-permute-start(bf16[128,1408]{1,0:T(8,128)(2,1)S(1)} %copy-done.2), channel_id=1, source_target_pairs={{0,4},{2,6},{4,8},{6,10},{8,12},{10,14},{12,16},{14,18},{16,20},{1... | collective-permute-start | bytes 1081352 | tf_op jit(solution)/shard_map/ppermute | solution.py:138
  119.8 4.9 %collective-permute-done.5 = bf16[128,1408]{1,0:T(8,128)(2,1)S(1)} collective-permute-done((bf16[128,1408]{1,0:T(8,128)(2,1)S(1)}, bf16[128,1408]{1,0:T(8,128)(2,1)S(1)}, u32[]{:S(2)}, u32[]{:S(2)}) %collective-permute-start.5) | collective-permute-done | bytes 360480 | tf_op jit(solution)/shard_map/ppermute | solution.py:138
  124.7 17.2 %collective-permute-done.6 = bf16[128,1408]{1,0:T(8,128)(2,1)S(1)} collective-permute-done((bf16[128,1408]{1,0:T(8,128)(2,1)S(1)}, bf16[128,1408]{1,0:T(8,128)(2,1)S(1)}, u32[]{:S(2)}, u32[]{:S(2)}) %collective-permute-start.6) | collective-permute-done | bytes 360480 | tf_op jit(solution)/shard_map/ppermute | solution.py:138
  141.9 9.6 %collective-permute-done.7 = bf16[128,1408]{1,0:T(8,128)(2,1)S(1)} collective-permute-done((bf16[128,1408]{1,0:T(8,128)(2,1)S(1)}, bf16[128,1408]{1,0:T(8,128)(2,1)S(1)}, u32[]{:S(2)}, u32[]{:S(2)}) %collective-permute-start.7) | collective-permute-done | bytes 360480 | tf_op jit(solution)/shard_map/ppermute | solution.py:138
  152.7 23.5 %all-to-all-done.2 = bf16[16,88,1232]{2,1,0:T(8,128)(2,1)} async-done(((bf16[16,88,1232]{2,1,0:T(8,128)(2,1)}), bf16[16,88,1232]{2,1,0:T(8,128)(2,1)}, u32[]{:S(2)}, u32[]{:S(2)}) %all-to-all-start.2) | async-done | bytes 3469344 | tf_op jit(solution)/shard_map/all_to_all | solution.py:40
  176.2 5.3 %fusion.22 = bf16[1024,528]{0,1:T(8,128)(2,1)} fusion(bf16[1024,1408]{1,0:T(8,128)(2,1)} %bitcast.95, bf16[1408,1232]{1,0:T(8,128)(2,1)} %bitcast.16), kind=kOutput, calls=%fused_computation.36 | convolution fusion | flops 1523073024 | bytes 5767168 | tf_op jit(solution)/shard_map/dot_general | solution.py:34
  181.5 2.5 reshape.458
  186.5 3.5 %all-to-all-start.3 = ((bf16[4,256,176]{1,2,0:T(8,128)(2,1)}), bf16[4,256,176]{1,2,0:T(8,128)(2,1)S(1)}, u32[]{:S(2)}, u32[]{:S(2)}) async-start(bf16[4,256,176]{1,2,0:T(8,128)(2,1)} %fusion.43), calls=%async_computation.3 | async-start | bytes 720896 | tf_op jit(solution)/shard_map/all_to_all | solution.py:161
  190.1 9.2 %all-to-all-done.3 = bf16[4,256,176]{1,2,0:T(8,128)(2,1)S(1)} async-done(((bf16[4,256,176]{1,2,0:T(8,128)(2,1)}), bf16[4,256,176]{1,2,0:T(8,128)(2,1)S(1)}, u32[]{:S(2)}, u32[]{:S(2)}) %all-to-all-start.3) | async-done | bytes 360480 | tf_op jit(solution)/shard_map/all_to_all | solution.py:161
  199.3 3.1 %convolution_convert_fusion = bf16[256,1408]{1,0:T(8,128)(2,1)S(1)} fusion(bf16[256,704]{0,1:T(8,128)(2,1)S(1)} %bitcast.105, bf16[1408,1232]{1,0:T(8,128)(2,1)} %bitcast.16), kind=kOutput, calls=%fused_computation.13 | convolution fusion | flops 507871232 | bytes 3244032 | tf_op jit(solution)/shard_map/dot_general | solution.py:163
  202.4 2.9 %collective-permute-start.8 = (bf16[256,1408]{1,0:T(8,128)(2,1)S(1)}, bf16[256,1408]{1,0:T(8,128)(2,1)S(1)}, u32[]{:S(2)}, u32[]{:S(2)}) collective-permute-start(bf16[256,1408]{1,0:T(8,128)(2,1)S(1)} %convolution_convert_fusion), channel_id=1, source_target_pairs={{0,1},{1,0},{2,3},{3,2},{4,5},{5,4},{6,7},{7,6},{8,9},{9,8},{10,11... | collective-permute-start | bytes 2162696 | tf_op jit(solution)/shard_map/ppermute | solution.py:30
  208.8 5.6 %convolution_convert_fusion.5 = bf16[64,704]{1,0:T(8,128)(2,1)S(1)} fusion(bf16[64,5632]{1,0:T(8,128)(2,1)S(1)} %reshape.461, bf16[5632,704]{1,0:T(8,128)(2,1)} %all-gather.3.cloned.1.call-done), kind=kOutput, calls=%fused_computation.53 | convolution fusion | flops 507555840 | bytes 8740864 | tf_op jit(solution)/shard_map/dot_general | solution.py:34
  215.8 4.6 %all-to-all-start.4 = ((bf16[64,8,768]{2,1,0:T(8,128)(2,1)}), bf16[64,8,768]{2,1,0:T(8,128)(2,1)S(1)}, u32[]{:S(2)}, u32[]{:S(2)}) async-start(bf16[64,8,768]{2,1,0:T(8,128)(2,1)} %fusion.32), calls=%async_computation.4 | async-start | bytes 1572864 | tf_op jit(solution)/shard_map/all_to_all | solution.py:172
  220.8 24.5 %all-to-all-done.4 = bf16[64,8,768]{2,1,0:T(8,128)(2,1)S(1)} async-done(((bf16[64,8,768]{2,1,0:T(8,128)(2,1)}), bf16[64,8,768]{2,1,0:T(8,128)(2,1)S(1)}, u32[]{:S(2)}, u32[]{:S(2)}) %all-to-all-start.4) | async-done | bytes 786464 | tf_op jit(solution)/shard_map/all_to_all | solution.py:172
  245.6 2.3 collective-permute-start.9
  250.2 2.6 fusion.94
  253.2 2.7 fusion.9
  257.0 6.6 %fusion.6 = bf16[512,1408]{1,0:T(8,128)(2,1)} fusion(bf16[512,1408]{1,0:T(8,128)(2,1)S(1)} %fusion.9, bf16[1408,2816]{1,0:T(8,128)(2,1)} %all-gather.5.cloned.1.call-done), kind=kOutput, calls=%fused_computation.8 | convolution fusion | flops 2030764032 | bytes 6848512 | tf_op jit(solution)/shard_map/dot_general | solution.py:34
  265.3 2.7 fusion.33
  269.4 2.8 convolution_convert_fusion.1
  273.8 2.3 fusion.10
  (123 shorter events, 39.3 us)
Async XLA Ops:
  6.5 24.9 %copy-start.3 = (bf16[11,1,3,704]{3,2,1,0:T(4,128)(2,1)S(1)}, bf16[11,1,3,704]{3,2,1,0:T(4,128)(2,1)}, u32[]{:S(2)}) copy-start(bf16[11,1,3,704]{3,2,1,0:T(4,128)(2,1)} %param.20) | copy-start | bytes 139396
  6.5 25.3 %copy-start.4 = (bf16[704,22]{0,1:T(8,128)(2,1)S(1)}, bf16[704,22]{0,1:T(8,128)(2,1)}, u32[]{:S(2)}) copy-start(bf16[704,22]{0,1:T(8,128)(2,1)} %param.15) | copy-start | bytes 92932
  8.3 24.8 %all-to-all-start = ((bf16[4,88,704]{2,1,0:T(8,128)(2,1)}), bf16[4,88,704]{2,1,0:T(8,128)(2,1)S(1)}, u32[]{:S(2)}, u32[]{:S(2)}) async-start(bf16[4,88,704]{2,1,0:T(8,128)(2,1)} %broadcast_in_dim.27), calls=%async_computation | async-start | bytes 1081344 | tf_op jit(solution)/shard_map/all_to_all | solution.py:40
  17.3 191.5 %all-gather.3.cloned.1.call-start = ((), (), s32[]{:S(2)}) async-start(), calls=%async_computation.5 | async-start | bytes 9191424 | tf_op jit(solution)/shard_map/all_gather | solution.py:81
  19.0 12.4 %collective-permute-start.4 = (bf16[4,11,704]{2,0,1:T(4,128)(2,1)S(1)}, bf16[4,11,704]{2,0,1:T(4,128)(2,1)S(1)}, u32[]{:S(2)}, u32[]{:S(2)}) collective-permute-start(bf16[4,11,704]{2,0,1:T(4,128)(2,1)S(1)} %pad_maximum_fusion.7), channel_id=1, source_target_pairs={{0,128},{128,0},{1,129},{129,1},{2,130},{130,2},{3,131},{131,3},{4... | collective-permute-start | bytes 185864 | tf_op jit(solution)/shard_map/ppermute | solution.py:74
  31.9 7.2 %copy-start = (bf16[256,1408]{1,0:T(8,128)(2,1)S(1)}, bf16[256,1408]{1,0:T(8,128)(2,1)}, u32[]{:S(2)}) copy-start(bf16[256,1408]{1,0:T(8,128)(2,1)} %param.12) | copy-start | bytes 2162692
  33.1 0.8 copy-start.1
  33.9 26.8 %all-to-all-start.1 = ((bf16[4,132,704]{2,1,0:T(8,128)(2,1)}), bf16[4,132,704]{2,1,0:T(8,128)(2,1)S(1)}, u32[]{:S(2)}, u32[]{:S(2)}) async-start(bf16[4,132,704]{2,1,0:T(8,128)(2,1)} %fusion.37), calls=%async_computation.1 | async-start | bytes 1671168 | tf_op jit(solution)/shard_map/all_to_all | solution.py:82
  39.1 216.8 %all-gather.5.cloned.1.call-start = ((), (), s32[]{:S(2)}) async-start(), calls=%async_computation.6 | async-start | bytes 8425472 | tf_op jit(solution)/shard_map/all_gather | solution.py:93
  60.9 1.7 copy-start.6
  63.6 15.8 %collective-permute-start = (bf16[144,1408]{1,0:T(8,128)(2,1)S(1)}, bf16[144,1408]{1,0:T(8,128)(2,1)S(1)}, u32[]{:S(2)}, u32[]{:S(2)}) collective-permute-start(bf16[144,1408]{1,0:T(8,128)(2,1)S(1)} %fusion.41), channel_id=1, source_target_pairs={{0,2},{2,4},{4,6},{6,0},{1,3},{3,5},{5,7},{7,1},{8,10},{10,12},{12... | collective-permute-start | bytes 1216520 | tf_op jit(solution)/shard_map/ppermute | solution.py:127
  66.6 23.1 %collective-permute-start.1 = (bf16[144,1408]{1,0:T(8,128)(2,1)S(1)}, bf16[144,1408]{1,0:T(8,128)(2,1)S(1)}, u32[]{:S(2)}, u32[]{:S(2)}) collective-permute-start(bf16[144,1408]{1,0:T(8,128)(2,1)S(1)} %fusion.41), channel_id=1, source_target_pairs={{0,4},{2,6},{4,0},{6,2},{1,5},{3,7},{5,1},{7,3},{8,12},{10,14},{12... | collective-permute-start | bytes 1216520 | tf_op jit(solution)/shard_map/ppermute | solution.py:127
  66.8 31.6 %collective-permute-start.2 = (bf16[144,1408]{1,0:T(8,128)(2,1)S(1)}, bf16[144,1408]{1,0:T(8,128)(2,1)S(1)}, u32[]{:S(2)}, u32[]{:S(2)}) collective-permute-start(bf16[144,1408]{1,0:T(8,128)(2,1)S(1)} %fusion.41), channel_id=1, source_target_pairs={{0,6},{2,0},{4,2},{6,4},{1,7},{3,1},{5,3},{7,5},{8,14},{10,8},{12,... | collective-permute-start | bytes 1216520 | tf_op jit(solution)/shard_map/ppermute | solution.py:127
  72.6 103.6 %all-to-all-start.2 = ((bf16[16,88,1232]{2,1,0:T(8,128)(2,1)}), bf16[16,88,1232]{2,1,0:T(8,128)(2,1)}, u32[]{:S(2)}, u32[]{:S(2)}) async-start(bf16[16,88,1232]{2,1,0:T(8,128)(2,1)} %broadcast_in_dim.28), calls=%async_computation.2 | async-start | bytes 7208960 | tf_op jit(solution)/shard_map/all_to_all | solution.py:40
  99.7 3.1 %collective-permute-start.3 = (bf16[3,128,1408]{2,1,0:T(8,128)(2,1)}, bf16[3,128,1408]{2,1,0:T(8,128)(2,1)}, u32[]{:S(2)}, u32[]{:S(2)}) collective-permute-start(bf16[3,128,1408]{2,1,0:T(8,128)(2,1)} %slice.107), channel_id=1, source_target_pairs={{0,1},{1,0},{2,3},{3,2},{4,5},{5,4},{6,7},{7,6},{8,9},{9,8},{10,11... | collective-permute-start | bytes 3244040 | tf_op jit(solution)/shard_map/ppermute | solution.py:30
  104.2 1.0 copy-start.2
  105.2 19.5 %collective-permute-start.5 = (bf16[128,1408]{1,0:T(8,128)(2,1)S(1)}, bf16[128,1408]{1,0:T(8,128)(2,1)S(1)}, u32[]{:S(2)}, u32[]{:S(2)}) collective-permute-start(bf16[128,1408]{1,0:T(8,128)(2,1)S(1)} %copy-done.2), channel_id=1, source_target_pairs={{0,6},{2,8},{4,10},{6,12},{8,14},{10,16},{12,18},{14,20},{16,22},{... | collective-permute-start | bytes 1081352 | tf_op jit(solution)/shard_map/ppermute | solution.py:138
  110.6 31.3 %collective-permute-start.6 = (bf16[128,1408]{1,0:T(8,128)(2,1)S(1)}, bf16[128,1408]{1,0:T(8,128)(2,1)S(1)}, u32[]{:S(2)}, u32[]{:S(2)}) collective-permute-start(bf16[128,1408]{1,0:T(8,128)(2,1)S(1)} %copy-done.2), channel_id=1, source_target_pairs={{0,4},{2,6},{4,8},{6,10},{8,12},{10,14},{12,16},{14,18},{16,20},{1... | collective-permute-start | bytes 1081352 | tf_op jit(solution)/shard_map/ppermute | solution.py:138
  116.2 35.4 %collective-permute-start.7 = (bf16[128,1408]{1,0:T(8,128)(2,1)S(1)}, bf16[128,1408]{1,0:T(8,128)(2,1)S(1)}, u32[]{:S(2)}, u32[]{:S(2)}) collective-permute-start(bf16[128,1408]{1,0:T(8,128)(2,1)S(1)} %copy-done.2), channel_id=1, source_target_pairs={{0,2},{2,4},{4,6},{6,8},{8,10},{10,12},{12,14},{14,16},{16,18},{18... | collective-permute-start | bytes 1081352 | tf_op jit(solution)/shard_map/ppermute | solution.py:138
  185.6 4.4 %copy-start.5 = (s32[1,64]{1,0:T(1,128)S(1)}, s32[1,64]{1,0:T(1,128)}, u32[]{:S(2)}) copy-start(s32[1,64]{1,0:T(1,128)} %param.18) | copy-start | bytes 772
  186.5 12.8 %all-to-all-start.3 = ((bf16[4,256,176]{1,2,0:T(8,128)(2,1)}), bf16[4,256,176]{1,2,0:T(8,128)(2,1)S(1)}, u32[]{:S(2)}, u32[]{:S(2)}) async-start(bf16[4,256,176]{1,2,0:T(8,128)(2,1)} %fusion.43), calls=%async_computation.3 | async-start | bytes 720896 | tf_op jit(solution)/shard_map/all_to_all | solution.py:161
  202.4 4.7 %collective-permute-start.8 = (bf16[256,1408]{1,0:T(8,128)(2,1)S(1)}, bf16[256,1408]{1,0:T(8,128)(2,1)S(1)}, u32[]{:S(2)}, u32[]{:S(2)}) collective-permute-start(bf16[256,1408]{1,0:T(8,128)(2,1)S(1)} %convolution_convert_fusion), channel_id=1, source_target_pairs={{0,1},{1,0},{2,3},{3,2},{4,5},{5,4},{6,7},{7,6},{8,9},{9,8},{10,11... | collective-permute-start | bytes 2162696 | tf_op jit(solution)/shard_map/ppermute | solution.py:30
  214.4 6.0 %copy-start.7 = (s32[1,2]{1,0:T(1,128)S(1)}, s32[1,2]{1,0:T(1,128)}, u32[]{:S(2)}) copy-start(s32[1,2]{1,0:T(1,128)} %param.19) | copy-start | bytes 28
  215.8 29.6 %all-to-all-start.4 = ((bf16[64,8,768]{2,1,0:T(8,128)(2,1)}), bf16[64,8,768]{2,1,0:T(8,128)(2,1)S(1)}, u32[]{:S(2)}, u32[]{:S(2)}) async-start(bf16[64,8,768]{2,1,0:T(8,128)(2,1)} %fusion.32), calls=%async_computation.4 | async-start | bytes 1572864 | tf_op jit(solution)/shard_map/all_to_all | solution.py:172
  245.6 4.1 %collective-permute-start.9 = (bf16[512,704]{0,1:T(8,128)(2,1)S(1)}, bf16[512,704]{0,1:T(8,128)(2,1)S(1)}, u32[]{:S(2)}, u32[]{:S(2)}) collective-permute-start(bf16[512,704]{0,1:T(8,128)(2,1)S(1)} %copy.74), channel_id=1, source_target_pairs={{0,1},{1,0},{2,3},{3,2},{4,5},{5,4},{6,7},{7,6},{8,9},{9,8},{10,11... | collective-permute-start | bytes 2162696 | tf_op jit(solution)/shard_map/ppermute | solution.py:30
  255.9 1.1 copy-start.8
  272.3 1.5 collective-permute-start.10
Sparse Core Ops, SparseCore 0:
  34.1 135.7 all-gather.2
  172.3 80.6 all-gather.4

commit v3 on v2

--- a/solution.py
+++ b/solution.py
@@ -32,6 +32,17 @@
 
 def dot(a, b):
     return jnp.dot(a, b, preferred_element_type=F32)
+
+
+def both_halves(part, first):
+    other = swap_sub(part)
+    return jnp.concatenate(
+        [jnp.where(first, part, other), jnp.where(first, other, part)], axis=1
+    )
+
+
+def pad_to(columns):
+    return -columns % 128
 
 
 def to_all(value, axes):
@@ -62,11 +73,19 @@
     krows = vision_inproj.shape[0]
     mrows = merger_weight.shape[0]
 
-    line_m = to_all(merger_weight, "zh").reshape(lines * mrows, half)
-
     vin = vision_inproj.reshape(krows, 3, lines, quarter).transpose(2, 0, 1, 3)
     vin = vin.reshape(lines, krows, 3 * quarter)
-    vin = jnp.pad(vin, ((0, 0), (0, 0), (0, half - 3 * quarter)))
+    vin = jnp.pad(vin, ((0, 0), (0, 0), (0, pad_to(3 * quarter))))
+    vout = jnp.pad(vision_outproj.T, ((0, 0), (0, pad_to(half))))
+    vout = jnp.broadcast_to(vout[None], (lines,) + vout.shape)
+    line = jnp.concatenate([vin, vout], axis=2)
+    line = lax.all_to_all(line, "zh", split_axis=0, concat_axis=0, tiled=True)
+    split_out = vin.shape[2]
+    split_merge = line.shape[2]
+    line_v = line.reshape(lines * krows, split_merge)
+    merge = jnp.pad(merger_weight, ((0, 0), (0, pad_to(half))))
+    line_v = jnp.concatenate([line_v, merge], axis=1)
+
     drows = decoder_inproj.shape[0]
     dec = jnp.concatenate(
         [decoder_inproj.reshape(drows, 3, half).transpose(1, 0, 2), decoder_outproj.T[None]], axis=0
@@ -74,26 +93,14 @@
     dec_other = lax.ppermute(dec, "grp", [(0, 1), (1, 0)])
     low = lax.axis_index("grp") == 0
     dec = jnp.stack([jnp.where(low, dec, dec_other), jnp.where(low, dec_other, dec)], axis=1)
-    rest = jnp.concatenate([vision_outproj.T, dec.reshape(8 * drows, half)], axis=0)
-    rest = jnp.broadcast_to(rest[None], (lines,) + rest.shape)
-    line = jnp.concatenate([vin, rest], axis=1)
-    line, line_m = lax.optimization_barrier((line, line_m))
-    w_merge = lax.all_gather(line_m, PLANE, axis=0, tiled=True)
-    line = lax.all_to_all(line, "zh", split_axis=0, concat_axis=0, tiled=True)
-    kline = lines * krows
-    line_v = jnp.concatenate(
-        [
-            line[:, :krows, : 3 * quarter].reshape(kline, 3 * quarter),
-            line[:, krows : 2 * krows].reshape(kline, half),
-        ],
-        axis=1,
-    )
-    line_d = line[:, 2 * krows :].reshape(lines, 4, 2 * drows, half).transpose(0, 2, 1, 3)
+    dec = dec.reshape(8 * drows, half)
+    patch_rows = patches.astype(F32)
+    normed = layer_norm(patch_rows).astype(BF)
+    line_v, dec, normed = lax.optimization_barrier((line_v, dec, normed))
+    full_v = lax.all_gather(line_v, PLANE, axis=0, tiled=True)
+    line_d = to_all(dec, "zh").reshape(lines, 4, 2 * drows, half).transpose(0, 2, 1, 3)
     line_d = line_d.reshape(lines * 2 * drows, 4 * half)
     full_d = lax.all_gather(line_d, PLANE, axis=0, tiled=True)
-    full_v = to_all(line_v, PLANE).reshape(width, 3 * quarter + half)
-    w_in = full_v[:, : 3 * quarter]
-    w_out = full_v[:, 3 * quarter :]
     order = jnp.arange(width, dtype=jnp.int32)
     natural = (
         order // drows % 2 * (width // 2) + order // (2 * drows) * drows + order % drows
@@ -115,30 +122,29 @@
     wanted = wanted & ((dest % cap)[:, None] == slot[None, :])
     window_rows = reach * piece_rows
 
-    patch_rows = patches.astype(F32)
     first = lax.axis_index("sub") == 0
     ends = jnp.cumsum(image_sizes[0]).astype(BF)
     mark = jnp.zeros((16, width), BF).at[0, : ends.shape[0]].set(ends)
-    normed = layer_norm(patch_rows).astype(BF)
     side = rows_v // 2
-    top, bottom = normed[:side], normed[side:]
-    mine = jnp.concatenate([jnp.where(first, top, bottom), mark], axis=0)
-    moved = [
-        lax.ppermute(mine, "zh", [(i, (i + s) % lines) for i in range(lines)])
-        for s in range(1, lines)
-    ]
-    moved = jnp.stack(moved)
-    traded = swap_sub(moved[:, :side])
-    kept = moved[:, :side]
-    others = jnp.concatenate(
-        [jnp.where(first, kept, traded), jnp.where(first, traded, kept)], axis=1
-    )
-    text, others = lax.optimization_barrier((text_embed, others))
-    earlier = [
-        lax.ppermute(text, TOK, [(i, i + s) for i in range(pieces - s)])
-        for s in range(REACH, 0, -1)
-    ]
-    window_text = jnp.concatenate(earlier + [text], axis=0)
+    mine = jnp.concatenate([jnp.where(first, normed[:side], normed[side:]), mark], axis=0)
+    moved = jnp.stack(
+        [
+            lax.ppermute(mine, "zh", [(i, (i + s) % lines) for i in range(lines)])
+            for s in range(1, lines)
+        ]
+    )
+    others = both_halves(moved[:, :side], first)
+    text, others, reorder = lax.optimization_barrier((text_embed, others, reorder))
+    side_t = piece_rows // 2
+    mine = jnp.where(first, text[:side_t], text[side_t:])
+    earlier = jnp.stack(
+        [
+            lax.ppermute(mine, TOK, [(i, i + s) for i in range(pieces - s)])
+            for s in range(REACH, 0, -1)
+        ]
+    )
+    earlier = both_halves(earlier, first).reshape(REACH * piece_rows, width)
+    window_text = jnp.concatenate([earlier, text], axis=0)
 
     normed = jnp.concatenate([normed[None], others]).reshape(lines * rows_v, width)
     ends_all = jnp.concatenate([ends[None], moved[:, side, : ends.shape[0]]]).astype(jnp.int32)
@@ -147,7 +153,7 @@
         (group_ids[None, :, None] >= ends_all[:, None, :]).astype(jnp.int32), axis=2
     )
     same = (image_ids[:, :, None] == image_ids[:, None, :]).astype(F32)
-    projected = dot(normed, w_in).astype(BF)
+    projected = dot(normed, full_v[:, : 3 * quarter]).astype(BF)
     triple = projected.reshape(lines, rows_v, 3, heads_line, HD)
     scores = jnp.einsum(
         "pqhe,pkhe->phqk", triple[:, :, 0], triple[:, :, 1], preferred_element_type=F32
@@ -160,27 +166,31 @@
     heads, window_text = lax.optimization_barrier((heads, window_text))
     heads = lax.all_to_all(heads, "zh", split_axis=0, concat_axis=0, tiled=True)
     heads = heads.transpose(1, 0, 2).reshape(rows_v, half)
+    w_out = full_v[:, split_out : split_out + half]
     partial = lax.dot_general(heads, w_out, (((1,), (1,)), ((), ())), preferred_element_type=F32)
     partial = partial.astype(BF)
     hidden = patch_rows + (partial.astype(F32) + swap_sub(partial).astype(F32))
-    merged = layer_norm(hidden).astype(BF).reshape(rows_v // 4, 4 * width)
-    embedded = dot(merged, w_merge).astype(BF)
+    tokens = rows_v // 4
+    merged = layer_norm(hidden).astype(BF).reshape(tokens, planes, lines, mrows)
+    merged = merged.transpose(2, 0, 1, 3).reshape(lines, tokens, planes * mrows)
+    merged = lax.all_to_all(merged, "zh", split_axis=0, concat_axis=0, tiled=True)
+    partial = dot(merged.reshape(lines * tokens, planes * mrows), full_v[:, split_merge : split_merge + half])
+    partial = partial.astype(BF).reshape(lines, tokens, half)
+    partial = lax.all_to_all(partial, "zh", split_axis=0, concat_axis=0, tiled=True)
+    embedded = jnp.sum(partial.astype(F32), axis=0).astype(BF)
 
     note = jnp.stack([target_row, jnp.ones_like(target_row)], axis=1).astype(BF)
-    note = jnp.pad(note, ((0, 0), (0, 62)))
+    note = jnp.pad(note, ((0, 0), (0, pad_to(half) - 2)))
     sent = dot(wanted.astype(BF), jnp.concatenate([embedded, note], axis=1)).astype(BF)
     got = lax.all_to_all(
-        sent.reshape(pieces, slots, half + 64), TOK, split_axis=0, concat_axis=0, tiled=True
-    ).reshape(pieces * slots, half + 64)
+        sent.reshape(pieces, slots, half + pad_to(half)), TOK, split_axis=0, concat_axis=0, tiled=True
+    ).reshape(pieces * slots, half + pad_to(half))
     note = got[:, half : half + 2].astype(jnp.int32)
     arrived = jnp.arange(pieces * slots, dtype=jnp.int32) // cap % reach
     arrived = jnp.where(note[:, 1] > 0, (REACH - arrived) * piece_rows + note[:, 0], window_rows)
     place = jnp.arange(window_rows, dtype=jnp.int32)[:, None] == arrived[None, :]
     got = got[:, :half]
-    other = swap_sub(got)
-    image_full = jnp.concatenate(
-        [jnp.where(first, got, other), jnp.where(first, other, got)], axis=1
-    )
+    image_full = both_halves(got, first)
     placed = dot(place.astype(BF), image_full)
     filled = jnp.any(place, axis=1)
     decoder_input = jnp.where(filled[:, None], placed, window_text.astype(F32))

time: 284 us -> 283 us (level)
  waiting for transfers between devices: 146 us -> 101 us
  starting transfers between devices: 55.1 us -> 77.2 us
  blocking collectives: 0 us -> 16.8 us
  other arithmetic: 13.1 us -> 17.7 us
    all_to_all x2 -> x1, waiting for transfers between devices: 23.5 us -> 0.01 us  [to_all(): return lax.all_to_all(spread, axes, split_axis=0, concat_axis=0, tiled=True)]
    ppermute x3, waiting for transfers between devices: 31.7 us -> 11 us  [shards(): lax.ppermute(mine, TOK, [(i, i + s) for i in range(pieces - s)])]
    all_to_all x2 -> x3, starting transfers between devices: 8.1 us -> 26.8 us  [the longest x1 15.3 us: shards(): lax.all_to_all(sent.reshape(pieces, slots, half + pad_to(half)), TOK, spl...]
    all_to_all x0 -> x1, blocking collectives: none -> 16.8 us  [shards(): heads = lax.all_to_all(heads, 'zh', split_axis=0, concat_axis=0, tiled=True)]
    ppermute x3, waiting for transfers between devices: 19 us -> 34.4 us  [shards(): lax.ppermute(mine, 'zh', [(i, (i + s) % lines) for i in range(lines)])]
    all_to_all x1, waiting for transfers between devices: 21.4 us -> 6.92 us  [shards(): line = lax.all_to_all(line, 'zh', split_axis=0, concat_axis=0, tiled=True)]
    all_to_all x2 -> x1, starting transfers between devices: 15.8 us -> 4.24 us  [to_all(): return lax.all_to_all(spread, axes, split_axis=0, concat_axis=0, tiled=True)]
    all_to_all x2 -> x3, waiting for transfers between devices: 33.7 us -> 44.5 us  [the longest x1 21.7 us: shards(): lax.all_to_all(sent.reshape(pieces, slots, half + pad_to(half)), TOK, spl...]
  transfers between devices with their start and end apart: 18 -> 19, of which waited for: 14 -> 13; matrix products, arithmetic and copies ran while one was open for 16% -> 17% of each run, Pallas kernels for 0% -> 0%
where the time goes in v3:
time: 283 us; the launch traced here: 282 us
  waiting for transfers between devices  101 us (36%)
  starting transfers between devices  77.2 us (27%)
  matrix products  36.1 us (13%)
  local copies, waits for them, and re-layouts  19.4 us (7%)
  other arithmetic  17.7 us (6%)
  blocking collectives  16.8 us (6%)
  between operations  14 us (5%)
    ppermute x3, waiting for transfers between devices, shards(): lax.ppermute(mine, 'zh', [(i, (i + s) % lines) for i in range(lines)])  34.4 us
    dot_general x7, matrix products, dot(): return jnp.dot(a, b, preferred_element_type=F32)  24 us
    all_to_all x1, waiting for transfers between devices, shards(): lax.all_to_all(sent.reshape(pieces, slots, half + pad_to(half)), TOK, spl...  21.7 us
    all_to_all x1, blocking collectives, shards(): heads = lax.all_to_all(heads, 'zh', split_axis=0, concat_axis=0, tiled=True)  16.8 us
    ppermute x3, starting transfers between devices, shards(): lax.ppermute(mine, TOK, [(i, i + s) for i in range(pieces - s)])  15.9 us
    all_to_all x1, starting transfers between devices, shards(): lax.all_to_all(sent.reshape(pieces, slots, half + pad_to(half)), TOK, spl...  15.3 us
    all_to_all x1, waiting for transfers between devices, shards(): lax.all_to_all(merged, 'zh', split_axis=0, concat_axis=0, tiled=True)  14.2 us
    ppermute x5, starting transfers between devices, swap_sub(): return lax.ppermute(value, 'sub', [(0, 1), (1, 0)])  11.4 us
  transfers between devices with their start and end apart: 19, of which 13 were waited for; matrix products, arithmetic and copies ran while one was open for 17% of the time, Pallas kernels for 0%

profile of v3, /device:TPU:1, one launch (start us, length us, event | category | flops | bytes accessed | tf_op | source)
XLA Modules:
  0.0 282.0 jit_solution(8578182631037667354)
XLA Ops:
  8.3 2.6 collective-permute-start
  13.7 7.3 %all-to-all-start = ((bf16[4,22,1408]{2,1,0:T(8,128)(2,1)}), bf16[4,22,1408]{2,1,0:T(8,128)(2,1)S(1)}, u32[]{:S(2)}, u32[]{:S(2)}) async-start(bf16[4,22,1408]{2,1,0:T(8,128)(2,1)} %fusion.47), calls=%async_computation | async-start | bytes 540672 | tf_op jit(solution)/shard_map/all_to_all | solution.py:82
  22.3 6.9 %all-to-all-done = bf16[4,22,1408]{2,1,0:T(8,128)(2,1)S(1)} async-done(((bf16[4,22,1408]{2,1,0:T(8,128)(2,1)}), bf16[4,22,1408]{2,1,0:T(8,128)(2,1)S(1)}, u32[]{:S(2)}, u32[]{:S(2)}) %all-to-all-start) | async-done | bytes 247840 | tf_op jit(solution)/shard_map/all_to_all | solution.py:82
  31.2 4.2 %all-to-all-start.5 = ((bf16[4,88,704]{2,1,0:T(8,128)(2,1)}), bf16[4,88,704]{2,1,0:T(8,128)(2,1)S(1)}, u32[]{:S(2)}, u32[]{:S(2)}) async-start(bf16[4,88,704]{2,1,0:T(8,128)(2,1)} %broadcast_in_dim.27), calls=%async_computation.5 | async-start | bytes 1081344 | tf_op jit(solution)/shard_map/all_to_all | solution.py:51
  37.9 3.3 %collective-permute-start.2 = (bf16[144,1408]{1,0:T(8,128)(2,1)S(1)}, bf16[144,1408]{1,0:T(8,128)(2,1)S(1)}, u32[]{:S(2)}, u32[]{:S(2)}) collective-permute-start(bf16[144,1408]{1,0:T(8,128)(2,1)S(1)} %fusion.41), channel_id=1, source_target_pairs={{0,4},{2,6},{4,0},{6,2},{1,5},{3,7},{5,1},{7,3},{8,12},{10,14},{12... | collective-permute-start | bytes 1216520 | tf_op jit(solution)/shard_map/ppermute | solution.py:132
  41.2 3.3 %collective-permute-start.3 = (bf16[144,1408]{1,0:T(8,128)(2,1)S(1)}, bf16[144,1408]{1,0:T(8,128)(2,1)S(1)}, u32[]{:S(2)}, u32[]{:S(2)}) collective-permute-start(bf16[144,1408]{1,0:T(8,128)(2,1)S(1)} %fusion.41), channel_id=1, source_target_pairs={{0,6},{2,0},{4,2},{6,4},{1,7},{3,1},{5,3},{7,5},{8,14},{10,8},{12,... | collective-permute-start | bytes 1216520 | tf_op jit(solution)/shard_map/ppermute | solution.py:132
  44.5 12.8 %collective-permute-done.1 = bf16[144,1408]{1,0:T(8,128)(2,1)S(1)} collective-permute-done((bf16[144,1408]{1,0:T(8,128)(2,1)S(1)}, bf16[144,1408]{1,0:T(8,128)(2,1)S(1)}, u32[]{:S(2)}, u32[]{:S(2)}) %collective-permute-start.1) | collective-permute-done | bytes 405536 | tf_op jit(solution)/shard_map/ppermute | solution.py:132
  57.4 14.6 %collective-permute-done.2 = bf16[144,1408]{1,0:T(8,128)(2,1)S(1)} collective-permute-done((bf16[144,1408]{1,0:T(8,128)(2,1)S(1)}, bf16[144,1408]{1,0:T(8,128)(2,1)S(1)}, u32[]{:S(2)}, u32[]{:S(2)}) %collective-permute-start.2) | collective-permute-done | bytes 405536 | tf_op jit(solution)/shard_map/ppermute | solution.py:132
  72.0 7.0 %collective-permute-done.3 = bf16[144,1408]{1,0:T(8,128)(2,1)S(1)} collective-permute-done((bf16[144,1408]{1,0:T(8,128)(2,1)S(1)}, bf16[144,1408]{1,0:T(8,128)(2,1)S(1)}, u32[]{:S(2)}, u32[]{:S(2)}) %collective-permute-start.3) | collective-permute-done | bytes 405536 | tf_op jit(solution)/shard_map/ppermute | solution.py:132
  80.2 3.8 %collective-permute-start.4 = (bf16[3,128,1408]{2,1,0:T(8,128)(2,1)}, bf16[3,128,1408]{2,1,0:T(8,128)(2,1)}, u32[]{:S(2)}, u32[]{:S(2)}) collective-permute-start(bf16[3,128,1408]{2,1,0:T(8,128)(2,1)} %slice.104), channel_id=1, source_target_pairs={{0,1},{1,0},{2,3},{3,2},{4,5},{5,4},{6,7},{7,6},{8,9},{9,8},{10,11... | collective-permute-start | bytes 3244040 | tf_op jit(solution)/shard_map/ppermute | solution.py:30
  85.7 3.5 %fusion = bf16[1408,1408]{1,0:T(8,128)(2,1)} fusion(s32[1408]{0:T(1024)S(1)} %fusion.70), kind=kLoop, calls=%fused_computation.1 | loop fusion | flops 3964928 | bytes 3970560 | tf_op jit(solution)/shard_map/convert_element_type | solution.py:108
  92.4 8.1 %collective-permute-start.5 = (bf16[64,1408]{1,0:T(8,128)(2,1)S(1)}, bf16[64,1408]{1,0:T(8,128)(2,1)S(1)}, u32[]{:S(2)}, u32[]{:S(2)}) collective-permute-start(bf16[64,1408]{1,0:T(8,128)(2,1)S(1)} %slice_select_fusion.1), channel_id=1, source_target_pairs={{0,6},{2,8},{4,10},{6,12},{8,14},{10,16},{12,18},{14,20},{16,22},{... | collective-permute-start | bytes 540680 | tf_op jit(solution)/shard_map/ppermute | solution.py:142
  100.5 6.5 %collective-permute-start.6 = (bf16[64,1408]{1,0:T(8,128)(2,1)S(1)}, bf16[64,1408]{1,0:T(8,128)(2,1)S(1)}, u32[]{:S(2)}, u32[]{:S(2)}) collective-permute-start(bf16[64,1408]{1,0:T(8,128)(2,1)S(1)} %slice_select_fusion.1), channel_id=1, source_target_pairs={{0,4},{2,6},{4,8},{6,10},{8,12},{10,14},{12,16},{14,18},{16,20},{1... | collective-permute-start | bytes 540680 | tf_op jit(solution)/shard_map/ppermute | solution.py:142
  108.4 4.3 %collective-permute-done.5 = bf16[64,1408]{1,0:T(8,128)(2,1)S(1)} collective-permute-done((bf16[64,1408]{1,0:T(8,128)(2,1)S(1)}, bf16[64,1408]{1,0:T(8,128)(2,1)S(1)}, u32[]{:S(2)}, u32[]{:S(2)}) %collective-permute-start.5) | collective-permute-done | bytes 180256 | tf_op jit(solution)/shard_map/ppermute | solution.py:142
  115.2 4.3 %collective-permute-done.7 = bf16[64,1408]{1,0:T(8,128)(2,1)S(1)} collective-permute-done((bf16[64,1408]{1,0:T(8,128)(2,1)S(1)}, bf16[64,1408]{1,0:T(8,128)(2,1)S(1)}, u32[]{:S(2)}, u32[]{:S(2)}) %collective-permute-start.7) | collective-permute-done | bytes 180256 | tf_op jit(solution)/shard_map/ppermute | solution.py:142
  124.7 5.4 %fusion.18 = bf16[1024,528]{0,1:T(8,128)(2,1)} fusion(bf16[1024,1408]{1,0:T(8,128)(2,1)} %bitcast.108, bf16[1408,2176]{1,0:T(8,128)(2,1)} %all-gather.3.cloned.1.call-done), kind=kOutput, calls=%fused_computation.33 | convolution fusion | flops 1523073024 | bytes 5767168 | tf_op jit(solution)/shard_map/dot_general | solution.py:34
  134.4 16.8 %all_to_all.30 = bf16[4,256,176]{1,2,0:T(8,128)(2,1)S(1)} all-to-all(bf16[4,256,176]{1,2,0:T(8,128)(2,1)S(1)} %fusion.44), channel_id=1, replica_groups=mesh['grp'=2,'y'=4,'x'=4,'zh'=4,'sub'=2] {'zh'}, dimensions={0} | all-to-all | bytes 720896 | tf_op jit(solution)/shard_map/all_to_all | solution.py:167
  153.7 3.4 %collective-permute-start.9 = (bf16[256,1408]{1,0:T(8,128)(2,1)S(1)}, bf16[256,1408]{1,0:T(8,128)(2,1)S(1)}, u32[]{:S(2)}, u32[]{:S(2)}) collective-permute-start(bf16[256,1408]{1,0:T(8,128)(2,1)S(1)} %convolution_convert_fusion.1), channel_id=1, source_target_pairs={{0,1},{1,0},{2,3},{3,2},{4,5},{5,4},{6,7},{7,6},{8,9},{9,8},{10,11... | collective-permute-start | bytes 2162696 | tf_op jit(solution)/shard_map/ppermute | solution.py:30
  164.6 3.5 %all-to-all-start.2 = ((bf16[4,64,1408]{2,1,0:T(8,128)(2,1)}), bf16[4,64,1408]{2,1,0:T(8,128)(2,1)S(1)}, u32[]{:S(2)}, u32[]{:S(2)}) async-start(bf16[4,64,1408]{2,1,0:T(8,128)(2,1)} %reshape.462), calls=%async_computation.2 | async-start | bytes 1441792 | tf_op jit(solution)/shard_map/all_to_all | solution.py:176
  168.4 14.2 %all-to-all-done.2 = bf16[4,64,1408]{2,1,0:T(8,128)(2,1)S(1)} async-done(((bf16[4,64,1408]{2,1,0:T(8,128)(2,1)}), bf16[4,64,1408]{2,1,0:T(8,128)(2,1)S(1)}, u32[]{:S(2)}, u32[]{:S(2)}) %all-to-all-start.2) | async-done | bytes 720928 | tf_op jit(solution)/shard_map/all_to_all | solution.py:176
  182.6 2.6 fusion.29
  186.1 8.0 %all-to-all-start.3 = ((bf16[4,64,704]{2,1,0:T(8,128)(2,1)}), bf16[4,64,704]{2,1,0:T(8,128)(2,1)S(1)}, u32[]{:S(2)}, u32[]{:S(2)}) async-start(bf16[4,64,704]{2,1,0:T(8,128)(2,1)} %bitcast.28), calls=%async_computation.3 | async-start | bytes 786432 | tf_op jit(solution)/shard_map/all_to_all | solution.py:179
  194.3 8.6 %all-to-all-done.3 = bf16[4,64,704]{2,1,0:T(8,128)(2,1)S(1)} async-done(((bf16[4,64,704]{2,1,0:T(8,128)(2,1)}), bf16[4,64,704]{2,1,0:T(8,128)(2,1)S(1)}, u32[]{:S(2)}, u32[]{:S(2)}) %all-to-all-start.3) | async-done | bytes 360480 | tf_op jit(solution)/shard_map/all_to_all | solution.py:179
  204.4 15.3 %all-to-all-start.4 = ((bf16[64,8,768]{2,1,0:T(8,128)(2,1)}), bf16[64,8,768]{2,1,0:T(8,128)(2,1)S(1)}, u32[]{:S(2)}, u32[]{:S(2)}) async-start(bf16[64,8,768]{2,1,0:T(8,128)(2,1)} %fusion.28), calls=%async_computation.4 | async-start | bytes 1572864 | tf_op jit(solution)/shard_map/all_to_all | solution.py:185
  220.1 21.7 %all-to-all-done.4 = bf16[64,8,768]{2,1,0:T(8,128)(2,1)S(1)} async-done(((bf16[64,8,768]{2,1,0:T(8,128)(2,1)}), bf16[64,8,768]{2,1,0:T(8,128)(2,1)S(1)}, u32[]{:S(2)}, u32[]{:S(2)}) %all-to-all-start.4) | async-done | bytes 786464 | tf_op jit(solution)/shard_map/all_to_all | solution.py:185
  242.0 3.1 %collective-permute-start.10 = (bf16[512,704]{0,1:T(8,128)(2,1)S(1)}, bf16[512,704]{0,1:T(8,128)(2,1)S(1)}, u32[]{:S(2)}, u32[]{:S(2)}) collective-permute-start(bf16[512,704]{0,1:T(8,128)(2,1)S(1)} %copy.74), channel_id=1, source_target_pairs={{0,1},{1,0},{2,3},{3,2},{4,5},{5,4},{6,7},{7,6},{8,9},{9,8},{10,11... | collective-permute-start | bytes 2162696 | tf_op jit(solution)/shard_map/ppermute | solution.py:30
  247.3 2.7 fusion.96
  250.5 2.7 convolution_convert_fusion
  254.3 6.6 %fusion.3 = bf16[512,1408]{1,0:T(8,128)(2,1)} fusion(bf16[512,1408]{1,0:T(8,128)(2,1)S(1)} %convolution_convert_fusion, bf16[1408,2816]{1,0:T(8,128)(2,1)} %all-gather.5.cloned.1.call-done), kind=kOutput, calls=%fused_computation.5 | convolution fusion | flops 2030764032 | bytes 6848512 | tf_op jit(solution)/shard_map/dot_general | solution.py:34
  262.6 2.7 fusion.32
  266.8 2.8 convolution_convert_fusion.2
  271.1 4.1 %convolution_convert_fusion.3 = bf16[64,1408]{1,0:T(8,128)(2,1)} fusion(bf16[1408,1408]{1,0:T(8,128)(2,1)} %fusion, bf16[64,1408]{1,0:T(8,128)(2,1)S(1)} %collective-permute-done.11, bf16[128,1408]{1,0:T(8,128)(2,1)S(1)} %convolution_convert_fusion.2, s32[]{:T(128)S(6)} %select_n.249), kind=kOutput, calls=%fused_computation.12 | convolution fusion | flops 254205952 | bytes 4505604 | tf_op jit(solution)/shard_map/dot_general | solution.py:228
  (141 shorter events, 51.7 us)
Async XLA Ops:
  6.5 14.5 %copy-start = (bf16[256,1408]{1,0:T(8,128)(2,1)S(1)}, bf16[256,1408]{1,0:T(8,128)(2,1)}, u32[]{:S(2)}) copy-start(bf16[256,1408]{1,0:T(8,128)(2,1)} %param.12) | copy-start | bytes 2162692
  8.3 13.6 %collective-permute-start = (bf16[4,11,704]{2,0,1:T(4,128)(2,1)S(1)}, bf16[4,11,704]{2,0,1:T(4,128)(2,1)S(1)}, u32[]{:S(2)}, u32[]{:S(2)}) collective-permute-start(bf16[4,11,704]{2,0,1:T(4,128)(2,1)S(1)} %pad_maximum_fusion.7), channel_id=1, source_target_pairs={{0,128},{128,0},{1,129},{129,1},{2,130},{130,2},{3,131},{131,3},{4... | collective-permute-start | bytes 185864 | tf_op jit(solution)/shard_map/ppermute | solution.py:93
  13.0 8.9 %copy-start.9 = (bf16[11,1,3,704]{3,2,1,0:T(4,128)(2,1)S(1)}, bf16[11,1,3,704]{3,2,1,0:T(4,128)(2,1)}, u32[]{:S(2)}) copy-start(bf16[11,1,3,704]{3,2,1,0:T(4,128)(2,1)} %param.20) | copy-start | bytes 139396
  13.7 15.5 %all-to-all-start = ((bf16[4,22,1408]{2,1,0:T(8,128)(2,1)}), bf16[4,22,1408]{2,1,0:T(8,128)(2,1)S(1)}, u32[]{:S(2)}, u32[]{:S(2)}) async-start(bf16[4,22,1408]{2,1,0:T(8,128)(2,1)} %fusion.47), calls=%async_computation | async-start | bytes 540672 | tf_op jit(solution)/shard_map/all_to_all | solution.py:82
  21.0 103.7 %all-gather.3.cloned.1.call-start = ((), (), s32[]{:S(2)}) async-start(), calls=%async_computation.6 | async-start | bytes 6510592 | tf_op jit(solution)/shard_map/all_gather | solution.py:100
  21.2 8.1 %copy-start.10 = (bf16[88,704]{1,0:T(8,128)(2,1)S(1)}, bf16[88,704]{1,0:T(8,128)(2,1)}, u32[]{:S(2)}) copy-start(bf16[88,704]{1,0:T(8,128)(2,1)} %param.16) | copy-start | bytes 371716
  21.6 8.6 %copy-start.11 = (s32[1,4]{1,0:T(1,128)S(1)}, s32[1,4]{1,0:T(1,128)}, u32[]{:S(2)}) copy-start(s32[1,4]{1,0:T(1,128)} %param.13) | copy-start | bytes 52
  31.2 52.8 %all-to-all-start.5 = ((bf16[4,88,704]{2,1,0:T(8,128)(2,1)}), bf16[4,88,704]{2,1,0:T(8,128)(2,1)S(1)}, u32[]{:S(2)}, u32[]{:S(2)}) async-start(bf16[4,88,704]{2,1,0:T(8,128)(2,1)} %broadcast_in_dim.27), calls=%async_computation.5 | async-start | bytes 1081344 | tf_op jit(solution)/shard_map/all_to_all | solution.py:51
  35.4 217.8 %all-gather.5.cloned.1.call-start = ((), (), s32[]{:S(2)}) async-start(), calls=%async_computation.7 | async-start | bytes 8425472 | tf_op jit(solution)/shard_map/all_gather | solution.py:103
  35.5 21.9 %collective-permute-start.1 = (bf16[144,1408]{1,0:T(8,128)(2,1)S(1)}, bf16[144,1408]{1,0:T(8,128)(2,1)S(1)}, u32[]{:S(2)}, u32[]{:S(2)}) collective-permute-start(bf16[144,1408]{1,0:T(8,128)(2,1)S(1)} %fusion.41), channel_id=1, source_target_pairs={{0,2},{2,4},{4,6},{6,0},{1,3},{3,5},{5,7},{7,1},{8,10},{10,12},{12... | collective-permute-start | bytes 1216520 | tf_op jit(solution)/shard_map/ppermute | solution.py:132
  37.9 34.0 %collective-permute-start.2 = (bf16[144,1408]{1,0:T(8,128)(2,1)S(1)}, bf16[144,1408]{1,0:T(8,128)(2,1)S(1)}, u32[]{:S(2)}, u32[]{:S(2)}) collective-permute-start(bf16[144,1408]{1,0:T(8,128)(2,1)S(1)} %fusion.41), channel_id=1, source_target_pairs={{0,4},{2,6},{4,0},{6,2},{1,5},{3,7},{5,1},{7,3},{8,12},{10,14},{12... | collective-permute-start | bytes 1216520 | tf_op jit(solution)/shard_map/ppermute | solution.py:132
  41.2 37.7 %collective-permute-start.3 = (bf16[144,1408]{1,0:T(8,128)(2,1)S(1)}, bf16[144,1408]{1,0:T(8,128)(2,1)S(1)}, u32[]{:S(2)}, u32[]{:S(2)}) collective-permute-start(bf16[144,1408]{1,0:T(8,128)(2,1)S(1)} %fusion.41), channel_id=1, source_target_pairs={{0,6},{2,0},{4,2},{6,4},{1,7},{3,1},{5,3},{7,5},{8,14},{10,8},{12,... | collective-permute-start | bytes 1216520 | tf_op jit(solution)/shard_map/ppermute | solution.py:132
  57.3 22.9 %copy-start.3 = (bf16[144,1408]{1,0:T(8,128)(2,1)}, bf16[144,1408]{1,0:T(8,128)(2,1)S(1)}, u32[]{:S(2)}) copy-start(bf16[144,1408]{1,0:T(8,128)(2,1)S(1)} %collective-permute-done.1) | copy-start | bytes 1216516
  72.0 8.3 %copy-start.5 = (bf16[144,1408]{1,0:T(8,128)(2,1)}, bf16[144,1408]{1,0:T(8,128)(2,1)S(1)}, u32[]{:S(2)}) copy-start(bf16[144,1408]{1,0:T(8,128)(2,1)S(1)} %collective-permute-done.2) | copy-start | bytes 1216516
  79.0 1.3 copy-start.7
  80.2 9.7 %collective-permute-start.4 = (bf16[3,128,1408]{2,1,0:T(8,128)(2,1)}, bf16[3,128,1408]{2,1,0:T(8,128)(2,1)}, u32[]{:S(2)}, u32[]{:S(2)}) collective-permute-start(bf16[3,128,1408]{2,1,0:T(8,128)(2,1)} %slice.104), channel_id=1, source_target_pairs={{0,1},{1,0},{2,3},{3,2},{4,5},{5,4},{6,7},{7,6},{8,9},{9,8},{10,11... | collective-permute-start | bytes 3244040 | tf_op jit(solution)/shard_map/ppermute | solution.py:30
  85.7 3.6 %copy-start.4 = (bf16[144,1408]{1,0:T(8,128)(2,1)S(1)}, bf16[144,1408]{1,0:T(8,128)(2,1)}, u32[]{:S(2)}) copy-start(bf16[144,1408]{1,0:T(8,128)(2,1)} %copy-done.3) | copy-start | bytes 1216516
  85.7 3.6 %copy-start.6 = (bf16[144,1408]{1,0:T(8,128)(2,1)S(1)}, bf16[144,1408]{1,0:T(8,128)(2,1)}, u32[]{:S(2)}) copy-start(bf16[144,1408]{1,0:T(8,128)(2,1)} %copy-done.5) | copy-start | bytes 1216516
  92.4 20.3 %collective-permute-start.5 = (bf16[64,1408]{1,0:T(8,128)(2,1)S(1)}, bf16[64,1408]{1,0:T(8,128)(2,1)S(1)}, u32[]{:S(2)}, u32[]{:S(2)}) collective-permute-start(bf16[64,1408]{1,0:T(8,128)(2,1)S(1)} %slice_select_fusion.1), channel_id=1, source_target_pairs={{0,6},{2,8},{4,10},{6,12},{8,14},{10,16},{12,18},{14,20},{16,22},{... | collective-permute-start | bytes 540680 | tf_op jit(solution)/shard_map/ppermute | solution.py:142
  100.5 14.7 %collective-permute-start.6 = (bf16[64,1408]{1,0:T(8,128)(2,1)S(1)}, bf16[64,1408]{1,0:T(8,128)(2,1)S(1)}, u32[]{:S(2)}, u32[]{:S(2)}) collective-permute-start(bf16[64,1408]{1,0:T(8,128)(2,1)S(1)} %slice_select_fusion.1), channel_id=1, source_target_pairs={{0,4},{2,6},{4,8},{6,10},{8,12},{10,14},{12,16},{14,18},{16,20},{1... | collective-permute-start | bytes 540680 | tf_op jit(solution)/shard_map/ppermute | solution.py:142
  107.0 12.4 %collective-permute-start.7 = (bf16[64,1408]{1,0:T(8,128)(2,1)S(1)}, bf16[64,1408]{1,0:T(8,128)(2,1)S(1)}, u32[]{:S(2)}, u32[]{:S(2)}) collective-permute-start(bf16[64,1408]{1,0:T(8,128)(2,1)S(1)} %slice_select_fusion.1), channel_id=1, source_target_pairs={{0,2},{2,4},{4,6},{6,8},{8,10},{10,12},{12,14},{14,16},{16,18},{18... | collective-permute-start | bytes 540680 | tf_op jit(solution)/shard_map/ppermute | solution.py:142
  119.5 3.7 %collective-permute-start.8 = (bf16[3,64,1408]{2,1,0:T(8,128)(2,1)S(1)}, bf16[3,64,1408]{2,1,0:T(8,128)(2,1)S(1)}, u32[]{:S(2)}, u32[]{:S(2)}) collective-permute-start(bf16[3,64,1408]{2,1,0:T(8,128)(2,1)S(1)} %pad_maximum_fusion.5), channel_id=1, source_target_pairs={{0,1},{1,0},{2,3},{3,2},{4,5},{5,4},{6,7},{7,6},{8,9},{9,8},{10,11... | collective-permute-start | bytes 1622024 | tf_op jit(solution)/shard_map/ppermute | solution.py:30
  130.1 2.9 %copy-start.2 = (f32[4,256,256]{1,2,0:T(8,128)S(1)}, f32[4,256,256]{1,2,0:T(8,128)}, u32[]{:S(2)}) copy-start(f32[4,256,256]{1,2,0:T(8,128)} %compare_convert_fusion) | copy-start | bytes 3145732
  153.7 5.2 %collective-permute-start.9 = (bf16[256,1408]{1,0:T(8,128)(2,1)S(1)}, bf16[256,1408]{1,0:T(8,128)(2,1)S(1)}, u32[]{:S(2)}, u32[]{:S(2)}) collective-permute-start(bf16[256,1408]{1,0:T(8,128)(2,1)S(1)} %convolution_convert_fusion.1), channel_id=1, source_target_pairs={{0,1},{1,0},{2,3},{3,2},{4,5},{5,4},{6,7},{7,6},{8,9},{9,8},{10,11... | collective-permute-start | bytes 2162696 | tf_op jit(solution)/shard_map/ppermute | solution.py:30
  162.3 5.8 %copy-start.12 = (s32[1,64]{1,0:T(1,128)S(1)}, s32[1,64]{1,0:T(1,128)}, u32[]{:S(2)}) copy-start(s32[1,64]{1,0:T(1,128)} %param.18) | copy-start | bytes 772
  164.6 18.0 %all-to-all-start.2 = ((bf16[4,64,1408]{2,1,0:T(8,128)(2,1)}), bf16[4,64,1408]{2,1,0:T(8,128)(2,1)S(1)}, u32[]{:S(2)}, u32[]{:S(2)}) async-start(bf16[4,64,1408]{2,1,0:T(8,128)(2,1)} %reshape.462), calls=%async_computation.2 | async-start | bytes 1441792 | tf_op jit(solution)/shard_map/all_to_all | solution.py:176
  186.1 33.6 %copy-start.13 = (s32[1,2]{1,0:T(1,128)S(1)}, s32[1,2]{1,0:T(1,128)}, u32[]{:S(2)}) copy-start(s32[1,2]{1,0:T(1,128)} %param.19) | copy-start | bytes 28
  186.1 16.8 %all-to-all-start.3 = ((bf16[4,64,704]{2,1,0:T(8,128)(2,1)}), bf16[4,64,704]{2,1,0:T(8,128)(2,1)S(1)}, u32[]{:S(2)}, u32[]{:S(2)}) async-start(bf16[4,64,704]{2,1,0:T(8,128)(2,1)} %bitcast.28), calls=%async_computation.3 | async-start | bytes 786432 | tf_op jit(solution)/shard_map/all_to_all | solution.py:179
  204.4 37.4 %all-to-all-start.4 = ((bf16[64,8,768]{2,1,0:T(8,128)(2,1)}), bf16[64,8,768]{2,1,0:T(8,128)(2,1)S(1)}, u32[]{:S(2)}, u32[]{:S(2)}) async-start(bf16[64,8,768]{2,1,0:T(8,128)(2,1)} %fusion.28), calls=%async_computation.4 | async-start | bytes 1572864 | tf_op jit(solution)/shard_map/all_to_all | solution.py:185
  242.0 4.9 %collective-permute-start.10 = (bf16[512,704]{0,1:T(8,128)(2,1)S(1)}, bf16[512,704]{0,1:T(8,128)(2,1)S(1)}, u32[]{:S(2)}, u32[]{:S(2)}) collective-permute-start(bf16[512,704]{0,1:T(8,128)(2,1)S(1)} %copy.74), channel_id=1, source_target_pairs={{0,1},{1,0},{2,3},{3,2},{4,5},{5,4},{6,7},{7,6},{8,9},{9,8},{10,11... | collective-permute-start | bytes 2162696 | tf_op jit(solution)/shard_map/ppermute | solution.py:30
  247.3 3.2 %copy-start.1 = (bf16[1408,1408]{1,0:T(8,128)(2,1)S(1)}, bf16[1408,1408]{1,0:T(8,128)(2,1)}, u32[]{:S(2)}) copy-start(bf16[1408,1408]{1,0:T(8,128)(2,1)} %fusion) | copy-start | bytes 11894788
  269.6 1.5 collective-permute-start.11
  (2 other events, 2.2 us)
Sparse Core Ops, SparseCore 0:
  30.2 65.9 all-gather.2
  98.7 76.0 all-gather.4

commit v4 on v3

--- a/solution.py
+++ b/solution.py
@@ -79,6 +79,9 @@
     vout = jnp.pad(vision_outproj.T, ((0, 0), (0, pad_to(half))))
     vout = jnp.broadcast_to(vout[None], (lines,) + vout.shape)
     line = jnp.concatenate([vin, vout], axis=2)
+    line, decoder_inproj, decoder_outproj = lax.optimization_barrier(
+        (line, decoder_inproj, decoder_outproj)
+    )
     line = lax.all_to_all(line, "zh", split_axis=0, concat_axis=0, tiled=True)
     split_out = vin.shape[2]
     split_merge = line.shape[2]
@@ -96,7 +99,7 @@
     dec = dec.reshape(8 * drows, half)
     patch_rows = patches.astype(F32)
     normed = layer_norm(patch_rows).astype(BF)
-    line_v, dec, normed = lax.optimization_barrier((line_v, dec, normed))
+    line_v, dec, normed, text = lax.optimization_barrier((line_v, dec, normed, text_embed))
     full_v = lax.all_gather(line_v, PLANE, axis=0, tiled=True)
     line_d = to_all(dec, "zh").reshape(lines, 4, 2 * drows, half).transpose(0, 2, 1, 3)
     line_d = line_d.reshape(lines * 2 * drows, 4 * half)
@@ -134,7 +137,7 @@
         ]
     )
     others = both_halves(moved[:, :side], first)
-    text, others, reorder = lax.optimization_barrier((text_embed, others, reorder))
+    others, reorder = lax.optimization_barrier((others, reorder))
     side_t = piece_rows // 2
     mine = jnp.where(first, text[:side_t], text[side_t:])
     earlier = jnp.stack(

time: 283 us -> 261 us (0.922)
  waiting for transfers between devices: 101 us -> 88.1 us
  starting transfers between devices: 77.2 us -> 70.8 us
    ppermute x3, waiting for transfers between devices: 11 us -> 0.01 us  [shards(): lax.ppermute(mine, TOK, [(i, i + s) for i in range(pieces - s)])]
    all_to_all x1, starting transfers between devices: 15.3 us -> 10.2 us  [shards(): lax.all_to_all(sent.reshape(pieces, slots, half + pad_to(half)), TOK, spl...]
    all_to_all x1, waiting for transfers between devices: 14.2 us -> 18.6 us  [shards(): lax.all_to_all(merged, 'zh', split_axis=0, concat_axis=0, tiled=True)]
    ppermute x5, starting transfers between devices: 11.4 us -> 15.7 us  [swap_sub(): return lax.ppermute(value, 'sub', [(0, 1), (1, 0)])]
    all_to_all x1, waiting for transfers between devices: 21.7 us -> 18 us  [shards(): lax.all_to_all(sent.reshape(pieces, slots, half + pad_to(half)), TOK, spl...]
    all_to_all x1, starting transfers between devices: 8.01 us -> 4.52 us  [shards(): lax.all_to_all(partial, 'zh', split_axis=0, concat_axis=0, tiled=True)]
  transfers between devices with their start and end apart: 19 -> 19, of which waited for: 13 -> 10; matrix products, arithmetic and copies ran while one was open for 17% -> 18% of each run, Pallas kernels for 0% -> 0%
where the time goes in v4:
time: 261 us; the launch traced here: 260 us
  waiting for transfers between devices  88.1 us (34%)
  starting transfers between devices  70.8 us (27%)
  matrix products  35.9 us (14%)
  other arithmetic  18.4 us (7%)
  local copies, waits for them, and re-layouts  17.5 us (7%)
  blocking collectives  15.1 us (6%)
  between operations  13.9 us (5%)
    ppermute x3, waiting for transfers between devices, shards(): lax.ppermute(mine, 'zh', [(i, (i + s) % lines) for i in range(lines)])  31.6 us
    dot_general x7, matrix products, dot(): return jnp.dot(a, b, preferred_element_type=F32)  23.9 us
    all_to_all x1, waiting for transfers between devices, shards(): lax.all_to_all(merged, 'zh', split_axis=0, concat_axis=0, tiled=True)  18.6 us
    all_to_all x1, waiting for transfers between devices, shards(): lax.all_to_all(sent.reshape(pieces, slots, half + pad_to(half)), TOK, spl...  18 us
    ppermute x3, starting transfers between devices, shards(): lax.ppermute(mine, TOK, [(i, i + s) for i in range(pieces - s)])  15.7 us
    ppermute x5, starting transfers between devices, swap_sub(): return lax.ppermute(value, 'sub', [(0, 1), (1, 0)])  15.7 us
    all_to_all x1, blocking collectives, shards(): heads = lax.all_to_all(heads, 'zh', split_axis=0, concat_axis=0, tiled=True)  15.1 us
    all_to_all x1, starting transfers between devices, shards(): lax.all_to_all(sent.reshape(pieces, slots, half + pad_to(half)), TOK, spl...  10.2 us
  transfers between devices with their start and end apart: 19, of which 10 were waited for; matrix products, arithmetic and copies ran while one was open for 18% of the time, Pallas kernels for 0%

profile of v4, /device:TPU:1, one launch (start us, length us, event | category | flops | bytes accessed | tf_op | source)
XLA Modules:
  0.0 259.7 jit_solution(10452889643673918663)
XLA Ops:
  11.2 2.6 collective-permute-start
  13.8 7.3 %all-to-all-start = ((bf16[4,22,1408]{2,1,0:T(8,128)(2,1)}), bf16[4,22,1408]{2,1,0:T(8,128)(2,1)S(1)}, u32[]{:S(2)}, u32[]{:S(2)}) async-start(bf16[4,22,1408]{2,1,0:T(8,128)(2,1)} %fusion.47), calls=%async_computation | async-start | bytes 540672 | tf_op jit(solution)/shard_map/all_to_all | solution.py:85
  22.3 6.9 %all-to-all-done = bf16[4,22,1408]{2,1,0:T(8,128)(2,1)S(1)} async-done(((bf16[4,22,1408]{2,1,0:T(8,128)(2,1)}), bf16[4,22,1408]{2,1,0:T(8,128)(2,1)S(1)}, u32[]{:S(2)}, u32[]{:S(2)}) %all-to-all-start) | async-done | bytes 247840 | tf_op jit(solution)/shard_map/all_to_all | solution.py:85
  31.2 4.2 %all-to-all-start.5 = ((bf16[4,88,704]{2,1,0:T(8,128)(2,1)}), bf16[4,88,704]{2,1,0:T(8,128)(2,1)S(1)}, u32[]{:S(2)}, u32[]{:S(2)}) async-start(bf16[4,88,704]{2,1,0:T(8,128)(2,1)} %broadcast_in_dim.27), calls=%async_computation.5 | async-start | bytes 1081344 | tf_op jit(solution)/shard_map/all_to_all | solution.py:51
  36.1 5.5 %collective-permute-start.5 = (bf16[64,1408]{1,0:T(8,128)(2,1)}, bf16[64,1408]{1,0:T(8,128)(2,1)S(1)}, u32[]{:S(2)}, u32[]{:S(2)}) collective-permute-start(bf16[64,1408]{1,0:T(8,128)(2,1)} %slice_select_fusion.1), channel_id=1, source_target_pairs={{0,6},{2,8},{4,10},{6,12},{8,14},{10,16},{12,18},{14,20},{16,22},{... | collective-permute-start | bytes 540680 | tf_op jit(solution)/shard_map/ppermute | solution.py:145
  41.6 5.6 %collective-permute-start.6 = (bf16[64,1408]{1,0:T(8,128)(2,1)}, bf16[64,1408]{1,0:T(8,128)(2,1)}, u32[]{:S(2)}, u32[]{:S(2)}) collective-permute-start(bf16[64,1408]{1,0:T(8,128)(2,1)} %slice_select_fusion.1), channel_id=1, source_target_pairs={{0,4},{2,6},{4,8},{6,10},{8,12},{10,14},{12,16},{14,18},{16,20},{1... | collective-permute-start | bytes 540680 | tf_op jit(solution)/shard_map/ppermute | solution.py:145
  47.2 4.6 %collective-permute-start.7 = (bf16[64,1408]{1,0:T(8,128)(2,1)}, bf16[64,1408]{1,0:T(8,128)(2,1)}, u32[]{:S(2)}, u32[]{:S(2)}) collective-permute-start(bf16[64,1408]{1,0:T(8,128)(2,1)} %slice_select_fusion.1), channel_id=1, source_target_pairs={{0,2},{2,4},{4,6},{6,8},{8,10},{10,12},{12,14},{14,16},{16,18},{18... | collective-permute-start | bytes 540680 | tf_op jit(solution)/shard_map/ppermute | solution.py:145
  52.9 3.0 %collective-permute-start.2 = (bf16[144,1408]{1,0:T(8,128)(2,1)}, bf16[144,1408]{1,0:T(8,128)(2,1)S(1)}, u32[]{:S(2)}, u32[]{:S(2)}) collective-permute-start(bf16[144,1408]{1,0:T(8,128)(2,1)} %fusion.41), channel_id=1, source_target_pairs={{0,4},{2,6},{4,0},{6,2},{1,5},{3,7},{5,1},{7,3},{8,12},{10,14},{12... | collective-permute-start | bytes 1216520 | tf_op jit(solution)/shard_map/ppermute | solution.py:135
  57.6 3.9 %collective-permute-start.3 = (bf16[144,1408]{1,0:T(8,128)(2,1)}, bf16[144,1408]{1,0:T(8,128)(2,1)S(1)}, u32[]{:S(2)}, u32[]{:S(2)}) collective-permute-start(bf16[144,1408]{1,0:T(8,128)(2,1)} %fusion.41), channel_id=1, source_target_pairs={{0,6},{2,0},{4,2},{6,4},{1,7},{3,1},{5,3},{7,5},{8,14},{10,8},{12,... | collective-permute-start | bytes 1216520 | tf_op jit(solution)/shard_map/ppermute | solution.py:135
  61.5 3.5 %fusion = bf16[1408,1408]{1,0:T(8,128)(2,1)} fusion(s32[1408]{0:T(1024)S(1)} %fusion.70), kind=kLoop, calls=%fused_computation.1 | loop fusion | flops 3964928 | bytes 3970560 | tf_op jit(solution)/shard_map/convert_element_type | solution.py:111
  66.1 2.5 collective-permute-start.8
  68.7 6.3 %collective-permute-done.1 = bf16[144,1408]{1,0:T(8,128)(2,1)S(1)} collective-permute-done((bf16[144,1408]{1,0:T(8,128)(2,1)}, bf16[144,1408]{1,0:T(8,128)(2,1)S(1)}, u32[]{:S(2)}, u32[]{:S(2)}) %collective-permute-start.1) | collective-permute-done | bytes 405536 | tf_op jit(solution)/shard_map/ppermute | solution.py:135
  75.0 22.3 %collective-permute-done.2 = bf16[144,1408]{1,0:T(8,128)(2,1)S(1)} collective-permute-done((bf16[144,1408]{1,0:T(8,128)(2,1)}, bf16[144,1408]{1,0:T(8,128)(2,1)S(1)}, u32[]{:S(2)}, u32[]{:S(2)}) %collective-permute-start.2) | collective-permute-done | bytes 405536 | tf_op jit(solution)/shard_map/ppermute | solution.py:135
  97.3 3.0 %collective-permute-done.3 = bf16[144,1408]{1,0:T(8,128)(2,1)S(1)} collective-permute-done((bf16[144,1408]{1,0:T(8,128)(2,1)}, bf16[144,1408]{1,0:T(8,128)(2,1)S(1)}, u32[]{:S(2)}, u32[]{:S(2)}) %collective-permute-start.3) | collective-permute-done | bytes 405536 | tf_op jit(solution)/shard_map/ppermute | solution.py:135
  100.6 4.2 %collective-permute-start.4 = (bf16[3,128,1408]{2,1,0:T(8,128)(2,1)S(1)}, bf16[3,128,1408]{2,1,0:T(8,128)(2,1)S(1)}, u32[]{:S(2)}, u32[]{:S(2)}) collective-permute-start(bf16[3,128,1408]{2,1,0:T(8,128)(2,1)S(1)} %slice.104), channel_id=1, source_target_pairs={{0,1},{1,0},{2,3},{3,2},{4,5},{5,4},{6,7},{7,6},{8,9},{9,8},{10,11... | collective-permute-start | bytes 3244040 | tf_op jit(solution)/shard_map/ppermute | solution.py:30
  109.7 5.3 %fusion.18 = bf16[1024,528]{0,1:T(8,128)(2,1)} fusion(bf16[1024,1408]{1,0:T(8,128)(2,1)} %bitcast.108, bf16[1408,2176]{1,0:T(8,128)(2,1)} %all-gather.3.cloned.1.call-done), kind=kOutput, calls=%fused_computation.33 | convolution fusion | flops 1523073024 | bytes 5767168 | tf_op jit(solution)/shard_map/dot_general | solution.py:34
  115.0 2.5 reshape.457
  119.3 15.1 %all_to_all.30 = bf16[4,256,176]{1,2,0:T(8,128)(2,1)S(1)} all-to-all(bf16[4,256,176]{1,2,0:T(8,128)(2,1)S(1)} %fusion.44), channel_id=1, replica_groups=mesh['grp'=2,'y'=4,'x'=4,'zh'=4,'sub'=2] {'zh'}, dimensions={0} | all-to-all | bytes 720896 | tf_op jit(solution)/shard_map/all_to_all | solution.py:170
  145.4 3.5 %all-to-all-start.2 = ((bf16[4,64,1408]{2,1,0:T(8,128)(2,1)}), bf16[4,64,1408]{2,1,0:T(8,128)(2,1)S(1)}, u32[]{:S(2)}, u32[]{:S(2)}) async-start(bf16[4,64,1408]{2,1,0:T(8,128)(2,1)} %reshape.462), calls=%async_computation.2 | async-start | bytes 1441792 | tf_op jit(solution)/shard_map/all_to_all | solution.py:179
  149.2 18.6 %all-to-all-done.2 = bf16[4,64,1408]{2,1,0:T(8,128)(2,1)S(1)} async-done(((bf16[4,64,1408]{2,1,0:T(8,128)(2,1)}), bf16[4,64,1408]{2,1,0:T(8,128)(2,1)S(1)}, u32[]{:S(2)}, u32[]{:S(2)}) %all-to-all-start.2) | async-done | bytes 720928 | tf_op jit(solution)/shard_map/all_to_all | solution.py:179
  167.8 2.6 fusion.29
  171.3 4.5 %all-to-all-start.3 = ((bf16[4,64,704]{2,1,0:T(8,128)(2,1)}), bf16[4,64,704]{2,1,0:T(8,128)(2,1)S(1)}, u32[]{:S(2)}, u32[]{:S(2)}) async-start(bf16[4,64,704]{2,1,0:T(8,128)(2,1)} %bitcast.28), calls=%async_computation.3 | async-start | bytes 786432 | tf_op jit(solution)/shard_map/all_to_all | solution.py:182
  176.0 8.8 %all-to-all-done.3 = bf16[4,64,704]{2,1,0:T(8,128)(2,1)S(1)} async-done(((bf16[4,64,704]{2,1,0:T(8,128)(2,1)}), bf16[4,64,704]{2,1,0:T(8,128)(2,1)S(1)}, u32[]{:S(2)}, u32[]{:S(2)}) %all-to-all-start.3) | async-done | bytes 360480 | tf_op jit(solution)/shard_map/all_to_all | solution.py:182
  186.3 10.2 %all-to-all-start.4 = ((bf16[64,8,768]{2,1,0:T(8,128)(2,1)}), bf16[64,8,768]{2,1,0:T(8,128)(2,1)S(1)}, u32[]{:S(2)}, u32[]{:S(2)}) async-start(bf16[64,8,768]{2,1,0:T(8,128)(2,1)} %fusion.28), calls=%async_computation.4 | async-start | bytes 1572864 | tf_op jit(solution)/shard_map/all_to_all | solution.py:188
  197.0 18.0 %all-to-all-done.4 = bf16[64,8,768]{2,1,0:T(8,128)(2,1)S(1)} async-done(((bf16[64,8,768]{2,1,0:T(8,128)(2,1)}), bf16[64,8,768]{2,1,0:T(8,128)(2,1)S(1)}, u32[]{:S(2)}, u32[]{:S(2)}) %all-to-all-start.4) | async-done | bytes 786464 | tf_op jit(solution)/shard_map/all_to_all | solution.py:188
  215.3 7.5 %collective-permute-start.10 = (bf16[512,704]{0,1:T(8,128)(2,1)S(1)}, bf16[512,704]{0,1:T(8,128)(2,1)S(1)}, u32[]{:S(2)}, u32[]{:S(2)}) collective-permute-start(bf16[512,704]{0,1:T(8,128)(2,1)S(1)} %copy.74), channel_id=1, source_target_pairs={{0,1},{1,0},{2,3},{3,2},{4,5},{5,4},{6,7},{7,6},{8,9},{9,8},{10,11... | collective-permute-start | bytes 2162696 | tf_op jit(solution)/shard_map/ppermute | solution.py:30
  224.9 2.7 %fusion.96 = (f32[512]{0:T(512)S(1)}, f32[512,1408]{1,0:T(8,128)S(1)}) fusion(bf16[512,1408]{1,0:T(8,128)(2,1)} %pad_maximum_fusion.2, bf16[512,704]{1,0:T(8,128)(2,1)S(1)} %get-tuple-element.42, bf16[512,704]{1,0:T(8,128)(2,1)S(1)} %get-tuple-element.41, s32[512]{0:T(512)S(1)} %add_select_fusion.6, pred[512]{0:T(512)(128)(4,1)S(1)} %fusion.35), kind=kOutput, calls=%fused_computation.200 | convolution fusion | flops 743505408 | bytes 5771776 | tf_op jit(solution)/shard_map/dot_general | solution.py:34
  228.1 2.7 %convolution_convert_fusion = bf16[512,1408]{1,0:T(8,128)(2,1)S(1)} fusion(bf16[1408,1408]{1,0:T(8,128)(2,1)S(1)} %copy-done.1, f32[512,1408]{1,0:T(8,128)S(1)} %get-tuple-element.53, f32[512]{0:T(512)S(1)} %add_rsqrt_fusion, f32[512]{0:T(512)S(1)} %broadcast_multiply_fusion), kind=kOutput, calls=%fused_computation.6 | convolution fusion | flops 2032926720 | bytes 8294400 | tf_op jit(solution)/shard_map/dot_general | solution.py:34
  232.0 6.6 %fusion.3 = bf16[512,1408]{1,0:T(8,128)(2,1)} fusion(bf16[512,1408]{1,0:T(8,128)(2,1)S(1)} %convolution_convert_fusion, bf16[1408,2816]{1,0:T(8,128)(2,1)} %all-gather.5.cloned.1.call-done), kind=kOutput, calls=%fused_computation.5 | convolution fusion | flops 2030764032 | bytes 6848512 | tf_op jit(solution)/shard_map/dot_general | solution.py:34
  240.3 2.7 %fusion.32 = bf16[128,704]{0,1:T(8,128)(2,1)S(1)} fusion(bf16[1408,2816]{1,0:T(8,128)(2,1)} %all-gather.5.cloned.1.call-done, bf16[512,1408]{1,0:T(8,128)(2,1)} %copy-done.8), kind=kOutput, calls=%fused_computation.49 | convolution fusion | flops 253845504 | bytes 2703360 | tf_op jit(solution)/shard_map/dot_general | solution.py:34
  244.4 2.8 %convolution_convert_fusion.2 = bf16[128,1408]{1,0:T(8,128)(2,1)S(1)} fusion(bf16[128,704]{0,1:T(8,128)(2,1)S(1)} %bitcast.128, bf16[1408,2816]{1,0:T(8,128)(2,1)} %all-gather.5.cloned.1.call-done), kind=kOutput, calls=%fused_computation.11 | convolution fusion | flops 253935616 | bytes 2703360 | tf_op jit(solution)/shard_map/dot_general | solution.py:223
  248.7 4.1 %convolution_convert_fusion.3 = bf16[64,1408]{1,0:T(8,128)(2,1)} fusion(bf16[1408,1408]{1,0:T(8,128)(2,1)} %fusion, bf16[64,1408]{1,0:T(8,128)(2,1)S(1)} %collective-permute-done.11, bf16[128,1408]{1,0:T(8,128)(2,1)S(1)} %convolution_convert_fusion.2, s32[]{:T(128)S(6)} %select_n.249), kind=kOutput, calls=%fused_computation.12 | convolution fusion | flops 254205952 | bytes 4505604 | tf_op jit(solution)/shard_map/dot_general | solution.py:231
  (129 shorter events, 42.1 us)
Async XLA Ops:
  6.5 14.5 %copy-start = (bf16[256,1408]{1,0:T(8,128)(2,1)S(1)}, bf16[256,1408]{1,0:T(8,128)(2,1)}, u32[]{:S(2)}) copy-start(bf16[256,1408]{1,0:T(8,128)(2,1)} %param.12) | copy-start | bytes 2162692
  8.7 13.2 %copy-start.3 = (bf16[11,1,3,704]{3,2,1,0:T(4,128)(2,1)S(1)}, bf16[11,1,3,704]{3,2,1,0:T(4,128)(2,1)}, u32[]{:S(2)}) copy-start(bf16[11,1,3,704]{3,2,1,0:T(4,128)(2,1)} %param.20) | copy-start | bytes 139396
  11.2 10.7 %collective-permute-start = (bf16[4,11,704]{2,0,1:T(4,128)(2,1)S(1)}, bf16[4,11,704]{2,0,1:T(4,128)(2,1)S(1)}, u32[]{:S(2)}, u32[]{:S(2)}) collective-permute-start(bf16[4,11,704]{2,0,1:T(4,128)(2,1)S(1)} %pad_maximum_fusion.7), channel_id=1, source_target_pairs={{0,128},{128,0},{1,129},{129,1},{2,130},{130,2},{3,131},{131,3},{4... | collective-permute-start | bytes 185864 | tf_op jit(solution)/shard_map/ppermute | solution.py:96
  13.8 15.5 %all-to-all-start = ((bf16[4,22,1408]{2,1,0:T(8,128)(2,1)}), bf16[4,22,1408]{2,1,0:T(8,128)(2,1)S(1)}, u32[]{:S(2)}, u32[]{:S(2)}) async-start(bf16[4,22,1408]{2,1,0:T(8,128)(2,1)} %fusion.47), calls=%async_computation | async-start | bytes 540672 | tf_op jit(solution)/shard_map/all_to_all | solution.py:85
  21.0 88.7 %all-gather.3.cloned.1.call-start = ((), (), s32[]{:S(2)}) async-start(), calls=%async_computation.6 | async-start | bytes 6510592 | tf_op jit(solution)/shard_map/all_gather | solution.py:103
  21.2 8.1 %copy-start.4 = (bf16[88,704]{1,0:T(8,128)(2,1)S(1)}, bf16[88,704]{1,0:T(8,128)(2,1)}, u32[]{:S(2)}) copy-start(bf16[88,704]{1,0:T(8,128)(2,1)} %param.16) | copy-start | bytes 371716
  21.6 8.6 %copy-start.5 = (s32[1,4]{1,0:T(1,128)S(1)}, s32[1,4]{1,0:T(1,128)}, u32[]{:S(2)}) copy-start(s32[1,4]{1,0:T(1,128)} %param.13) | copy-start | bytes 52
  22.2 13.2 %copy-start.2 = (bf16[128,1408]{1,0:T(8,128)(2,1)S(1)}, bf16[128,1408]{1,0:T(8,128)(2,1)}, u32[]{:S(2)}) copy-start(bf16[128,1408]{1,0:T(8,128)(2,1)} %param.17) | copy-start | bytes 1081348
  31.2 24.7 %all-to-all-start.5 = ((bf16[4,88,704]{2,1,0:T(8,128)(2,1)}), bf16[4,88,704]{2,1,0:T(8,128)(2,1)S(1)}, u32[]{:S(2)}, u32[]{:S(2)}) async-start(bf16[4,88,704]{2,1,0:T(8,128)(2,1)} %broadcast_in_dim.27), calls=%async_computation.5 | async-start | bytes 1081344 | tf_op jit(solution)/shard_map/all_to_all | solution.py:51
  35.4 195.4 %all-gather.5.cloned.1.call-start = ((), (), s32[]{:S(2)}) async-start(), calls=%async_computation.7 | async-start | bytes 8425472 | tf_op jit(solution)/shard_map/all_gather | solution.py:106
  36.1 21.4 %collective-permute-start.5 = (bf16[64,1408]{1,0:T(8,128)(2,1)}, bf16[64,1408]{1,0:T(8,128)(2,1)S(1)}, u32[]{:S(2)}, u32[]{:S(2)}) collective-permute-start(bf16[64,1408]{1,0:T(8,128)(2,1)} %slice_select_fusion.1), channel_id=1, source_target_pairs={{0,6},{2,8},{4,10},{6,12},{8,14},{10,16},{12,18},{14,20},{16,22},{... | collective-permute-start | bytes 540680 | tf_op jit(solution)/shard_map/ppermute | solution.py:145
  41.6 23.4 %collective-permute-start.6 = (bf16[64,1408]{1,0:T(8,128)(2,1)}, bf16[64,1408]{1,0:T(8,128)(2,1)}, u32[]{:S(2)}, u32[]{:S(2)}) collective-permute-start(bf16[64,1408]{1,0:T(8,128)(2,1)} %slice_select_fusion.1), channel_id=1, source_target_pairs={{0,4},{2,6},{4,8},{6,10},{8,12},{10,14},{12,16},{14,18},{16,20},{1... | collective-permute-start | bytes 540680 | tf_op jit(solution)/shard_map/ppermute | solution.py:145
  47.2 17.8 %collective-permute-start.7 = (bf16[64,1408]{1,0:T(8,128)(2,1)}, bf16[64,1408]{1,0:T(8,128)(2,1)}, u32[]{:S(2)}, u32[]{:S(2)}) collective-permute-start(bf16[64,1408]{1,0:T(8,128)(2,1)} %slice_select_fusion.1), channel_id=1, source_target_pairs={{0,2},{2,4},{4,6},{6,8},{8,10},{10,12},{12,14},{14,16},{16,18},{18... | collective-permute-start | bytes 540680 | tf_op jit(solution)/shard_map/ppermute | solution.py:145
  52.7 22.3 %collective-permute-start.1 = (bf16[144,1408]{1,0:T(8,128)(2,1)}, bf16[144,1408]{1,0:T(8,128)(2,1)S(1)}, u32[]{:S(2)}, u32[]{:S(2)}) collective-permute-start(bf16[144,1408]{1,0:T(8,128)(2,1)} %fusion.41), channel_id=1, source_target_pairs={{0,2},{2,4},{4,6},{6,0},{1,3},{3,5},{5,7},{7,1},{8,10},{10,12},{12... | collective-permute-start | bytes 1216520 | tf_op jit(solution)/shard_map/ppermute | solution.py:135
  52.9 44.4 %collective-permute-start.2 = (bf16[144,1408]{1,0:T(8,128)(2,1)}, bf16[144,1408]{1,0:T(8,128)(2,1)S(1)}, u32[]{:S(2)}, u32[]{:S(2)}) collective-permute-start(bf16[144,1408]{1,0:T(8,128)(2,1)} %fusion.41), channel_id=1, source_target_pairs={{0,4},{2,6},{4,0},{6,2},{1,5},{3,7},{5,1},{7,3},{8,12},{10,14},{12... | collective-permute-start | bytes 1216520 | tf_op jit(solution)/shard_map/ppermute | solution.py:135
  57.6 42.8 %collective-permute-start.3 = (bf16[144,1408]{1,0:T(8,128)(2,1)}, bf16[144,1408]{1,0:T(8,128)(2,1)S(1)}, u32[]{:S(2)}, u32[]{:S(2)}) collective-permute-start(bf16[144,1408]{1,0:T(8,128)(2,1)} %fusion.41), channel_id=1, source_target_pairs={{0,6},{2,0},{4,2},{6,4},{1,7},{3,1},{5,3},{7,5},{8,14},{10,8},{12,... | collective-permute-start | bytes 1216520 | tf_op jit(solution)/shard_map/ppermute | solution.py:135
  66.1 38.9 %collective-permute-start.8 = (bf16[3,64,1408]{2,1,0:T(8,128)(2,1)S(1)}, bf16[3,64,1408]{2,1,0:T(8,128)(2,1)S(1)}, u32[]{:S(2)}, u32[]{:S(2)}) collective-permute-start(bf16[3,64,1408]{2,1,0:T(8,128)(2,1)S(1)} %pad_maximum_fusion.5), channel_id=1, source_target_pairs={{0,1},{1,0},{2,3},{3,2},{4,5},{5,4},{6,7},{7,6},{8,9},{9,8},{10,11... | collective-permute-start | bytes 1622024 | tf_op jit(solution)/shard_map/ppermute | solution.py:30
  100.6 7.0 %collective-permute-start.4 = (bf16[3,128,1408]{2,1,0:T(8,128)(2,1)S(1)}, bf16[3,128,1408]{2,1,0:T(8,128)(2,1)S(1)}, u32[]{:S(2)}, u32[]{:S(2)}) collective-permute-start(bf16[3,128,1408]{2,1,0:T(8,128)(2,1)S(1)} %slice.104), channel_id=1, source_target_pairs={{0,1},{1,0},{2,3},{3,2},{4,5},{5,4},{6,7},{7,6},{8,9},{9,8},{10,11... | collective-permute-start | bytes 3244040 | tf_op jit(solution)/shard_map/ppermute | solution.py:30
  136.8 2.9 %collective-permute-start.9 = (bf16[256,1408]{1,0:T(8,128)(2,1)S(1)}, bf16[256,1408]{1,0:T(8,128)(2,1)S(1)}, u32[]{:S(2)}, u32[]{:S(2)}) collective-permute-start(bf16[256,1408]{1,0:T(8,128)(2,1)S(1)} %convolution_convert_fusion.1), channel_id=1, source_target_pairs={{0,1},{1,0},{2,3},{3,2},{4,5},{5,4},{6,7},{7,6},{8,9},{9,8},{10,11... | collective-permute-start | bytes 2162696 | tf_op jit(solution)/shard_map/ppermute | solution.py:30
  143.1 5.8 %copy-start.6 = (s32[1,64]{1,0:T(1,128)S(1)}, s32[1,64]{1,0:T(1,128)}, u32[]{:S(2)}) copy-start(s32[1,64]{1,0:T(1,128)} %param.18) | copy-start | bytes 772
  145.4 22.4 %all-to-all-start.2 = ((bf16[4,64,1408]{2,1,0:T(8,128)(2,1)}), bf16[4,64,1408]{2,1,0:T(8,128)(2,1)S(1)}, u32[]{:S(2)}, u32[]{:S(2)}) async-start(bf16[4,64,1408]{2,1,0:T(8,128)(2,1)} %reshape.462), calls=%async_computation.2 | async-start | bytes 1441792 | tf_op jit(solution)/shard_map/all_to_all | solution.py:179
  171.3 25.3 %copy-start.7 = (s32[1,2]{1,0:T(1,128)S(1)}, s32[1,2]{1,0:T(1,128)}, u32[]{:S(2)}) copy-start(s32[1,2]{1,0:T(1,128)} %param.19) | copy-start | bytes 28
  171.3 13.6 %all-to-all-start.3 = ((bf16[4,64,704]{2,1,0:T(8,128)(2,1)}), bf16[4,64,704]{2,1,0:T(8,128)(2,1)S(1)}, u32[]{:S(2)}, u32[]{:S(2)}) async-start(bf16[4,64,704]{2,1,0:T(8,128)(2,1)} %bitcast.28), calls=%async_computation.3 | async-start | bytes 786432 | tf_op jit(solution)/shard_map/all_to_all | solution.py:182
  186.3 28.7 %all-to-all-start.4 = ((bf16[64,8,768]{2,1,0:T(8,128)(2,1)}), bf16[64,8,768]{2,1,0:T(8,128)(2,1)S(1)}, u32[]{:S(2)}, u32[]{:S(2)}) async-start(bf16[64,8,768]{2,1,0:T(8,128)(2,1)} %fusion.28), calls=%async_computation.4 | async-start | bytes 1572864 | tf_op jit(solution)/shard_map/all_to_all | solution.py:188
  215.3 9.3 %collective-permute-start.10 = (bf16[512,704]{0,1:T(8,128)(2,1)S(1)}, bf16[512,704]{0,1:T(8,128)(2,1)S(1)}, u32[]{:S(2)}, u32[]{:S(2)}) collective-permute-start(bf16[512,704]{0,1:T(8,128)(2,1)S(1)} %copy.74), channel_id=1, source_target_pairs={{0,1},{1,0},{2,3},{3,2},{4,5},{5,4},{6,7},{7,6},{8,9},{9,8},{10,11... | collective-permute-start | bytes 2162696 | tf_op jit(solution)/shard_map/ppermute | solution.py:30
  224.9 3.2 %copy-start.1 = (bf16[1408,1408]{1,0:T(8,128)(2,1)S(1)}, bf16[1408,1408]{1,0:T(8,128)(2,1)}, u32[]{:S(2)}) copy-start(bf16[1408,1408]{1,0:T(8,128)(2,1)} %fusion) | copy-start | bytes 11894788
  230.8 1.2 copy-start.8
  247.2 1.5 collective-permute-start.11
Sparse Core Ops, SparseCore 0:
  30.2 68.8 all-gather.2
  101.6 73.6 all-gather.4

commit v5 on v3

v5 whole, which is shorter than its diff:
```python
import functools
import math

import jax
import jax.numpy as jnp
from jax import lax
from jax.experimental import pallas as pl
from jax.experimental.pallas import tpu as pltpu
from jax.sharding import Mesh
from jax.sharding import PartitionSpec as P

HD = 88
REACH = 3
EPS = 1e-06
TOK = ("y", "x", "zh")
PLANE = ("y", "x")
BF = jnp.bfloat16
F32 = jnp.float32


def layer_norm(values):
    center = values - jnp.mean(values, axis=-1, keepdims=True)
    spread = jnp.mean(center * center, axis=-1, keepdims=True)
    return center * lax.rsqrt(spread + EPS)


def softmax_weights(scores, allowed):
    raw = jnp.exp(scores * (1.0 / math.sqrt(HD))) * allowed
    return (raw / jnp.sum(raw, axis=-1, keepdims=True)).astype(BF)


def swap_sub(value):
    return lax.ppermute(value, "sub", [(0, 1), (1, 0)])


def dot(a, b):
    return jnp.dot(a, b, preferred_element_type=F32)


def both_halves(part, first):
    return join_halves(part, swap_sub(part), first)


def join_halves(part, other, first):
    return jnp.concatenate(
        [jnp.where(first, part, other), jnp.where(first, other, part)], axis=1
    )


def pad_to(columns):
    return -columns % 128


def to_all(value, axes):
    count = lax.axis_size(axes)
    spread = jnp.broadcast_to(value[None], (count,) + value.shape)
    return lax.all_to_all(spread, axes, split_axis=0, concat_axis=0, tiled=True)


def contract_last(a, b):
    return lax.dot_general(a, b, (((1,), (1,)), ((), ())), preferred_element_type=F32)


def contract_first(a, b):
    return lax.dot_general(a, b, (((0,), (0,)), ((), ())), preferred_element_type=F32)


def decoder_block(
    half, cap, info, got, other, text, reorder, weights_hbm, out, weights, heads, sem
):
    load = pltpu.make_async_copy(weights_hbm, weights, sem)
    load.start()
    sub = info[0]
    piece = info[1]
    rows = text.shape[0]
    block = rows // (REACH + 1)
    tokens = got.shape[0]

    note = got[:, half - half % 128 :].astype(F32)
    spare = half % 128
    row = note[:, spare : spare + 1].astype(jnp.int32)
    flag = note[:, spare + 1 : spare + 2]
    index = lax.broadcasted_iota(jnp.int32, (tokens, 1), 0)
    back = lax.rem(lax.div(index, cap), REACH + 1)
    target = jnp.where(flag > 0.5, (REACH - back) * block + row, rows)
    place = lax.broadcasted_iota(jnp.int32, (tokens, rows), 1) == target
    place = jnp.where(place, 1.0, 0.0).astype(BF)
    mine = reorder[pl.ds(pl.multiple_of(sub * half, 16), half), :]
    theirs = reorder[pl.ds(pl.multiple_of((1 - sub) * half, 16), half), :]
    image = dot(got[:, :half], mine) + dot(other[:, :half], theirs)
    placed = contract_first(place, image.astype(BF))
    filled = contract_first(place, jnp.ones((tokens, 128), BF))
    values = jnp.where(filled[:, :1] > 0.5, placed, text[...].astype(F32))
    normed = layer_norm(values).astype(BF)

    load.wait()
    query_pos = piece * block + lax.broadcasted_iota(jnp.int32, (block, 1), 0)
    key_pos = (piece - REACH) * block + lax.broadcasted_iota(jnp.int32, (1, rows), 1)
    start = jnp.zeros((block, 1), jnp.int32)
    for prompt in range(2, info.shape[0]):
        start = jnp.where(query_pos >= info[prompt], jnp.maximum(start, info[prompt]), start)
    allowed = jnp.where((key_pos <= query_pos) & (key_pos >= start), 1.0, 0.0)
    partial = attention(half, normed[REACH * block :], normed, weights, heads, allowed, None)
    out[...] = contract_last(partial, reorder[...]).astype(BF)


def attention(half, asking, asked, weights, heads, allowed, late):
    spare = half % 128
    span = half + spare
    query = dot(asking, weights[:, :span])
    key = dot(asked, weights[:, half - spare : 2 * half])
    if late is not None:
        late.wait()
    value = dot(asked, weights[:, 2 * half : 2 * half + span])
    heads[:, :spare] = jnp.zeros((asking.shape[0], spare), F32)
    for head in range(half // HD):
        at = head * HD
        score = contract_last(
            query[:, at : at + HD].astype(BF), key[:, spare + at : spare + at + HD].astype(BF)
        )
        raw = jnp.exp(score * (1.0 / math.sqrt(HD))) * allowed
        share = (raw * (1.0 / jnp.sum(raw, axis=1, keepdims=True))).astype(BF)
        heads[:, spare + at : spare + at + HD] = dot(share, value[:, at : at + HD].astype(BF))
    return contract_last(heads[...].astype(BF), weights[:, 3 * half - spare : 4 * half]).astype(BF)


def vision_block(half, ends, normed, weights_hbm, out, weights, heads, sems):
    early = pltpu.make_async_copy(
        weights_hbm.at[:, : 2 * half], weights.at[:, : 2 * half], sems.at[0]
    )
    late = pltpu.make_async_copy(
        weights_hbm.at[:, 2 * half : 4 * half], weights.at[:, 2 * half :], sems.at[1]
    )
    early.start()
    late.start()
    rows = normed.shape[0]

    def image_of(row):
        token = lax.shift_right_logical(row, 2)
        image = jnp.zeros(row.shape, jnp.int32)
        for step in range(ends.shape[0]):
            image = image + jnp.where(token >= ends[step], 1, 0)
        return image

    own = image_of(lax.broadcasted_iota(jnp.int32, (rows, 1), 0))
    seen = image_of(lax.broadcasted_iota(jnp.int32, (1, rows), 1))
    allowed = jnp.where(own == seen, 1.0, 0.0)
    patches = normed[...]
    early.wait()
    out[...] = attention(half, patches, patches, weights, heads, allowed, late)


def run_vision_block(half, ends, normed, weights):
    rows, width = normed.shape
    vmem = pl.BlockSpec(memory_space=pltpu.VMEM)
    return pl.pallas_call(
        functools.partial(vision_block, half),
        out_shape=jax.ShapeDtypeStruct((rows, width), BF),
        in_specs=[
            pl.BlockSpec(memory_space=pltpu.SMEM),
            vmem,
            pl.BlockSpec(memory_space=pl.ANY),
        ],
        out_specs=vmem,
        scratch_shapes=[
            pltpu.VMEM((width, 4 * half), BF),
            pltpu.VMEM((rows, half + half % 128), F32),
            pltpu.SemaphoreType.DMA((2,)),
        ],
        compiler_params=pltpu.CompilerParams(vmem_limit_bytes=56 << 20),
    )(ends, normed, weights)


def run_decoder_block(half, cap, info, got, other, text, reorder, weights):
    rows, width = text.shape
    block = rows // (REACH + 1)
    vmem = pl.BlockSpec(memory_space=pltpu.VMEM)
    return pl.pallas_call(
        functools.partial(decoder_block, half, cap),
        out_shape=jax.ShapeDtypeStruct((block, width), BF),
        in_specs=[pl.BlockSpec(memory_space=pltpu.SMEM)]
        + [vmem] * 4
        + [pl.BlockSpec(memory_space=pl.ANY)],
        out_specs=vmem,
        scratch_shapes=[
            pltpu.VMEM(weights.shape, BF),
            pltpu.VMEM((block, half + half % 128), F32),
            pltpu.SemaphoreType.DMA,
        ],
        compiler_params=pltpu.CompilerParams(vmem_limit_bytes=56 << 20),
    )(info, got, other, text, reorder, weights)


def shards(
    patches,
    image_sizes,
    vision_inproj,
    vision_outproj,
    merger_weight,
    text_embed,
    image_positions,
    prompt_lengths,
    decoder_inproj,
    decoder_outproj,
):
    lines = lax.axis_size("zh")
    planes = lax.axis_size(PLANE)
    pieces = lax.axis_size(TOK)
    rows_v, width = patches.shape
    half = vision_inproj.shape[3]
    krows = vision_inproj.shape[0]
    mrows = merger_weight.shape[0]

    line = jnp.concatenate(
        [vision_inproj.reshape(krows, 3 * half), vision_outproj.T], axis=1
    )
    line = to_all(line, "zh").reshape(lines * krows, 4 * half)
    merge = jnp.pad(merger_weight, ((0, 0), (0, pad_to(half))))
    line_v = jnp.concatenate([line, merge], axis=1)

    drows = decoder_inproj.shape[0]
    dec = decoder_inproj.reshape(drows, 3 * half)
    dec = jnp.stack(
        [
            dec[:, : 2 * half],
            jnp.concatenate([dec[:, 2 * half :], decoder_outproj.T], axis=1),
        ]
    )
    dec_other = lax.ppermute(dec, "grp", [(0, 1), (1, 0)])
    low = lax.axis_index("grp") == 0
    dec = jnp.stack([jnp.where(low, dec, dec_other), jnp.where(low, dec_other, dec)], axis=1)
    dec = dec.reshape(4 * drows, width)
    patch_rows = patches.astype(F32)
    normed = layer_norm(patch_rows).astype(BF)
    me = lax.axis_index("zh")
    order = jnp.arange(width, dtype=jnp.int32)
    fan = 2 * drows
    natural = (
        order // drows % 2 * (width // 2)
        + order // (lines * fan) * (lines * drows)
        + (me - order // fan) % lines * drows
        + order % drows
    )
    reorder = (natural[None, :] == order[:, None]).astype(BF)
    first = lax.axis_index("sub") == 0
    side_t = text_embed.shape[0] // 2
    mine = jnp.concatenate(
        [
            jnp.where(first, text_embed[:side_t], text_embed[side_t:]),
            dec,
            jnp.zeros((-4 * drows % 16, width), BF),
        ],
        axis=0,
    )
    line_v, normed, reorder, mine = lax.optimization_barrier((line_v, normed, reorder, mine))
    full_v = lax.all_gather(line_v, PLANE, axis=0, tiled=True)

    piece_rows = text_embed.shape[0]
    reach = REACH + 1
    cap = rows_v // (2 * pieces)
    slots = reach * cap
    targets = image_positions[0]
    target_piece = targets // piece_rows
    target_row = targets % piece_rows
    hits = (target_piece[:, None] == jnp.arange(pieces, dtype=jnp.int32)[None, :]).astype(jnp.int32)
    slot = jnp.sum((jnp.cumsum(hits, axis=0) - hits) * hits, axis=1)
    dest = jnp.arange(pieces * slots, dtype=jnp.int32)
    back = dest // cap % reach
    wanted = (dest // slots)[:, None] - back[:, None] == target_piece[None, :]
    wanted = wanted & ((dest % cap)[:, None] == slot[None, :])
    window_rows = reach * piece_rows

    moved = [
        lax.ppermute(mine, "zh", [(i, (i + s) % lines) for i in range(lines)])
        for s in range(1, lines)
    ]
    line_d = jnp.stack([m[side_t : side_t + 4 * drows] for m in [mine] + moved])
    line_d = jnp.concatenate([line_d[:, : 2 * drows], line_d[:, 2 * drows :]], axis=2)
    full_d = lax.all_gather(
        line_d.reshape(lines * 2 * drows, 4 * half), PLANE, axis=0, tiled=True
    )

    text = jnp.stack([m[:side_t] for m in moved[::-1]])
    before = lax.ppermute(text, PLANE, [(i, i + 1) for i in range(planes - 1)])
    steps = jnp.arange(REACH, 0, -1, dtype=jnp.int32)[:, None, None]
    text = both_halves(jnp.where(steps <= me, text, before), first)
    window_text = jnp.concatenate([text.reshape(REACH * piece_rows, width), text_embed], axis=0)
    window_text = dot(window_text, reorder).astype(BF)

    ends = jnp.cumsum(image_sizes[0])
    partial = run_vision_block(half, ends, normed, full_v)
    hidden = patch_rows + (partial.astype(F32) + swap_sub(partial).astype(F32))
    tokens = rows_v // 4
    merged = layer_norm(hidden).astype(BF).reshape(tokens, planes, lines, mrows)
    merged = merged.transpose(2, 0, 1, 3).reshape(lines, tokens, planes * mrows)
    merged = lax.all_to_all(merged, "zh", split_axis=0, concat_axis=0, tiled=True)
    partial = dot(merged.reshape(lines * tokens, planes * mrows), full_v[:, 4 * half : 5 * half])
    partial = partial.astype(BF).reshape(lines, tokens, half)
    partial = lax.all_to_all(partial, "zh", split_axis=0, concat_axis=0, tiled=True)
    embedded = jnp.sum(partial.astype(F32), axis=0).astype(BF)

    note = jnp.stack([target_row, jnp.ones_like(target_row)], axis=1).astype(BF)
    note = jnp.pad(note, ((0, 0), (0, pad_to(half) - 2)))
    sent = dot(wanted.astype(BF), jnp.concatenate([embedded, note], axis=1)).astype(BF)
    got = lax.all_to_all(
        sent.reshape(pieces, slots, half + pad_to(half)), TOK, split_axis=0, concat_axis=0, tiled=True
    ).reshape(pieces * slots, half + pad_to(half))
    got, window_text = lax.optimization_barrier((got, window_text))
    lengths = prompt_lengths[0]
    starts = jnp.cumsum(lengths) - lengths
    info = jnp.concatenate(
        [jnp.stack([lax.axis_index("sub"), lax.axis_index(TOK)]).astype(jnp.int32), starts]
    )
    partial = run_decoder_block(
        half, cap, info, got, swap_sub(got), window_text, reorder, full_d
    )
    sub = lax.axis_index("sub")
    keep_rows = piece_rows // 2
    give = lax.dynamic_slice_in_dim(partial, (1 - sub) * keep_rows, keep_rows, 0)
    keep = lax.dynamic_slice_in_dim(partial, sub * keep_rows, keep_rows, 0)
    return (keep.astype(F32) + swap_sub(give).astype(F32)).astype(BF)


def solution(mesh):
    grp, tok, sub = mesh.devices.shape
    lined = Mesh(mesh.devices.reshape(grp, 4, 4, tok // 16, sub), ("grp", "y", "x", "zh", "sub"))
    whole = ("grp",) + TOK
    placed = (
        P(whole, None),
        P(whole, None),
        P(TOK, "sub", None, None),
        P("sub", TOK),
        P(TOK, "sub"),
        P(whole, None),
        P("grp", TOK),
        P("grp", None),
        P(whole, "sub", None, None),
        P("sub", whole),
    )
    return jax.shard_map(
        shards,
        mesh=lined,
        in_specs=placed,
        out_specs=P(whole + ("sub",), None),
        check_vma=False,
    )
```

time: 283 us -> 251 us (0.89)
  matrix products: 36.1 us -> 7.84 us
  starting transfers between devices: 77.2 us -> 49.2 us
  Pallas kernels: 0 us -> 25.3 us
  waiting for transfers between devices: 101 us -> 126 us
  blocking collectives: 16.8 us -> 0 us
  local copies, waits for them, and re-layouts: 19.4 us -> 13.8 us
  other arithmetic: 17.7 us -> 14.1 us
    all_gather x1, waiting for transfers between devices: 0.01 us -> 49.5 us  [shards(): full_v = lax.all_gather(line_v, PLANE, axis=0, tiled=True)]
    pallas_call x0 -> x2, Pallas kernels: none -> 25.3 us  [the longest x1 15.9 us: run_decoder_block(): pl.pallas_call(functools.partial(decoder_block, half, cap), out_shape=jax...]
    all_to_all x1 -> x0, blocking collectives: 16.8 us -> none  [shards(): heads = lax.all_to_all(heads, 'zh', split_axis=0, concat_axis=0, tiled=True)]
    dot_general x7 -> x3, matrix products: 24 us -> 7.84 us  [dot(): return jnp.dot(a, b, preferred_element_type=F32)]
    ppermute x3 -> x1, starting transfers between devices: 15.9 us -> 3.14 us  [shards(): before = lax.ppermute(text, PLANE, [(i, i + 1) for i in range(planes - 1)])]
    dot_general x7 -> x0, matrix products: 12.1 us -> none  [the longest x1 4.08 us: shards(): lax.dot_general(total, reorder, (((1,), (1,)), ((), ())), preferred_eleme...]
    ppermute x3 -> x1, waiting for transfers between devices: 11 us -> 0.01 us  [shards(): before = lax.ppermute(text, PLANE, [(i, i + 1) for i in range(planes - 1)])]
    ppermute x3, waiting for transfers between devices: 34.4 us -> 25.6 us  [shards(): lax.ppermute(mine, 'zh', [(i, (i + s) % lines) for i in range(lines)])]
  transfers between devices with their start and end apart: 19 -> 15, of which waited for: 13 -> 9; matrix products, arithmetic and copies ran while one was open for 17% -> 10% of each run, Pallas kernels for 0% -> 4%
where the time goes in v5:
time: 251 us; the launch traced here: 250 us
  waiting for transfers between devices  126 us (50%)
  starting transfers between devices  49.2 us (20%)
  Pallas kernels  25.3 us (10%)
  other arithmetic  14.1 us (6%)
  local copies, waits for them, and re-layouts  13.8 us (5%)
  between operations  13.8 us (5%)
  matrix products  7.84 us (3%)
    all_gather x1, waiting for transfers between devices, shards(): full_v = lax.all_gather(line_v, PLANE, axis=0, tiled=True)  49.5 us
    ppermute x3, waiting for transfers between devices, shards(): lax.ppermute(mine, 'zh', [(i, (i + s) % lines) for i in range(lines)])  25.6 us
    pallas_call x1, Pallas kernels, run_decoder_block(): pl.pallas_call(functools.partial(decoder_block, half, cap), out_shape=jax...  15.9 us
    all_to_all x1, waiting for transfers between devices, shards(): lax.all_to_all(merged, 'zh', split_axis=0, concat_axis=0, tiled=True)  15.5 us
    all_to_all x1, waiting for transfers between devices, shards(): lax.all_to_all(sent.reshape(pieces, slots, half + pad_to(half)), TOK, spl...  14.7 us
    all_to_all x1, starting transfers between devices, shards(): lax.all_to_all(sent.reshape(pieces, slots, half + pad_to(half)), TOK, spl...  9.9 us
    pallas_call x1, Pallas kernels, run_vision_block(): pl.pallas_call(functools.partial(vision_block, half), out_shape=jax.Shape...  9.39 us
    all_to_all x1, starting transfers between devices, to_all(): return lax.all_to_all(spread, axes, split_axis=0, concat_axis=0, tiled=True)  9.01 us
  transfers between devices with their start and end apart: 15, of which 9 were waited for; matrix products, arithmetic and copies ran while one was open for 10% of the time, Pallas kernels for 4%

profile of v5, /device:TPU:1, one launch (start us, length us, event | category | flops | bytes accessed | tf_op | source)
XLA Modules:
  0.0 250.1 jit_solution(3989956883718091892)
XLA Ops:
  6.5 1.0 copy.12
  9.4 9.0 %all-to-all-start = ((bf16[4,22,2816]{2,1,0:T(8,128)(2,1)}), bf16[4,22,2816]{2,1,0:T(8,128)(2,1)S(1)}, u32[]{:S(2)}, u32[]{:S(2)}) async-start(bf16[4,22,2816]{2,1,0:T(8,128)(2,1)} %broadcast_in_dim.9), calls=%async_computation | async-start | bytes 1081344 | tf_op jit(solution)/shard_map/all_to_all | solution.py:57
  20.0 1.2 fusion.6.normed
  21.3 3.6 %fusion.reorder = bf16[1408,1408]{1,0:T(8,128)(2,1)} fusion(s32[1408]{0:T(1024)S(1)} %fusion.39), kind=kLoop, calls=%fused_computation.1 | loop fusion | flops 3964928 | bytes 3970560 | tf_op jit(solution)/shard_map/convert_element_type | solution.py:244
  25.0 7.9 %collective-permute-done = bf16[2,11,1408]{2,1,0:T(8,128)(2,1)S(1)} collective-permute-done((bf16[2,11,1408]{2,1,0:T(8,128)(2,1)S(1)}, bf16[2,11,1408]{2,1,0:T(8,128)(2,1)S(1)}, u32[]{:S(2)}, u32[]{:S(2)}) %collective-permute-start) | collective-permute-done | bytes 61984 | tf_op jit(solution)/shard_map/ppermute | solution.py:229
  35.1 4.3 %collective-permute-start.3 = (bf16[112,1408]{1,0:T(8,128)(2,1)S(1)}, bf16[112,1408]{1,0:T(8,128)(2,1)S(1)}, u32[]{:S(2)}, u32[]{:S(2)}) collective-permute-start(bf16[112,1408]{1,0:T(8,128)(2,1)S(1)} %maximum_maximum_fusion), channel_id=1, source_target_pairs={{0,4},{2,6},{4,0},{6,2},{1,5},{3,7},{5,1},{7,3},{8,12},{10,14},{12... | collective-permute-start | bytes 946184 | tf_op jit(solution)/shard_map/ppermute | solution.py:274
  39.4 3.3 %collective-permute-start.2 = (bf16[112,1408]{1,0:T(8,128)(2,1)S(1)}, bf16[112,1408]{1,0:T(8,128)(2,1)S(1)}, u32[]{:S(2)}, u32[]{:S(2)}) collective-permute-start(bf16[112,1408]{1,0:T(8,128)(2,1)S(1)} %maximum_maximum_fusion), channel_id=1, source_target_pairs={{0,6},{2,0},{4,2},{6,4},{1,7},{3,1},{5,3},{7,5},{8,14},{10,8},{12,... | collective-permute-start | bytes 946184 | tf_op jit(solution)/shard_map/ppermute | solution.py:274
  42.7 25.6 %collective-permute-done.2 = bf16[112,1408]{1,0:T(8,128)(2,1)S(1)} collective-permute-done((bf16[112,1408]{1,0:T(8,128)(2,1)S(1)}, bf16[112,1408]{1,0:T(8,128)(2,1)S(1)}, u32[]{:S(2)}, u32[]{:S(2)}) %collective-permute-start.2) | collective-permute-done | bytes 315424 | tf_op jit(solution)/shard_map/ppermute | solution.py:274
  71.0 49.5 %all-gather.3.cloned.1.call-done.weights_hbm = bf16[1408,3584]{1,0:T(8,128)(2,1)} async-done(((bf16[88,3584]{1,0:T(8,128)(2,1)}), bf16[1408,3584]{1,0:T(8,128)(2,1)}) %all-gather.3.cloned.1.call-update) | async-done | bytes 10092560 | tf_op jit(solution)/shard_map/all_gather | solution.py:256
  120.5 9.4 %shard_map.100 = bf16[256,1408]{1,0:T(8,128)(2,1)} custom-call(s32[4]{0:T(128)} %bitcast.67, bf16[256,1408]{1,0:T(8,128)(2,1)} %fusion.6.normed, bf16[1408,3584]{1,0:T(8,128)(2,1)} %all-gather.3.cloned.1.call-done.weights_hbm), custom_call_target="tpu_custom_call" | custom-call | tf_op jit(solution)/shard_map/pallas_call | solution.py:156
  129.9 0.9 collective-permute-start.1
  130.9 1.9 collective-permute-done.1
  132.9 1.5 fusion.16
  135.2 2.0 reshape.316
  137.4 2.3 reshape.317
  139.7 6.7 %all-to-all-start.1 = ((bf16[4,64,1408]{2,1,0:T(8,128)(2,1)}), bf16[4,64,1408]{2,1,0:T(8,128)(2,1)S(1)}, u32[]{:S(2)}, u32[]{:S(2)}) async-start(bf16[4,64,1408]{2,1,0:T(8,128)(2,1)} %reshape.317), calls=%async_computation.1 | async-start | bytes 1441792 | tf_op jit(solution)/shard_map/all_to_all | solution.py:296
  146.5 3.1 %collective-permute-start.5 = (bf16[3,64,1408]{2,1,0:T(8,128)(2,1)S(1)}, bf16[3,64,1408]{2,1,0:T(8,128)(2,1)S(1)}, u32[]{:S(2)}, u32[]{:S(2)}) collective-permute-start(bf16[3,64,1408]{2,1,0:T(8,128)(2,1)S(1)} %pad_maximum_fusion.1), channel_id=1, source_target_pairs={{0,8},{8,16},{16,24},{24,32},{32,40},{40,48},{48,56},{56,64},{64,7... | collective-permute-start | bytes 1622024 | tf_op jit(solution)/shard_map/ppermute | solution.py:284
  150.1 15.5 %all-to-all-done.1 = bf16[4,64,1408]{2,1,0:T(8,128)(2,1)S(1)} async-done(((bf16[4,64,1408]{2,1,0:T(8,128)(2,1)}), bf16[4,64,1408]{2,1,0:T(8,128)(2,1)S(1)}, u32[]{:S(2)}, u32[]{:S(2)}) %all-to-all-start.1) | async-done | bytes 720928 | tf_op jit(solution)/shard_map/all_to_all | solution.py:296
  165.5 2.6 %fusion.12 = bf16[256,704]{0,1:T(8,128)(2,1)S(1)} fusion(bf16[256,1408]{1,0:T(8,128)(2,1)S(1)} %bitcast.64, bf16[1408,3584]{1,0:T(8,128)(2,1)} %all-gather.3.cloned.1.call-done.weights_hbm), kind=kOutput, calls=%fused_computation.21 | convolution fusion | flops 507691008 | bytes 3244032 | tf_op jit(solution)/shard_map/dot_general | solution.py:37
  169.0 4.2 %all-to-all-start.2 = ((bf16[4,64,704]{2,1,0:T(8,128)(2,1)}), bf16[4,64,704]{2,1,0:T(8,128)(2,1)S(1)}, u32[]{:S(2)}, u32[]{:S(2)}) async-start(bf16[4,64,704]{2,1,0:T(8,128)(2,1)} %bitcast.17), calls=%async_computation.2 | async-start | bytes 786432 | tf_op jit(solution)/shard_map/all_to_all | solution.py:299
  173.4 1.2 collective-permute-start.6
  174.6 8.8 %all-to-all-done.2 = bf16[4,64,704]{2,1,0:T(8,128)(2,1)S(1)} async-done(((bf16[4,64,704]{2,1,0:T(8,128)(2,1)}), bf16[4,64,704]{2,1,0:T(8,128)(2,1)S(1)}, u32[]{:S(2)}, u32[]{:S(2)}) %all-to-all-start.2) | async-done | bytes 360480 | tf_op jit(solution)/shard_map/all_to_all | solution.py:299
  183.4 1.4 fusion.10
  184.8 9.9 %all-to-all-start.3 = ((bf16[64,8,768]{2,1,0:T(8,128)(2,1)}), bf16[64,8,768]{2,1,0:T(8,128)(2,1)S(1)}, u32[]{:S(2)}, u32[]{:S(2)}) async-start(bf16[64,8,768]{2,1,0:T(8,128)(2,1)} %fusion.10), calls=%async_computation.3 | async-start | bytes 1572864 | tf_op jit(solution)/shard_map/all_to_all | solution.py:305
  195.0 1.8 copy-done.1
  196.9 3.9 %convolution_convert_fusion.text = bf16[512,1408]{1,0:T(8,128)(2,1)} fusion(bf16[1408,1408]{1,0:T(8,128)(2,1)S(1)} %copy-done.1, bf16[128,1408]{1,0:T(8,128)(2,1)S(1)} %copy-done.6, bf16[384,1408]{1,0:T(8,128)(2,1)S(1)} %bitcast.63), kind=kOutput, calls=%fused_computation.2 | convolution fusion | flops 2033647616 | bytes 6848512 | tf_op jit(solution)/shard_map/dot_general | solution.py:37
  200.8 14.7 %all-to-all-done.3 = bf16[64,8,768]{2,1,0:T(8,128)(2,1)S(1)} async-done(((bf16[64,8,768]{2,1,0:T(8,128)(2,1)}), bf16[64,8,768]{2,1,0:T(8,128)(2,1)S(1)}, u32[]{:S(2)}, u32[]{:S(2)}) %all-to-all-start.3) | async-done | bytes 786464 | tf_op jit(solution)/shard_map/all_to_all | solution.py:305
  215.6 4.9 %collective-permute-start.7 = (bf16[512,768]{1,0:T(8,128)(2,1)S(1)}, bf16[512,768]{1,0:T(8,128)(2,1)S(1)}, u32[]{:S(2)}, u32[]{:S(2)}) collective-permute-start(bf16[512,768]{1,0:T(8,128)(2,1)S(1)} %bitcast.61), channel_id=1, source_target_pairs={{0,1},{1,0},{2,3},{3,2},{4,5},{5,4},{6,7},{7,6},{8,9},{9,8},{10,11... | collective-permute-start | bytes 2359304 | tf_op jit(solution)/shard_map/ppermute | solution.py:33
  221.3 1.1 collective-permute-done.7.other
  223.3 15.9 %shard_map.101 = bf16[128,1408]{1,0:T(8,128)(2,1)} custom-call(s32[4]{0:T(128)} %pad_add_fusion.info, bf16[512,768]{1,0:T(8,128)(2,1)} %bitcast.62, bf16[512,768]{1,0:T(8,128)(2,1)} %copy-done.4, bf16[512,1408]{1,0:T(8,128)(2,1)} %convolution_convert_fusion.text, bf16[1408,1408]{1,0:T(8,128)(2,1)} %fusion.reorder, ...), custom_call_target="tpu_custom_call" | custom-call | tf_op jit(solution)/shard_map/pallas_call | solution.py:178
  240.6 1.0 collective-permute-done.8
  241.6 1.6 add_convert_fusion
  (101 shorter events, 14.6 us)
Async XLA Ops:
  6.5 11.9 %copy-start.10 = (bf16[11,1,3,704]{3,2,1,0:T(4,128)(2,1)S(1)}, bf16[11,1,3,704]{3,2,1,0:T(4,128)(2,1)}, u32[]{:S(2)}) copy-start(bf16[11,1,3,704]{3,2,1,0:T(4,128)(2,1)} %param.18) | copy-start | bytes 139396
  6.5 12.0 %copy-start.11 = (bf16[704,11]{0,1:T(8,128)(2,1)S(1)}, bf16[704,11]{0,1:T(8,128)(2,1)}, u32[]{:S(2)}) copy-start(bf16[704,11]{0,1:T(8,128)(2,1)} %param.19) | copy-start | bytes 46468
  7.5 12.0 %copy-start = (bf16[256,1408]{1,0:T(8,128)(2,1)S(1)}, bf16[256,1408]{1,0:T(8,128)(2,1)}, u32[]{:S(2)}) copy-start(bf16[256,1408]{1,0:T(8,128)(2,1)} %param.10) | copy-start | bytes 2162692
  9.4 23.8 %all-to-all-start = ((bf16[4,22,2816]{2,1,0:T(8,128)(2,1)}), bf16[4,22,2816]{2,1,0:T(8,128)(2,1)S(1)}, u32[]{:S(2)}, u32[]{:S(2)}) async-start(bf16[4,22,2816]{2,1,0:T(8,128)(2,1)} %broadcast_in_dim.9), calls=%async_computation | async-start | bytes 1081344 | tf_op jit(solution)/shard_map/all_to_all | solution.py:57
  18.4 102.1 %all-gather.3.cloned.1.call-start = ((), (), s32[]{:S(2)}) async-start(), calls=%async_computation.4 | async-start | bytes 10723328 | tf_op jit(solution)/shard_map/all_gather | solution.py:256
  18.7 14.3 %collective-permute-start = (bf16[2,11,1408]{2,1,0:T(8,128)(2,1)S(1)}, bf16[2,11,1408]{2,1,0:T(8,128)(2,1)S(1)}, u32[]{:S(2)}, u32[]{:S(2)}) collective-permute-start(bf16[2,11,1408]{2,1,0:T(8,128)(2,1)S(1)} %pad_maximum_fusion.6), channel_id=1, source_target_pairs={{0,128},{128,0},{1,129},{129,1},{2,130},{130,2},{3,131},{131,3},{4... | collective-permute-start | bytes 185864 | tf_op jit(solution)/shard_map/ppermute | solution.py:229
  21.3 3.6 %copy-start.5 = (bf16[128,1408]{1,0:T(8,128)(2,1)S(1)}, bf16[128,1408]{1,0:T(8,128)(2,1)}, u32[]{:S(2)}) copy-start(bf16[128,1408]{1,0:T(8,128)(2,1)} %param.15) | copy-start | bytes 1081348
  33.0 0.9 copy-start.9
  34.8 186.5 %all-gather.5.cloned.1.call-start = ((), (), s32[]{:S(2)}) async-start(), calls=%async_computation.5 | async-start | bytes 8425472 | tf_op jit(solution)/shard_map/all_gather | solution.py:279
  34.9 34.2 %collective-permute-start.4 = (bf16[112,1408]{1,0:T(8,128)(2,1)S(1)}, bf16[112,1408]{1,0:T(8,128)(2,1)S(1)}, u32[]{:S(2)}, u32[]{:S(2)}) collective-permute-start(bf16[112,1408]{1,0:T(8,128)(2,1)S(1)} %maximum_maximum_fusion), channel_id=1, source_target_pairs={{0,2},{2,4},{4,6},{6,0},{1,3},{3,5},{5,7},{7,1},{8,10},{10,12},{12... | collective-permute-start | bytes 946184 | tf_op jit(solution)/shard_map/ppermute | solution.py:274
  35.1 33.9 %collective-permute-start.3 = (bf16[112,1408]{1,0:T(8,128)(2,1)S(1)}, bf16[112,1408]{1,0:T(8,128)(2,1)S(1)}, u32[]{:S(2)}, u32[]{:S(2)}) collective-permute-start(bf16[112,1408]{1,0:T(8,128)(2,1)S(1)} %maximum_maximum_fusion), channel_id=1, source_target_pairs={{0,4},{2,6},{4,0},{6,2},{1,5},{3,7},{5,1},{7,3},{8,12},{10,14},{12... | collective-permute-start | bytes 946184 | tf_op jit(solution)/shard_map/ppermute | solution.py:274
  39.4 28.9 %collective-permute-start.2 = (bf16[112,1408]{1,0:T(8,128)(2,1)S(1)}, bf16[112,1408]{1,0:T(8,128)(2,1)S(1)}, u32[]{:S(2)}, u32[]{:S(2)}) collective-permute-start(bf16[112,1408]{1,0:T(8,128)(2,1)S(1)} %maximum_maximum_fusion), channel_id=1, source_target_pairs={{0,6},{2,0},{4,2},{6,4},{1,7},{3,1},{5,3},{7,5},{8,14},{10,8},{12,... | collective-permute-start | bytes 946184 | tf_op jit(solution)/shard_map/ppermute | solution.py:274
  68.3 0.7 copy-start.7
  69.3 1.0 copy-start.12
  69.3 1.7 copy-start.13
  129.9 4.5 %copy-start.2 = (bf16[256,1408]{1,0:T(8,128)(2,1)S(1)}, bf16[256,1408]{1,0:T(8,128)(2,1)}, u32[]{:S(2)}) copy-start(bf16[256,1408]{1,0:T(8,128)(2,1)} %shard_map.100) | copy-start | bytes 2162692
  129.9 3.0 %collective-permute-start.1 = (bf16[256,1408]{1,0:T(8,128)(2,1)}, bf16[256,1408]{1,0:T(8,128)(2,1)S(1)}, u32[]{:S(2)}, u32[]{:S(2)}) collective-permute-start(bf16[256,1408]{1,0:T(8,128)(2,1)} %shard_map.100), channel_id=1, source_target_pairs={{0,1},{1,0},{2,3},{3,2},{4,5},{5,4},{6,7},{7,6},{8,9},{9,8},{10,11... | collective-permute-start | bytes 2162696 | tf_op jit(solution)/shard_map/ppermute | solution.py:33
  137.4 9.0 %copy-start.8 = (bf16[112,1408]{1,0:T(8,128)(2,1)S(1)}, bf16[112,1408]{1,0:T(8,128)(2,1)}, u32[]{:S(2)}) copy-start(bf16[112,1408]{1,0:T(8,128)(2,1)} %copy-done.7) | copy-start | bytes 946180
  139.7 25.9 %all-to-all-start.1 = ((bf16[4,64,1408]{2,1,0:T(8,128)(2,1)}), bf16[4,64,1408]{2,1,0:T(8,128)(2,1)S(1)}, u32[]{:S(2)}, u32[]{:S(2)}) async-start(bf16[4,64,1408]{2,1,0:T(8,128)(2,1)} %reshape.317), calls=%async_computation.1 | async-start | bytes 1441792 | tf_op jit(solution)/shard_map/all_to_all | solution.py:296
  146.5 26.8 %collective-permute-start.5 = (bf16[3,64,1408]{2,1,0:T(8,128)(2,1)S(1)}, bf16[3,64,1408]{2,1,0:T(8,128)(2,1)S(1)}, u32[]{:S(2)}, u32[]{:S(2)}) collective-permute-start(bf16[3,64,1408]{2,1,0:T(8,128)(2,1)S(1)} %pad_maximum_fusion.1), channel_id=1, source_target_pairs={{0,8},{8,16},{16,24},{24,32},{32,40},{40,48},{48,56},{56,64},{64,7... | collective-permute-start | bytes 1622024 | tf_op jit(solution)/shard_map/ppermute | solution.py:284
  169.0 14.3 %all-to-all-start.2 = ((bf16[4,64,704]{2,1,0:T(8,128)(2,1)}), bf16[4,64,704]{2,1,0:T(8,128)(2,1)S(1)}, u32[]{:S(2)}, u32[]{:S(2)}) async-start(bf16[4,64,704]{2,1,0:T(8,128)(2,1)} %bitcast.17), calls=%async_computation.2 | async-start | bytes 786432 | tf_op jit(solution)/shard_map/all_to_all | solution.py:299
  173.4 21.3 %collective-permute-start.6 = (bf16[3,64,1408]{2,1,0:T(8,128)(2,1)S(1)}, bf16[3,64,1408]{2,1,0:T(8,128)(2,1)S(1)}, u32[]{:S(2)}, u32[]{:S(2)}) collective-permute-start(bf16[3,64,1408]{2,1,0:T(8,128)(2,1)S(1)} %broadcast_select_fusion), channel_id=1, source_target_pairs={{0,1},{1,0},{2,3},{3,2},{4,5},{5,4},{6,7},{7,6},{8,9},{9,8},{10,11... | collective-permute-start | bytes 1622024 | tf_op jit(solution)/shard_map/ppermute | solution.py:33
  184.8 30.8 %all-to-all-start.3 = ((bf16[64,8,768]{2,1,0:T(8,128)(2,1)}), bf16[64,8,768]{2,1,0:T(8,128)(2,1)S(1)}, u32[]{:S(2)}, u32[]{:S(2)}) async-start(bf16[64,8,768]{2,1,0:T(8,128)(2,1)} %fusion.10), calls=%async_computation.3 | async-start | bytes 1572864 | tf_op jit(solution)/shard_map/all_to_all | solution.py:305
  194.7 2.1 copy-start.1
  194.9 2.0 copy-start.6
  196.9 23.6 %copy-start.14 = (s32[1,2]{1,0:T(1,128)S(1)}, s32[1,2]{1,0:T(1,128)}, u32[]{:S(2)}) copy-start(s32[1,2]{1,0:T(1,128)} %param.17) | copy-start | bytes 28
  215.6 6.9 %copy-start.3 = (bf16[64,8,768]{2,1,0:T(8,128)(2,1)}, bf16[64,8,768]{2,1,0:T(8,128)(2,1)S(1)}, u32[]{:S(2)}) copy-start(bf16[64,8,768]{2,1,0:T(8,128)(2,1)S(1)} %all-to-all-done.3) | copy-start | bytes 2359300
  215.6 6.9 %collective-permute-start.7 = (bf16[512,768]{1,0:T(8,128)(2,1)S(1)}, bf16[512,768]{1,0:T(8,128)(2,1)S(1)}, u32[]{:S(2)}, u32[]{:S(2)}) collective-permute-start(bf16[512,768]{1,0:T(8,128)(2,1)S(1)} %bitcast.61), channel_id=1, source_target_pairs={{0,1},{1,0},{2,3},{3,2},{4,5},{5,4},{6,7},{7,6},{8,9},{9,8},{10,11... | collective-permute-start | bytes 2359304 | tf_op jit(solution)/shard_map/ppermute | solution.py:33
  222.4 0.9 copy-start.4
  240.1 1.5 collective-permute-start.8
Sparse Core Ops, SparseCore 0:
  34.9 85.4 all-gather.2
  122.9 74.1 all-gather.4

commit v6 on v5

--- a/solution.py
+++ b/solution.py
@@ -66,7 +66,7 @@
 
 
 def decoder_block(
-    half, cap, info, got, other, text, reorder, weights_hbm, out, weights, heads, sem
+    half, cap, info, got, other, text, reorder, weights_hbm, keep, give, weights, heads, whole, sem
 ):
     load = pltpu.make_async_copy(weights_hbm, weights, sem)
     load.start()
@@ -101,7 +101,7 @@
         start = jnp.where(query_pos >= info[prompt], jnp.maximum(start, info[prompt]), start)
     allowed = jnp.where((key_pos <= query_pos) & (key_pos >= start), 1.0, 0.0)
     partial = attention(half, normed[REACH * block :], normed, weights, heads, allowed, None)
-    out[...] = contract_last(partial, reorder[...]).astype(BF)
+    split_rows(contract_last(partial, reorder[...]).astype(BF), sub, keep, give, whole)
 
 
 def attention(half, asking, asked, weights, heads, allowed, late):
@@ -124,7 +124,14 @@
     return contract_last(heads[...].astype(BF), weights[:, 3 * half - spare : 4 * half]).astype(BF)
 
 
-def vision_block(half, ends, normed, weights_hbm, out, weights, heads, sems):
+def split_rows(values, sub, keep, give, whole):
+    rows = keep.shape[0]
+    whole[...] = values
+    keep[...] = whole[pl.ds(pl.multiple_of(sub * rows, 16), rows), :]
+    give[...] = whole[pl.ds(pl.multiple_of((1 - sub) * rows, 16), rows), :]
+
+
+def vision_block(half, info, normed, weights_hbm, keep, give, weights, heads, whole, sems):
     early = pltpu.make_async_copy(
         weights_hbm.at[:, : 2 * half], weights.at[:, : 2 * half], sems.at[0]
     )
@@ -136,10 +143,10 @@
     rows = normed.shape[0]
 
     def image_of(row):
-        token = lax.shift_right_logical(row, 2)
+        token = lax.rem(row, rows // 4)
         image = jnp.zeros(row.shape, jnp.int32)
-        for step in range(ends.shape[0]):
-            image = image + jnp.where(token >= ends[step], 1, 0)
+        for step in range(1, info.shape[0]):
+            image = image + jnp.where(token >= info[step], 1, 0)
         return image
 
     own = image_of(lax.broadcasted_iota(jnp.int32, (rows, 1), 0))
@@ -147,28 +154,84 @@
     allowed = jnp.where(own == seen, 1.0, 0.0)
     patches = normed[...]
     early.wait()
-    out[...] = attention(half, patches, patches, weights, heads, allowed, late)
-
-
-def run_vision_block(half, ends, normed, weights):
+    partial = attention(half, patches, patches, weights, heads, allowed, late)
+    split_rows(partial, info[0], keep, give, whole)
+
+
+def run_vision_block(half, info, normed, weights):
     rows, width = normed.shape
     vmem = pl.BlockSpec(memory_space=pltpu.VMEM)
     return pl.pallas_call(
         functools.partial(vision_block, half),
-        out_shape=jax.ShapeDtypeStruct((rows, width), BF),
+        out_shape=[jax.ShapeDtypeStruct((rows // 2, width), BF)] * 2,
         in_specs=[
             pl.BlockSpec(memory_space=pltpu.SMEM),
             vmem,
             pl.BlockSpec(memory_space=pl.ANY),
         ],
-        out_specs=vmem,
+        out_specs=[vmem] * 2,
         scratch_shapes=[
             pltpu.VMEM((width, 4 * half), BF),
             pltpu.VMEM((rows, half + half % 128), F32),
+            pltpu.VMEM((rows, width), BF),
             pltpu.SemaphoreType.DMA((2,)),
         ],
         compiler_params=pltpu.CompilerParams(vmem_limit_bytes=56 << 20),
-    )(ends, normed, weights)
+    )(info, normed, weights)
+
+
+def merger_rows(patches, keep, other, spread, out):
+    hidden = patches[...].astype(F32) + (keep[...].astype(F32) + other[...].astype(F32))
+    ready = dot(layer_norm(hidden).astype(BF), spread[...]).astype(BF)
+    columns = out.shape[2]
+    for place in range(out.shape[0]):
+        out[place] = ready[:, place * columns : (place + 1) * columns]
+
+
+def run_merger_rows(lines, patches, keep, other, spread):
+    rows = patches.shape[0]
+    vmem = pl.BlockSpec(memory_space=pltpu.VMEM)
+    return pl.pallas_call(
+        merger_rows,
+        out_shape=jax.ShapeDtypeStruct((lines, rows, spread.shape[1] // lines), BF),
+        in_specs=[vmem] * 4,
+        out_specs=vmem,
+        compiler_params=pltpu.CompilerParams(vmem_limit_bytes=56 << 20),
+    )(patches, keep, other, spread)
+
+
+def merger_dot(at, depth, info, mine, theirs, weights_hbm, out, weights, sem):
+    load = pltpu.make_async_copy(weights_hbm.at[:, at : at + weights.shape[1]], weights, sem)
+    load.start()
+    sub = info[0]
+    lines, rows = mine.shape[:2]
+    half_rows = rows // 2
+    load.wait()
+    total = jnp.zeros((lines * half_rows, weights.shape[1]), F32)
+    for side, values in ((sub, mine), (1 - sub, theirs)):
+        for step in range(2):
+            part = values[:, step * half_rows : (step + 1) * half_rows, :]
+            part = part.reshape(lines * half_rows, part.shape[2])[:, :depth]
+            row = pl.multiple_of((2 * side + step) * depth, 16)
+            total = total + dot(part, weights[pl.ds(row, depth), :])
+    out[...] = total[:, : out.shape[1]].astype(BF)
+
+
+def run_merger_dot(half, depth, info, mine, theirs, weights):
+    lines, rows = mine.shape[:2]
+    vmem = pl.BlockSpec(memory_space=pltpu.VMEM)
+    return pl.pallas_call(
+        functools.partial(merger_dot, 4 * half, depth),
+        out_shape=jax.ShapeDtypeStruct((lines * rows // 2, half), BF),
+        in_specs=[pl.BlockSpec(memory_space=pltpu.SMEM), vmem, vmem]
+        + [pl.BlockSpec(memory_space=pl.ANY)],
+        out_specs=vmem,
+        scratch_shapes=[
+            pltpu.VMEM((weights.shape[0], weights.shape[1] - 4 * half), BF),
+            pltpu.SemaphoreType.DMA,
+        ],
+        compiler_params=pltpu.CompilerParams(vmem_limit_bytes=56 << 20),
+    )(info, mine, theirs, weights)
 
 
 def run_decoder_block(half, cap, info, got, other, text, reorder, weights):
@@ -177,14 +240,15 @@
     vmem = pl.BlockSpec(memory_space=pltpu.VMEM)
     return pl.pallas_call(
         functools.partial(decoder_block, half, cap),
-        out_shape=jax.ShapeDtypeStruct((block, width), BF),
+        out_shape=[jax.ShapeDtypeStruct((block // 2, width), BF)] * 2,
         in_specs=[pl.BlockSpec(memory_space=pltpu.SMEM)]
         + [vmem] * 4
         + [pl.BlockSpec(memory_space=pl.ANY)],
-        out_specs=vmem,
+        out_specs=[vmem] * 2,
         scratch_shapes=[
             pltpu.VMEM(weights.shape, BF),
             pltpu.VMEM((block, half + half % 128), F32),
+            pltpu.VMEM((block, width), BF),
             pltpu.SemaphoreType.DMA,
         ],
         compiler_params=pltpu.CompilerParams(vmem_limit_bytes=56 << 20),
@@ -230,8 +294,19 @@
     low = lax.axis_index("grp") == 0
     dec = jnp.stack([jnp.where(low, dec, dec_other), jnp.where(low, dec_other, dec)], axis=1)
     dec = dec.reshape(4 * drows, width)
-    patch_rows = patches.astype(F32)
-    normed = layer_norm(patch_rows).astype(BF)
+    tokens = rows_v // 4
+    patches = patches.reshape(tokens, 4, width).transpose(1, 0, 2).reshape(rows_v, width)
+    sub = lax.axis_index("sub")
+    side_v = rows_v // 2
+    own_patches = jnp.where(sub == 0, patches[:side_v], patches[side_v:])
+    normed = layer_norm(patches.astype(F32)).astype(BF)
+    depth = 4 * mrows
+    spread_at = jnp.arange(lines * (depth + pad_to(depth)), dtype=jnp.int32)
+    inner = spread_at % (depth + pad_to(depth))
+    source = inner // mrows * (lines * mrows) + inner % mrows
+    source = source + spread_at // (depth + pad_to(depth)) * mrows
+    source = jnp.where(inner < depth, source, width)
+    spread = (jnp.arange(width, dtype=jnp.int32)[:, None] == source[None, :]).astype(BF)
     me = lax.axis_index("zh")
     order = jnp.arange(width, dtype=jnp.int32)
     fan = 2 * drows
@@ -252,7 +327,9 @@
         ],
         axis=0,
     )
-    line_v, normed, reorder, mine = lax.optimization_barrier((line_v, normed, reorder, mine))
+    line_v, normed, reorder, mine, spread, own_patches = lax.optimization_barrier(
+        (line_v, normed, reorder, mine, spread, own_patches)
+    )
     full_v = lax.all_gather(line_v, PLANE, axis=0, tiled=True)
 
     piece_rows = text_embed.shape[0]
@@ -287,15 +364,12 @@
     window_text = jnp.concatenate([text.reshape(REACH * piece_rows, width), text_embed], axis=0)
     window_text = dot(window_text, reorder).astype(BF)
 
-    ends = jnp.cumsum(image_sizes[0])
-    partial = run_vision_block(half, ends, normed, full_v)
-    hidden = patch_rows + (partial.astype(F32) + swap_sub(partial).astype(F32))
-    tokens = rows_v // 4
-    merged = layer_norm(hidden).astype(BF).reshape(tokens, planes, lines, mrows)
-    merged = merged.transpose(2, 0, 1, 3).reshape(lines, tokens, planes * mrows)
+    place_info = jnp.concatenate([sub.astype(jnp.int32)[None], jnp.cumsum(image_sizes[0])])
+    keep, give = run_vision_block(half, place_info, normed, full_v)
+    merged = run_merger_rows(lines, own_patches, keep, swap_sub(give), spread)
     merged = lax.all_to_all(merged, "zh", split_axis=0, concat_axis=0, tiled=True)
-    partial = dot(merged.reshape(lines * tokens, planes * mrows), full_v[:, 4 * half : 5 * half])
-    partial = partial.astype(BF).reshape(lines, tokens, half)
+    partial = run_merger_dot(half, depth, place_info, merged, swap_sub(merged), full_v)
+    partial = partial.reshape(lines, tokens, half)
     partial = lax.all_to_all(partial, "zh", split_axis=0, concat_axis=0, tiled=True)
     embedded = jnp.sum(partial.astype(F32), axis=0).astype(BF)
 
@@ -311,13 +385,9 @@
     info = jnp.concatenate(
         [jnp.stack([lax.axis_index("sub"), lax.axis_index(TOK)]).astype(jnp.int32), starts]
     )
-    partial = run_decoder_block(
+    keep, give = run_decoder_block(
         half, cap, info, got, swap_sub(got), window_text, reorder, full_d
     )
-    sub = lax.axis_index("sub")
-    keep_rows = piece_rows // 2
-    give = lax.dynamic_slice_in_dim(partial, (1 - sub) * keep_rows, keep_rows, 0)
-    keep = lax.dynamic_slice_in_dim(partial, sub * keep_rows, keep_rows, 0)
     return (keep.astype(F32) + swap_sub(give).astype(F32)).astype(BF)
 
 

time: 251 us -> 245 us (0.976)
  Pallas kernels: 25.3 us -> 34.3 us
  waiting for transfers between devices: 126 us -> 121 us
  local copies, waits for them, and re-layouts: 13.8 us -> 8.86 us
  starting transfers between devices: 49.2 us -> 44.8 us
  matrix products: 7.84 us -> 5.31 us
    pallas_call x2 -> x4, Pallas kernels: 25.3 us -> 34.3 us  [the longest x1 15.9 us: run_decoder_block(): pl.pallas_call(functools.partial(decoder_block, half, cap), out_shape=[ja...]
    all_to_all x1, waiting for transfers between devices: 15.5 us -> 8.65 us  [shards(): lax.all_to_all(merged, 'zh', split_axis=0, concat_axis=0, tiled=True)]
    ppermute x1, waiting for transfers between devices: 7.94 us -> 2.82 us  [shards(): dec_other = lax.ppermute(dec, 'grp', [(0, 1), (1, 0)])]
    reshape x3 -> x2, local copies, waits for them, and re-layouts: 4.39 us -> 0.24 us  [shards(): patches.reshape(tokens, 4, width).transpose(1, 0, 2).reshape(rows_v, width)]
    convert_element_type x2, other arithmetic: 1.61 us -> 5.16 us  [the longest x1 3.98 us: shards(): (jnp.arange(width, dtype=jnp.int32)[:, None] == source[None, :]).astype(BF)]
    all_to_all x1, waiting for transfers between devices: 14.7 us -> 18.2 us  [shards(): lax.all_to_all(sent.reshape(pieces, slots, half + pad_to(half)), TOK, spl...]
    dot_general x3 -> x2, matrix products: 7.84 us -> 5.31 us  [dot(): return jnp.dot(a, b, preferred_element_type=F32)]
    ppermute x4 -> x5, starting transfers between devices: 7.51 us -> 5.11 us  [swap_sub(): return lax.ppermute(value, 'sub', [(0, 1), (1, 0)])]
  transfers between devices with their start and end apart: 15 -> 16, of which waited for: 9 -> 10; matrix products, arithmetic and copies ran while one was open for 10% -> 8% of each run, Pallas kernels for 4% -> 8%
where the time goes in v6:
time: 245 us
  waiting for transfers between devices  121 us (49%)
  starting transfers between devices  44.8 us (18%)
  Pallas kernels  34.3 us (14%)
  other arithmetic  16.5 us (7%)
  between operations  13.8 us (6%)
  local copies, waits for them, and re-layouts  8.86 us (4%)
  matrix products  5.31 us (2%)
    all_gather x1, waiting for transfers between devices, shards(): full_v = lax.all_gather(line_v, PLANE, axis=0, tiled=True)  50 us
    ppermute x3, waiting for transfers between devices, shards(): lax.ppermute(mine, 'zh', [(i, (i + s) % lines) for i in range(lines)])  25.6 us
    all_to_all x1, waiting for transfers between devices, shards(): lax.all_to_all(sent.reshape(pieces, slots, half + pad_to(half)), TOK, spl...  18.2 us
    pallas_call x1, Pallas kernels, run_decoder_block(): pl.pallas_call(functools.partial(decoder_block, half, cap), out_shape=[ja...  15.9 us
    all_to_all x1, waiting for transfers between devices, shards(): lax.all_to_all(partial, 'zh', split_axis=0, concat_axis=0, tiled=True)  11 us
    pallas_call x1, Pallas kernels, run_vision_block(): pl.pallas_call(functools.partial(vision_block, half), out_shape=[jax.Shap...  9.4 us
    all_to_all x1, starting transfers between devices, to_all(): return lax.all_to_all(spread, axes, split_axis=0, concat_axis=0, tiled=True)  9.01 us
    all_to_all x1, starting transfers between devices, shards(): lax.all_to_all(sent.reshape(pieces, slots, half + pad_to(half)), TOK, spl...  8.69 us
  transfers between devices with their start and end apart: 16, of which 10 were waited for; matrix products, arithmetic and copies ran while one was open for 8% of the time, Pallas kernels for 8%

profile of v6, /device:TPU:1, one launch (start us, length us, event | category | flops | bytes accessed | tf_op | source)
XLA Modules:
  0.0 244.7 jit_solution(10332660625574985614)
XLA Ops:
  6.5 1.0 copy.13
  9.4 9.0 %all-to-all-start = ((bf16[4,22,2816]{2,1,0:T(8,128)(2,1)}), bf16[4,22,2816]{2,1,0:T(8,128)(2,1)S(1)}, u32[]{:S(2)}, u32[]{:S(2)}) async-start(bf16[4,22,2816]{2,1,0:T(8,128)(2,1)} %broadcast_in_dim.13), calls=%async_computation | async-start | bytes 1081344 | tf_op jit(solution)/shard_map/all_to_all | solution.py:57
  20.5 3.6 %fusion.1.reorder = bf16[1408,1408]{1,0:T(8,128)(2,1)} fusion(s32[1408]{0:T(1024)S(1)} %fusion.40), kind=kLoop, calls=%fused_computation.3 | loop fusion | flops 3964928 | bytes 3970560 | tf_op jit(solution)/shard_map/convert_element_type | solution.py:319
  24.0 4.0 %fusion.spread = bf16[1408,1536]{1,0:T(8,128)(2,1)} fusion(s32[1536]{0:T(1024)S(1)} %fusion.41), kind=kLoop, calls=%fused_computation.1 | loop fusion | flops 4325376 | bytes 4331520 | tf_op jit(solution)/shard_map/convert_element_type | solution.py:309
  28.0 1.2 fusion.6.normed
  30.1 2.8 %collective-permute-done = bf16[2,11,1408]{2,1,0:T(8,128)(2,1)S(1)} collective-permute-done((bf16[2,11,1408]{2,1,0:T(8,128)(2,1)S(1)}, bf16[2,11,1408]{2,1,0:T(8,128)(2,1)S(1)}, u32[]{:S(2)}, u32[]{:S(2)}) %collective-permute-start) | collective-permute-done | bytes 61984 | tf_op jit(solution)/shard_map/ppermute | solution.py:293
  35.1 4.3 %collective-permute-start.4 = (bf16[112,1408]{1,0:T(8,128)(2,1)S(1)}, bf16[112,1408]{1,0:T(8,128)(2,1)S(1)}, u32[]{:S(2)}, u32[]{:S(2)}) collective-permute-start(bf16[112,1408]{1,0:T(8,128)(2,1)S(1)} %maximum_maximum_fusion), channel_id=1, source_target_pairs={{0,4},{2,6},{4,0},{6,2},{1,5},{3,7},{5,1},{7,3},{8,12},{10,14},{12... | collective-permute-start | bytes 946184 | tf_op jit(solution)/shard_map/ppermute | solution.py:351
  39.4 3.3 %collective-permute-start.3 = (bf16[112,1408]{1,0:T(8,128)(2,1)S(1)}, bf16[112,1408]{1,0:T(8,128)(2,1)S(1)}, u32[]{:S(2)}, u32[]{:S(2)}) collective-permute-start(bf16[112,1408]{1,0:T(8,128)(2,1)S(1)} %maximum_maximum_fusion), channel_id=1, source_target_pairs={{0,6},{2,0},{4,2},{6,4},{1,7},{3,1},{5,3},{7,5},{8,14},{10,8},{12,... | collective-permute-start | bytes 946184 | tf_op jit(solution)/shard_map/ppermute | solution.py:351
  42.7 25.6 %collective-permute-done.3 = bf16[112,1408]{1,0:T(8,128)(2,1)S(1)} collective-permute-done((bf16[112,1408]{1,0:T(8,128)(2,1)S(1)}, bf16[112,1408]{1,0:T(8,128)(2,1)S(1)}, u32[]{:S(2)}, u32[]{:S(2)}) %collective-permute-start.3) | collective-permute-done | bytes 315424 | tf_op jit(solution)/shard_map/ppermute | solution.py:351
  68.6 0.9 reshape.365
  70.5 50.0 %all-gather.3.cloned.1.call-done.weights_hbm = bf16[1408,3584]{1,0:T(8,128)(2,1)} async-done(((bf16[88,3584]{1,0:T(8,128)(2,1)}), bf16[1408,3584]{1,0:T(8,128)(2,1)}) %all-gather.3.cloned.1.call-update) | async-done | bytes 10092560 | tf_op jit(solution)/shard_map/all_gather | solution.py:333
  120.5 9.4 %shard_map.100 = (bf16[128,1408]{1,0:T(8,128)(2,1)}, bf16[128,1408]{1,0:T(8,128)(2,1)}) custom-call(s32[5]{0:T(128)} %pad_add_fusion.1.info, bf16[256,1408]{1,0:T(8,128)(2,1)} %fusion.6.normed, bf16[1408,3584]{1,0:T(8,128)(2,1)} %all-gather.3.cloned.1.call-done.weights_hbm), custom_call_target="tpu_custom_call" | custom-call | tf_op jit(solution)/shard_map/pallas_call | solution.py:164
  130.6 1.5 collective-permute-done.1.other
  132.9 4.5 %shard_map.101 = bf16[4,128,384]{2,1,0:T(8,128)(2,1)} custom-call(bf16[128,1408]{1,0:T(8,128)(2,1)} %bitcast.73, bf16[128,1408]{1,0:T(8,128)(2,1)} %get-tuple-element.20.keep, bf16[128,1408]{1,0:T(8,128)(2,1)} %copy-done.7, bf16[1408,1536]{1,0:T(8,128)(2,1)} %fusion.spread), custom_call_target="tpu_custom_call" | custom-call | tf_op jit(solution)/shard_map/pallas_call | solution.py:194
  137.4 6.7 %all-to-all-start.1 = ((bf16[4,128,384]{2,1,0:T(8,128)(2,1)}), bf16[4,128,384]{2,1,0:T(8,128)(2,1)S(1)}, u32[]{:S(2)}, u32[]{:S(2)}) async-start(bf16[4,128,384]{2,1,0:T(8,128)(2,1)} %shard_map.101), calls=%async_computation.1 | async-start | bytes 786432 | tf_op jit(solution)/shard_map/all_to_all | solution.py:370
  144.2 3.1 %collective-permute-start.6 = (bf16[3,64,1408]{2,1,0:T(8,128)(2,1)S(1)}, bf16[3,64,1408]{2,1,0:T(8,128)(2,1)S(1)}, u32[]{:S(2)}, u32[]{:S(2)}) collective-permute-start(bf16[3,64,1408]{2,1,0:T(8,128)(2,1)S(1)} %pad_maximum_fusion.1), channel_id=1, source_target_pairs={{0,8},{8,16},{16,24},{24,32},{32,40},{40,48},{48,56},{56,64},{64,7... | collective-permute-start | bytes 1622024 | tf_op jit(solution)/shard_map/ppermute | solution.py:361
  147.4 8.6 %all-to-all-done.1.mine = bf16[4,128,384]{2,1,0:T(8,128)(2,1)S(1)} async-done(((bf16[4,128,384]{2,1,0:T(8,128)(2,1)}), bf16[4,128,384]{2,1,0:T(8,128)(2,1)S(1)}, u32[]{:S(2)}, u32[]{:S(2)}) %all-to-all-start.1) | async-done | bytes 393248 | tf_op jit(solution)/shard_map/all_to_all | solution.py:370
  156.0 1.8 collective-permute-start.2
  158.2 0.9 collective-permute-done.2.theirs
  160.0 4.5 %shard_map.102 = bf16[256,704]{1,0:T(8,128)(2,1)} custom-call(s32[5]{0:T(128)} %pad_add_fusion.1.info, bf16[4,128,384]{2,1,0:T(8,128)(2,1)} %copy-done.2, bf16[4,128,384]{2,1,0:T(8,128)(2,1)} %copy-done.5, bf16[1408,3584]{1,0:T(8,128)(2,1)} %all-gather.3.cloned.1.call-done.weights_hbm), custom_call_target="tpu_custom_call" | custom-call | tf_op jit(solution)/shard_map/pallas_call | solution.py:223
  164.4 3.5 %all-to-all-start.2 = ((bf16[4,64,704]{2,1,0:T(8,128)(2,1)}), bf16[4,64,704]{2,1,0:T(8,128)(2,1)S(1)}, u32[]{:S(2)}, u32[]{:S(2)}) async-start(bf16[4,64,704]{2,1,0:T(8,128)(2,1)} %bitcast.72), calls=%async_computation.2 | async-start | bytes 786432 | tf_op jit(solution)/shard_map/all_to_all | solution.py:373
  168.8 11.0 %all-to-all-done.2 = bf16[4,64,704]{2,1,0:T(8,128)(2,1)S(1)} async-done(((bf16[4,64,704]{2,1,0:T(8,128)(2,1)}), bf16[4,64,704]{2,1,0:T(8,128)(2,1)S(1)}, u32[]{:S(2)}, u32[]{:S(2)}) %all-to-all-start.2) | async-done | bytes 360480 | tf_op jit(solution)/shard_map/all_to_all | solution.py:373
  179.9 1.4 fusion.7
  181.3 8.7 %all-to-all-start.3 = ((bf16[64,8,768]{2,1,0:T(8,128)(2,1)}), bf16[64,8,768]{2,1,0:T(8,128)(2,1)S(1)}, u32[]{:S(2)}, u32[]{:S(2)}) async-start(bf16[64,8,768]{2,1,0:T(8,128)(2,1)} %fusion.7), calls=%async_computation.3 | async-start | bytes 1572864 | tf_op jit(solution)/shard_map/all_to_all | solution.py:379
  190.3 2.0 copy-done
  192.3 3.9 %convolution_convert_fusion.text = bf16[512,1408]{1,0:T(8,128)(2,1)} fusion(bf16[1408,1408]{1,0:T(8,128)(2,1)S(1)} %copy-done, bf16[128,1408]{1,0:T(8,128)(2,1)S(1)} %copy-done.6, bf16[384,1408]{1,0:T(8,128)(2,1)S(1)} %bitcast.74), kind=kOutput, calls=%fused_computation.4 | convolution fusion | flops 2033647616 | bytes 6848512 | tf_op jit(solution)/shard_map/dot_general | solution.py:37
  196.2 18.2 %all-to-all-done.3 = bf16[64,8,768]{2,1,0:T(8,128)(2,1)S(1)} async-done(((bf16[64,8,768]{2,1,0:T(8,128)(2,1)}), bf16[64,8,768]{2,1,0:T(8,128)(2,1)S(1)}, u32[]{:S(2)}, u32[]{:S(2)}) %all-to-all-start.3) | async-done | bytes 786464 | tf_op jit(solution)/shard_map/all_to_all | solution.py:379
  214.4 1.4 collective-permute-start.8
  216.6 1.1 collective-permute-done.8.other
  218.6 15.9 %shard_map.103 = (bf16[64,1408]{1,0:T(8,128)(2,1)}, bf16[64,1408]{1,0:T(8,128)(2,1)}) custom-call(s32[4]{0:T(128)} %pad_add_fusion.info, bf16[512,768]{1,0:T(8,128)(2,1)} %bitcast.70, bf16[512,768]{1,0:T(8,128)(2,1)} %copy-done.3, bf16[512,1408]{1,0:T(8,128)(2,1)} %convolution_convert_fusion.text, bf16[1408,1408]{1,0:T(8,128)(2,1)} %fusion.1.reorder, ...), custom_call_target="tpu_custom_call" | custom-call | tf_op jit(solution)/shard_map/pallas_call | solution.py:241
  235.0 1.3 collective-permute-done.9
  236.2 1.6 add_convert_fusion
  (100 shorter events, 14.1 us)
Async XLA Ops:
  6.5 11.9 %copy-start.9 = (bf16[11,1,3,704]{3,2,1,0:T(4,128)(2,1)S(1)}, bf16[11,1,3,704]{3,2,1,0:T(4,128)(2,1)}, u32[]{:S(2)}) copy-start(bf16[11,1,3,704]{3,2,1,0:T(4,128)(2,1)} %param.18) | copy-start | bytes 139396
  6.5 12.0 %copy-start.10 = (bf16[704,11]{0,1:T(8,128)(2,1)S(1)}, bf16[704,11]{0,1:T(8,128)(2,1)}, u32[]{:S(2)}) copy-start(bf16[704,11]{0,1:T(8,128)(2,1)} %param.19) | copy-start | bytes 46468
  7.5 12.0 %copy-start.4 = (bf16[256,1408]{1,0:T(8,128)(2,1)S(1)}, bf16[256,1408]{1,0:T(8,128)(2,1)}, u32[]{:S(2)}) copy-start(bf16[256,1408]{1,0:T(8,128)(2,1)} %param.10) | copy-start | bytes 2162692
  9.4 23.8 %all-to-all-start = ((bf16[4,22,2816]{2,1,0:T(8,128)(2,1)}), bf16[4,22,2816]{2,1,0:T(8,128)(2,1)S(1)}, u32[]{:S(2)}, u32[]{:S(2)}) async-start(bf16[4,22,2816]{2,1,0:T(8,128)(2,1)} %broadcast_in_dim.13), calls=%async_computation | async-start | bytes 1081344 | tf_op jit(solution)/shard_map/all_to_all | solution.py:57
  18.4 102.0 %all-gather.3.cloned.1.call-start = ((), (), s32[]{:S(2)}) async-start(), calls=%async_computation.4 | async-start | bytes 10723328 | tf_op jit(solution)/shard_map/all_gather | solution.py:333
  18.7 14.3 %collective-permute-start = (bf16[2,11,1408]{2,1,0:T(8,128)(2,1)S(1)}, bf16[2,11,1408]{2,1,0:T(8,128)(2,1)S(1)}, u32[]{:S(2)}, u32[]{:S(2)}) collective-permute-start(bf16[2,11,1408]{2,1,0:T(8,128)(2,1)S(1)} %pad_maximum_fusion.6), channel_id=1, source_target_pairs={{0,128},{128,0},{1,129},{129,1},{2,130},{130,2},{3,131},{131,3},{4... | collective-permute-start | bytes 185864 | tf_op jit(solution)/shard_map/ppermute | solution.py:293
  28.0 2.0 copy-start.6
  33.0 0.9 copy-start.8
  34.8 181.8 %all-gather.5.cloned.1.call-start = ((), (), s32[]{:S(2)}) async-start(), calls=%async_computation.5 | async-start | bytes 8425472 | tf_op jit(solution)/shard_map/all_gather | solution.py:356
  34.8 33.5 %collective-permute-start.5 = (bf16[112,1408]{1,0:T(8,128)(2,1)S(1)}, bf16[112,1408]{1,0:T(8,128)(2,1)S(1)}, u32[]{:S(2)}, u32[]{:S(2)}) collective-permute-start(bf16[112,1408]{1,0:T(8,128)(2,1)S(1)} %maximum_maximum_fusion), channel_id=1, source_target_pairs={{0,2},{2,4},{4,6},{6,0},{1,3},{3,5},{5,7},{7,1},{8,10},{10,12},{12... | collective-permute-start | bytes 946184 | tf_op jit(solution)/shard_map/ppermute | solution.py:351
  35.1 33.2 %collective-permute-start.4 = (bf16[112,1408]{1,0:T(8,128)(2,1)S(1)}, bf16[112,1408]{1,0:T(8,128)(2,1)S(1)}, u32[]{:S(2)}, u32[]{:S(2)}) collective-permute-start(bf16[112,1408]{1,0:T(8,128)(2,1)S(1)} %maximum_maximum_fusion), channel_id=1, source_target_pairs={{0,4},{2,6},{4,0},{6,2},{1,5},{3,7},{5,1},{7,3},{8,12},{10,14},{12... | collective-permute-start | bytes 946184 | tf_op jit(solution)/shard_map/ppermute | solution.py:351
  39.4 28.9 %collective-permute-start.3 = (bf16[112,1408]{1,0:T(8,128)(2,1)S(1)}, bf16[112,1408]{1,0:T(8,128)(2,1)S(1)}, u32[]{:S(2)}, u32[]{:S(2)}) collective-permute-start(bf16[112,1408]{1,0:T(8,128)(2,1)S(1)} %maximum_maximum_fusion), channel_id=1, source_target_pairs={{0,6},{2,0},{4,2},{6,4},{1,7},{3,1},{5,3},{7,5},{8,14},{10,8},{12,... | collective-permute-start | bytes 946184 | tf_op jit(solution)/shard_map/ppermute | solution.py:351
  68.5 1.0 copy-start.11
  68.6 1.8 copy-start.12
  129.9 2.3 collective-permute-start.1
  132.1 0.7 copy-start.7
  137.4 18.6 %all-to-all-start.1 = ((bf16[4,128,384]{2,1,0:T(8,128)(2,1)}), bf16[4,128,384]{2,1,0:T(8,128)(2,1)S(1)}, u32[]{:S(2)}, u32[]{:S(2)}) async-start(bf16[4,128,384]{2,1,0:T(8,128)(2,1)} %shard_map.101), calls=%async_computation.1 | async-start | bytes 786432 | tf_op jit(solution)/shard_map/all_to_all | solution.py:370
  144.2 23.7 %collective-permute-start.6 = (bf16[3,64,1408]{2,1,0:T(8,128)(2,1)S(1)}, bf16[3,64,1408]{2,1,0:T(8,128)(2,1)S(1)}, u32[]{:S(2)}, u32[]{:S(2)}) collective-permute-start(bf16[3,64,1408]{2,1,0:T(8,128)(2,1)S(1)} %pad_maximum_fusion.1), channel_id=1, source_target_pairs={{0,8},{8,16},{16,24},{24,32},{32,40},{40,48},{48,56},{56,64},{64,7... | collective-permute-start | bytes 1622024 | tf_op jit(solution)/shard_map/ppermute | solution.py:361
  156.0 3.2 %copy-start.2 = (bf16[4,128,384]{2,1,0:T(8,128)(2,1)}, bf16[4,128,384]{2,1,0:T(8,128)(2,1)S(1)}, u32[]{:S(2)}) copy-start(bf16[4,128,384]{2,1,0:T(8,128)(2,1)S(1)} %all-to-all-done.1.mine) | copy-start | bytes 1179652
  156.0 3.2 %collective-permute-start.2 = (bf16[4,128,384]{2,1,0:T(8,128)(2,1)S(1)}, bf16[4,128,384]{2,1,0:T(8,128)(2,1)S(1)}, u32[]{:S(2)}, u32[]{:S(2)}) collective-permute-start(bf16[4,128,384]{2,1,0:T(8,128)(2,1)S(1)} %all-to-all-done.1.mine), channel_id=1, source_target_pairs={{0,1},{1,0},{2,3},{3,2},{4,5},{5,4},{6,7},{7,6},{8,9},{9,8},{10,11... | collective-permute-start | bytes 1179656 | tf_op jit(solution)/shard_map/ppermute | solution.py:33
  159.2 0.8 copy-start.5
  164.4 15.4 %all-to-all-start.2 = ((bf16[4,64,704]{2,1,0:T(8,128)(2,1)}), bf16[4,64,704]{2,1,0:T(8,128)(2,1)S(1)}, u32[]{:S(2)}, u32[]{:S(2)}) async-start(bf16[4,64,704]{2,1,0:T(8,128)(2,1)} %bitcast.72), calls=%async_computation.2 | async-start | bytes 786432 | tf_op jit(solution)/shard_map/all_to_all | solution.py:373
  168.1 21.9 %collective-permute-start.7 = (bf16[3,64,1408]{2,1,0:T(8,128)(2,1)S(1)}, bf16[3,64,1408]{2,1,0:T(8,128)(2,1)S(1)}, u32[]{:S(2)}, u32[]{:S(2)}) collective-permute-start(bf16[3,64,1408]{2,1,0:T(8,128)(2,1)S(1)} %broadcast_select_fusion), channel_id=1, source_target_pairs={{0,1},{1,0},{2,3},{3,2},{4,5},{5,4},{6,7},{7,6},{8,9},{9,8},{10,11... | collective-permute-start | bytes 1622024 | tf_op jit(solution)/shard_map/ppermute | solution.py:33
  181.3 33.1 %all-to-all-start.3 = ((bf16[64,8,768]{2,1,0:T(8,128)(2,1)}), bf16[64,8,768]{2,1,0:T(8,128)(2,1)S(1)}, u32[]{:S(2)}, u32[]{:S(2)}) async-start(bf16[64,8,768]{2,1,0:T(8,128)(2,1)} %fusion.7), calls=%async_computation.3 | async-start | bytes 1572864 | tf_op jit(solution)/shard_map/all_to_all | solution.py:379
  190.0 2.3 copy-start
  192.3 23.5 %copy-start.13 = (s32[1,2]{1,0:T(1,128)S(1)}, s32[1,2]{1,0:T(1,128)}, u32[]{:S(2)}) copy-start(s32[1,2]{1,0:T(1,128)} %param.17) | copy-start | bytes 28
  214.4 3.3 %copy-start.1 = (bf16[64,8,768]{2,1,0:T(8,128)(2,1)}, bf16[64,8,768]{2,1,0:T(8,128)(2,1)S(1)}, u32[]{:S(2)}) copy-start(bf16[64,8,768]{2,1,0:T(8,128)(2,1)S(1)} %all-to-all-done.3) | copy-start | bytes 2359300
  214.4 3.3 %collective-permute-start.8 = (bf16[512,768]{1,0:T(8,128)(2,1)S(1)}, bf16[512,768]{1,0:T(8,128)(2,1)S(1)}, u32[]{:S(2)}, u32[]{:S(2)}) collective-permute-start(bf16[512,768]{1,0:T(8,128)(2,1)S(1)} %bitcast.69), channel_id=1, source_target_pairs={{0,1},{1,0},{2,3},{3,2},{4,5},{5,4},{6,7},{7,6},{8,9},{9,8},{10,11... | collective-permute-start | bytes 2359304 | tf_op jit(solution)/shard_map/ppermute | solution.py:33
  217.7 0.9 copy-start.3
  234.5 1.7 collective-permute-start.9
Sparse Core Ops, SparseCore 0:
  34.9 85.4 all-gather.2
  122.9 88.1 all-gather.4

commit v7 on v6

--- a/solution.py
+++ b/solution.py
@@ -100,17 +100,15 @@
     for prompt in range(2, info.shape[0]):
         start = jnp.where(query_pos >= info[prompt], jnp.maximum(start, info[prompt]), start)
     allowed = jnp.where((key_pos <= query_pos) & (key_pos >= start), 1.0, 0.0)
-    partial = attention(half, normed[REACH * block :], normed, weights, heads, allowed, None)
+    partial = attention(half, normed[REACH * block :], normed, weights, heads, allowed)
     split_rows(contract_last(partial, reorder[...]).astype(BF), sub, keep, give, whole)
 
 
-def attention(half, asking, asked, weights, heads, allowed, late):
+def attention(half, asking, asked, weights, heads, allowed):
     spare = half % 128
     span = half + spare
     query = dot(asking, weights[:, :span])
     key = dot(asked, weights[:, half - spare : 2 * half])
-    if late is not None:
-        late.wait()
     value = dot(asked, weights[:, 2 * half : 2 * half + span])
     heads[:, :spare] = jnp.zeros((asking.shape[0], spare), F32)
     for head in range(half // HD):
@@ -131,53 +129,99 @@
     give[...] = whole[pl.ds(pl.multiple_of((1 - sub) * rows, 16), rows), :]
 
 
-def vision_block(half, info, normed, weights_hbm, keep, give, weights, heads, whole, sems):
-    early = pltpu.make_async_copy(
-        weights_hbm.at[:, : 2 * half], weights.at[:, : 2 * half], sems.at[0]
-    )
-    late = pltpu.make_async_copy(
-        weights_hbm.at[:, 2 * half : 4 * half], weights.at[:, 2 * half :], sems.at[1]
-    )
-    early.start()
-    late.start()
-    rows = normed.shape[0]
-
-    def image_of(row):
-        token = lax.rem(row, rows // 4)
-        image = jnp.zeros(row.shape, jnp.int32)
-        for step in range(1, info.shape[0]):
-            image = image + jnp.where(token >= info[step], 1, 0)
-        return image
-
-    own = image_of(lax.broadcasted_iota(jnp.int32, (rows, 1), 0))
-    seen = image_of(lax.broadcasted_iota(jnp.int32, (1, rows), 1))
-    allowed = jnp.where(own == seen, 1.0, 0.0)
-    patches = normed[...]
-    early.wait()
-    partial = attention(half, patches, patches, weights, heads, allowed, late)
-    split_rows(partial, info[0], keep, give, whole)
-
-
-def run_vision_block(half, info, normed, weights):
-    rows, width = normed.shape
+def vision_block(at, part, info, own, other, weights_hbm, own_out, other_out, weights, heads, sem):
+    base = at - at % 128
+    load = pltpu.make_async_copy(weights_hbm.at[:, base : base + weights.shape[1]], weights, sem)
+    load.start()
+    rows = own.shape[0]
+    images = info.shape[0] // 2
+    load.wait()
+    for side, (values, out) in enumerate(((own, own_out), (other, other_out))):
+
+        def image_of(row):
+            token = lax.rem(row, rows // 4)
+            image = jnp.zeros(row.shape, jnp.int32)
+            for step in range(images):
+                image = image + jnp.where(token >= info[side * images + step], 1, 0)
+            return image
+
+        asking = image_of(lax.broadcasted_iota(jnp.int32, (rows, 1), 0))
+        asked = image_of(lax.broadcasted_iota(jnp.int32, (1, rows), 1))
+        allowed = jnp.where(asking == asked, 1.0, 0.0)
+        triple = []
+        for member in range(3):
+            begin = at - base + member * part
+            end = begin + part
+            low = begin - begin % 128
+            high = end + -end % 128
+            triple.append((dot(values[...], weights[:, low:high]), begin - low))
+        heads[...] = jnp.zeros(heads.shape, F32)
+        for head in range(part // HD):
+            query, key, value = (
+                array[:, shift + head * HD : shift + (head + 1) * HD].astype(BF)
+                for array, shift in triple
+            )
+            raw = jnp.exp(contract_last(query, key) * (1.0 / math.sqrt(HD))) * allowed
+            share = (raw * (1.0 / jnp.sum(raw, axis=1, keepdims=True))).astype(BF)
+            heads[:, head * HD : (head + 1) * HD] = dot(share, value)
+        out[...] = heads[...].astype(BF)
+
+
+def run_vision_block(at, part, info, own, other, weights):
+    rows, width = own.shape
+    vmem = pl.BlockSpec(memory_space=pltpu.VMEM)
+    end = at + 3 * part
+    return pl.pallas_call(
+        functools.partial(vision_block, at, part),
+        out_shape=[jax.ShapeDtypeStruct((rows, part + pad_to(part)), BF)] * 2,
+        in_specs=[pl.BlockSpec(memory_space=pltpu.SMEM), vmem, vmem]
+        + [pl.BlockSpec(memory_space=pl.ANY)],
+        out_specs=[vmem] * 2,
+        scratch_shapes=[
+            pltpu.VMEM((width, end + pad_to(end) - (at - at % 128)), BF),
+            pltpu.VMEM((rows, part + pad_to(part)), F32),
+            pltpu.SemaphoreType.DMA,
+        ],
+        compiler_params=pltpu.CompilerParams(vmem_limit_bytes=56 << 20),
+    )(info, own, other, weights)
+
+
+def vision_output(at, part, info, own, other, weights_hbm, keep, give, weights, heads, whole, sem):
+    base = at - at % 128
+    load = pltpu.make_async_copy(weights_hbm.at[:, base : base + weights.shape[1]], weights, sem)
+    load.start()
+    heads[...] = jnp.zeros(heads.shape, F32)
+    low = info[1] == 0
+    begin = at - base
+    mine = own[...].astype(F32)[:, :part]
+    theirs = other[...].astype(F32)[:, :part]
+    heads[:, begin : begin + part] = jnp.where(low, mine, theirs)
+    heads[:, begin + part : begin + 2 * part] = jnp.where(low, theirs, mine)
+    load.wait()
+    partial = contract_last(heads[...].astype(BF), weights[...])
+    split_rows(partial.astype(BF), info[0], keep, give, whole)
+
+
+def run_vision_output(at, part, info, own, other, weights):
+    rows = own.shape[0]
+    width = weights.shape[0]
+    end = at + 2 * part
+    span = end + pad_to(end) - (at - at % 128)
     vmem = pl.BlockSpec(memory_space=pltpu.VMEM)
     return pl.pallas_call(
-        functools.partial(vision_block, half),
+        functools.partial(vision_output, at, part),
         out_shape=[jax.ShapeDtypeStruct((rows // 2, width), BF)] * 2,
-        in_specs=[
-            pl.BlockSpec(memory_space=pltpu.SMEM),
-            vmem,
-            pl.BlockSpec(memory_space=pl.ANY),
-        ],
+        in_specs=[pl.BlockSpec(memory_space=pltpu.SMEM), vmem, vmem]
+        + [pl.BlockSpec(memory_space=pl.ANY)],
         out_specs=[vmem] * 2,
         scratch_shapes=[
-            pltpu.VMEM((width, 4 * half), BF),
-            pltpu.VMEM((rows, half + half % 128), F32),
+            pltpu.VMEM((width, span), BF),
+            pltpu.VMEM((rows, span), F32),
             pltpu.VMEM((rows, width), BF),
-            pltpu.SemaphoreType.DMA((2,)),
+            pltpu.SemaphoreType.DMA,
         ],
         compiler_params=pltpu.CompilerParams(vmem_limit_bytes=56 << 20),
-    )(info, normed, weights)
+    )(info, own, other, weights)
 
 
 def merger_rows(patches, keep, other, spread, out):
@@ -200,8 +244,8 @@
     )(patches, keep, other, spread)
 
 
-def merger_dot(at, depth, info, mine, theirs, weights_hbm, out, weights, sem):
-    load = pltpu.make_async_copy(weights_hbm.at[:, at : at + weights.shape[1]], weights, sem)
+def merger_dot(depth, info, mine, theirs, weights_hbm, out, weights, sem):
+    load = pltpu.make_async_copy(weights_hbm.at[:, : weights.shape[1]], weights, sem)
     load.start()
     sub = info[0]
     lines, rows = mine.shape[:2]
@@ -221,13 +265,13 @@
     lines, rows = mine.shape[:2]
     vmem = pl.BlockSpec(memory_space=pltpu.VMEM)
     return pl.pallas_call(
-        functools.partial(merger_dot, 4 * half, depth),
+        functools.partial(merger_dot, depth),
         out_shape=jax.ShapeDtypeStruct((lines * rows // 2, half), BF),
         in_specs=[pl.BlockSpec(memory_space=pltpu.SMEM), vmem, vmem]
         + [pl.BlockSpec(memory_space=pl.ANY)],
         out_specs=vmem,
         scratch_shapes=[
-            pltpu.VMEM((weights.shape[0], weights.shape[1] - 4 * half), BF),
+            pltpu.VMEM((weights.shape[0], half + pad_to(half)), BF),
             pltpu.SemaphoreType.DMA,
         ],
         compiler_params=pltpu.CompilerParams(vmem_limit_bytes=56 << 20),
@@ -275,12 +319,17 @@
     krows = vision_inproj.shape[0]
     mrows = merger_weight.shape[0]
 
-    line = jnp.concatenate(
-        [vision_inproj.reshape(krows, 3 * half), vision_outproj.T], axis=1
-    )
-    line = to_all(line, "zh").reshape(lines * krows, 4 * half)
+    group = lax.axis_index("grp")
+    part = half // 2
+    vin = vision_inproj.reshape(krows, 3, 2, part)
+    vin = jnp.where(group == 0, vin[:, :, 0], vin[:, :, 1]).reshape(krows, 3 * part)
+    line = jnp.concatenate([vin, vision_outproj.T], axis=1)
+    line = to_all(line, "zh").reshape(lines * krows, 3 * part + half)
+    at_in = half + pad_to(half)
+    at_out = at_in + 3 * part
+    end = at_out + half
     merge = jnp.pad(merger_weight, ((0, 0), (0, pad_to(half))))
-    line_v = jnp.concatenate([line, merge], axis=1)
+    line_v = jnp.concatenate([merge, line, jnp.zeros((mrows, pad_to(end)), BF)], axis=1)
 
     drows = decoder_inproj.shape[0]
     dec = decoder_inproj.reshape(drows, 3 * half)
@@ -300,6 +349,9 @@
     side_v = rows_v // 2
     own_patches = jnp.where(sub == 0, patches[:side_v], patches[side_v:])
     normed = layer_norm(patches.astype(F32)).astype(BF)
+    ends = jnp.cumsum(image_sizes[0])
+    mark = jnp.pad(ends.astype(BF)[None], ((0, 15), (0, width - ends.shape[0])))
+    marked = jnp.concatenate([normed, mark], axis=0)
     depth = 4 * mrows
     spread_at = jnp.arange(lines * (depth + pad_to(depth)), dtype=jnp.int32)
     inner = spread_at % (depth + pad_to(depth))
@@ -327,8 +379,8 @@
         ],
         axis=0,
     )
-    line_v, normed, reorder, mine, spread, own_patches = lax.optimization_barrier(
-        (line_v, normed, reorder, mine, spread, own_patches)
+    line_v, marked, reorder, mine, spread, own_patches = lax.optimization_barrier(
+        (line_v, marked, reorder, mine, spread, own_patches)
     )
     full_v = lax.all_gather(line_v, PLANE, axis=0, tiled=True)
 
@@ -364,8 +416,15 @@
     window_text = jnp.concatenate([text.reshape(REACH * piece_rows, width), text_embed], axis=0)
     window_text = dot(window_text, reorder).astype(BF)
 
-    place_info = jnp.concatenate([sub.astype(jnp.int32)[None], jnp.cumsum(image_sizes[0])])
-    keep, give = run_vision_block(half, place_info, normed, full_v)
+    place_info = jnp.stack([sub, group]).astype(jnp.int32)
+    pair = [(0, 1), (1, 0)]
+    paired = lax.ppermute(marked, "grp", pair)
+    both_ends = jnp.concatenate([ends, paired[rows_v, : ends.shape[0]].astype(jnp.int32)])
+    heads, heads_away = run_vision_block(
+        at_in, part, both_ends, marked[:rows_v], paired[:rows_v], full_v
+    )
+    heads_back = lax.ppermute(heads_away, "grp", pair)
+    keep, give = run_vision_output(at_out, part, place_info, heads, heads_back, full_v)
     merged = run_merger_rows(lines, own_patches, keep, swap_sub(give), spread)
     merged = lax.all_to_all(merged, "zh", split_axis=0, concat_axis=0, tiled=True)
     partial = run_merger_dot(half, depth, place_info, merged, swap_sub(merged), full_v)

time: 245 us -> 241 us (0.984)
  waiting for transfers between devices: 121 us -> 104 us
  starting transfers between devices: 44.8 us -> 50.8 us
  local copies, waits for them, and re-layouts: 8.86 us -> 12.5 us
  Pallas kernels: 34.3 us -> 37.5 us
    all_gather x1, waiting for transfers between devices: 50 us -> 16.9 us  [shards(): full_v = lax.all_gather(line_v, PLANE, axis=0, tiled=True)]
    ppermute x0 -> x2, waiting for transfers between devices: none -> 21.3 us  [the longest x1 16.6 us: shards(): paired = lax.ppermute(marked, 'grp', pair)]
    pallas_call x2 -> x3, Pallas kernels: 13.9 us -> 17.1 us  [the longest x1 8.14 us: run_vision_block(): pl.pallas_call(functools.partial(vision_block, at, part), out_shape=[jax....]
    ppermute x1, waiting for transfers between devices: 2.82 us -> 0.01 us  [shards(): dec_other = lax.ppermute(dec, 'grp', [(0, 1), (1, 0)])]
    unnamed x30 -> x31, local copies, waits for them, and re-layouts: 6 us -> 5.58 us
  transfers between devices with their start and end apart: 16 -> 18, of which waited for: 10 -> 11; matrix products, arithmetic and copies ran while one was open for 8% -> 9% of each run, Pallas kernels for 8% -> 9%
where the time goes in v7:
time: 241 us; the launch traced here: 240 us
  waiting for transfers between devices  104 us (43%)
  starting transfers between devices  50.8 us (21%)
  Pallas kernels  37.5 us (16%)
  other arithmetic  15.4 us (6%)
  between operations  13.8 us (6%)
  local copies, waits for them, and re-layouts  12.5 us (5%)
  matrix products  5.29 us (2%)
    ppermute x3, waiting for transfers between devices, shards(): lax.ppermute(mine, 'zh', [(i, (i + s) % lines) for i in range(lines)])  25.5 us
    all_to_all x1, waiting for transfers between devices, shards(): lax.all_to_all(sent.reshape(pieces, slots, half + pad_to(half)), TOK, spl...  18.1 us
    all_gather x1, waiting for transfers between devices, shards(): full_v = lax.all_gather(line_v, PLANE, axis=0, tiled=True)  16.9 us
    ppermute x1, waiting for transfers between devices, shards(): paired = lax.ppermute(marked, 'grp', pair)  16.6 us
    pallas_call x1, Pallas kernels, run_decoder_block(): pl.pallas_call(functools.partial(decoder_block, half, cap), out_shape=[ja...  15.9 us
    all_to_all x1, starting transfers between devices, shards(): lax.all_to_all(sent.reshape(pieces, slots, half + pad_to(half)), TOK, spl...  9.74 us
    all_to_all x1, waiting for transfers between devices, shards(): lax.all_to_all(partial, 'zh', split_axis=0, concat_axis=0, tiled=True)  9.18 us
    ppermute x3, starting transfers between devices, shards(): lax.ppermute(mine, 'zh', [(i, (i + s) % lines) for i in range(lines)])  9.02 us
  transfers between devices with their start and end apart: 18, of which 11 were waited for; matrix products, arithmetic and copies ran while one was open for 9% of the time, Pallas kernels for 9%

profile of v7, /device:TPU:1, one launch (start us, length us, event | category | flops | bytes accessed | tf_op | source)
XLA Modules:
  0.0 239.8 jit_solution(4140013483083414428)
XLA Ops:
  9.7 9.0 %all-to-all-start = ((bf16[4,22,1760]{2,1,0:T(8,128)(2,1)}), bf16[4,22,1760]{2,1,0:T(8,128)(2,1)S(1)}, u32[]{:S(2)}, u32[]{:S(2)}) async-start(bf16[4,22,1760]{2,1,0:T(8,128)(2,1)} %broadcast_in_dim.15), calls=%async_computation | async-start | bytes 688128 | tf_op jit(solution)/shard_map/all_to_all | solution.py:57
  21.0 3.6 %fusion.1.reorder = bf16[1408,1408]{1,0:T(8,128)(2,1)} fusion(s32[1408]{0:T(1024)S(1)} %fusion.40), kind=kLoop, calls=%fused_computation.3 | loop fusion | flops 3964928 | bytes 3970560 | tf_op jit(solution)/shard_map/convert_element_type | solution.py:371
  24.5 3.9 %fusion.spread = bf16[1408,1536]{1,0:T(8,128)(2,1)} fusion(s32[1536]{0:T(1024)S(1)} %fusion.41), kind=kLoop, calls=%fused_computation.1 | loop fusion | flops 4325376 | bytes 4331520 | tf_op jit(solution)/shard_map/convert_element_type | solution.py:361
  31.7 2.4 %collective-permute-start.7 = (bf16[112,1408]{1,0:T(8,128)(2,1)S(1)}, bf16[112,1408]{1,0:T(8,128)(2,1)S(1)}, u32[]{:S(2)}, u32[]{:S(2)}) collective-permute-start(bf16[112,1408]{1,0:T(8,128)(2,1)S(1)} %maximum_maximum_fusion), channel_id=1, source_target_pairs={{0,2},{2,4},{4,6},{6,0},{1,3},{3,5},{5,7},{7,1},{8,10},{10,12},{12... | collective-permute-start | bytes 946184 | tf_op jit(solution)/shard_map/ppermute | solution.py:403
  34.2 3.3 %collective-permute-start.6 = (bf16[112,1408]{1,0:T(8,128)(2,1)S(1)}, bf16[112,1408]{1,0:T(8,128)(2,1)S(1)}, u32[]{:S(2)}, u32[]{:S(2)}) collective-permute-start(bf16[112,1408]{1,0:T(8,128)(2,1)S(1)} %maximum_maximum_fusion), channel_id=1, source_target_pairs={{0,4},{2,6},{4,0},{6,2},{1,5},{3,7},{5,1},{7,3},{8,12},{10,14},{12... | collective-permute-start | bytes 946184 | tf_op jit(solution)/shard_map/ppermute | solution.py:403
  37.4 3.3 %collective-permute-start.5 = (bf16[112,1408]{1,0:T(8,128)(2,1)S(1)}, bf16[112,1408]{1,0:T(8,128)(2,1)S(1)}, u32[]{:S(2)}, u32[]{:S(2)}) collective-permute-start(bf16[112,1408]{1,0:T(8,128)(2,1)S(1)} %maximum_maximum_fusion), channel_id=1, source_target_pairs={{0,6},{2,0},{4,2},{6,4},{1,7},{3,1},{5,3},{7,5},{8,14},{10,8},{12,... | collective-permute-start | bytes 946184 | tf_op jit(solution)/shard_map/ppermute | solution.py:403
  40.8 25.5 %collective-permute-done.5 = bf16[112,1408]{1,0:T(8,128)(2,1)S(1)} collective-permute-done((bf16[112,1408]{1,0:T(8,128)(2,1)S(1)}, bf16[112,1408]{1,0:T(8,128)(2,1)S(1)}, u32[]{:S(2)}, u32[]{:S(2)}) %collective-permute-start.5) | collective-permute-done | bytes 315424 | tf_op jit(solution)/shard_map/ppermute | solution.py:403
  69.5 16.6 %collective-permute-done.1 = bf16[272,1408]{1,0:T(8,128)(2,1)S(1)} collective-permute-done((bf16[272,1408]{1,0:T(8,128)(2,1)S(1)}, bf16[272,1408]{1,0:T(8,128)(2,1)S(1)}, u32[]{:S(2)}, u32[]{:S(2)}) %collective-permute-start.1) | collective-permute-done | bytes 765984 | tf_op jit(solution)/shard_map/ppermute | solution.py:421
  87.6 16.9 %all-gather.3.cloned.1.call-done.weights_hbm = bf16[1408,2560]{1,0:T(8,128)(2,1)} async-done(((bf16[88,2560]{1,0:T(8,128)(2,1)}), bf16[1408,2560]{1,0:T(8,128)(2,1)}) %all-gather.3.cloned.1.call-update) | async-done | bytes 7208976 | tf_op jit(solution)/shard_map/all_gather | solution.py:385
  104.5 8.1 %shard_map.100 = (bf16[256,384]{1,0:T(8,128)(2,1)}, bf16[256,384]{1,0:T(8,128)(2,1)}) custom-call(s32[8]{0:T(128)} %pad_add_fusion.2.info, bf16[256,1408]{1,0:T(8,128)(2,1)} %slice.71.own, bf16[256,1408]{1,0:T(8,128)(2,1)} %slice.89.other, bf16[1408,2560]{1,0:T(8,128)(2,1)} %all-gather.3.cloned.1.call-done.weights_hbm), custom_call_target="tpu_custom_call" | custom-call | tf_op jit(solution)/shard_map/pallas_call | solution.py:174
  112.7 1.4 collective-permute-start.2
  114.0 4.7 %collective-permute-done.2.other = bf16[256,384]{1,0:T(8,128)(2,1)S(1)} collective-permute-done((bf16[256,384]{1,0:T(8,128)(2,1)}, bf16[256,384]{1,0:T(8,128)(2,1)S(1)}, u32[]{:S(2)}, u32[]{:S(2)}) %collective-permute-start.2) | collective-permute-done | bytes 196640 | tf_op jit(solution)/shard_map/ppermute | solution.py:426
  119.4 4.4 %shard_map.101 = (bf16[128,1408]{1,0:T(8,128)(2,1)}, bf16[128,1408]{1,0:T(8,128)(2,1)}) custom-call(s32[2]{0:T(128)} %pad_add_fusion.1.info, bf16[256,384]{1,0:T(8,128)(2,1)} %get-tuple-element.22.own, bf16[256,384]{1,0:T(8,128)(2,1)} %copy-done.8, bf16[1408,2560]{1,0:T(8,128)(2,1)} %all-gather.3.cloned.1.call-done.weights_hbm), custom_call_target="tpu_custom_call" | custom-call | tf_op jit(solution)/shard_map/pallas_call | solution.py:211
  123.9 1.7 collective-permute-start.3
  125.6 1.5 collective-permute-done.3.other
  127.9 4.5 %shard_map.102 = bf16[4,128,384]{2,1,0:T(8,128)(2,1)} custom-call(bf16[128,1408]{1,0:T(8,128)(2,1)} %bitcast.83, bf16[128,1408]{1,0:T(8,128)(2,1)} %get-tuple-element.24.keep, bf16[128,1408]{1,0:T(8,128)(2,1)} %copy-done.7, bf16[1408,1536]{1,0:T(8,128)(2,1)} %fusion.spread), custom_call_target="tpu_custom_call" | custom-call | tf_op jit(solution)/shard_map/pallas_call | solution.py:238
  132.3 6.7 %all-to-all-start.1 = ((bf16[4,128,384]{2,1,0:T(8,128)(2,1)}), bf16[4,128,384]{2,1,0:T(8,128)(2,1)S(1)}, u32[]{:S(2)}, u32[]{:S(2)}) async-start(bf16[4,128,384]{2,1,0:T(8,128)(2,1)} %shard_map.102), calls=%async_computation.1 | async-start | bytes 786432 | tf_op jit(solution)/shard_map/all_to_all | solution.py:429
  139.1 3.1 %collective-permute-start.8 = (bf16[3,64,1408]{2,1,0:T(8,128)(2,1)S(1)}, bf16[3,64,1408]{2,1,0:T(8,128)(2,1)S(1)}, u32[]{:S(2)}, u32[]{:S(2)}) collective-permute-start(bf16[3,64,1408]{2,1,0:T(8,128)(2,1)S(1)} %pad_maximum_fusion.1), channel_id=1, source_target_pairs={{0,8},{8,16},{16,24},{24,32},{32,40},{40,48},{48,56},{56,64},{64,7... | collective-permute-start | bytes 1622024 | tf_op jit(solution)/shard_map/ppermute | solution.py:413
  142.2 8.7 %all-to-all-done.1.mine = bf16[4,128,384]{2,1,0:T(8,128)(2,1)S(1)} async-done(((bf16[4,128,384]{2,1,0:T(8,128)(2,1)}), bf16[4,128,384]{2,1,0:T(8,128)(2,1)S(1)}, u32[]{:S(2)}, u32[]{:S(2)}) %all-to-all-start.1) | async-done | bytes 393248 | tf_op jit(solution)/shard_map/all_to_all | solution.py:429
  150.9 1.8 collective-permute-start.4
  154.8 4.5 %shard_map.103 = bf16[256,704]{1,0:T(8,128)(2,1)} custom-call(s32[2]{0:T(128)} %pad_add_fusion.1.info, bf16[4,128,384]{2,1,0:T(8,128)(2,1)} %copy-done.2, bf16[4,128,384]{2,1,0:T(8,128)(2,1)} %copy-done.5, bf16[1408,2560]{1,0:T(8,128)(2,1)} %all-gather.3.cloned.1.call-done.weights_hbm), custom_call_target="tpu_custom_call" | custom-call | tf_op jit(solution)/shard_map/pallas_call | solution.py:267
  159.3 3.5 %all-to-all-start.2 = ((bf16[4,64,704]{2,1,0:T(8,128)(2,1)}), bf16[4,64,704]{2,1,0:T(8,128)(2,1)S(1)}, u32[]{:S(2)}, u32[]{:S(2)}) async-start(bf16[4,64,704]{2,1,0:T(8,128)(2,1)} %bitcast.82), calls=%async_computation.2 | async-start | bytes 786432 | tf_op jit(solution)/shard_map/all_to_all | solution.py:432
  162.9 2.0 collective-permute-start.9
  164.9 9.2 %all-to-all-done.2 = bf16[4,64,704]{2,1,0:T(8,128)(2,1)S(1)} async-done(((bf16[4,64,704]{2,1,0:T(8,128)(2,1)}), bf16[4,64,704]{2,1,0:T(8,128)(2,1)S(1)}, u32[]{:S(2)}, u32[]{:S(2)}) %all-to-all-start.2) | async-done | bytes 360480 | tf_op jit(solution)/shard_map/all_to_all | solution.py:432
  174.2 1.4 fusion.8
  175.5 9.7 %all-to-all-start.3 = ((bf16[64,8,768]{2,1,0:T(8,128)(2,1)}), bf16[64,8,768]{2,1,0:T(8,128)(2,1)S(1)}, u32[]{:S(2)}, u32[]{:S(2)}) async-start(bf16[64,8,768]{2,1,0:T(8,128)(2,1)} %fusion.8), calls=%async_computation.3 | async-start | bytes 1572864 | tf_op jit(solution)/shard_map/all_to_all | solution.py:438
  185.6 1.8 copy-done
  187.4 3.9 %convolution_convert_fusion.text = bf16[512,1408]{1,0:T(8,128)(2,1)} fusion(bf16[1408,1408]{1,0:T(8,128)(2,1)S(1)} %copy-done, bf16[128,1408]{1,0:T(8,128)(2,1)S(1)} %copy-done.6, bf16[384,1408]{1,0:T(8,128)(2,1)S(1)} %bitcast.84), kind=kOutput, calls=%fused_computation.4 | convolution fusion | flops 2033647616 | bytes 6848512 | tf_op jit(solution)/shard_map/dot_general | solution.py:37
  191.3 18.1 %all-to-all-done.3 = bf16[64,8,768]{2,1,0:T(8,128)(2,1)S(1)} async-done(((bf16[64,8,768]{2,1,0:T(8,128)(2,1)}), bf16[64,8,768]{2,1,0:T(8,128)(2,1)S(1)}, u32[]{:S(2)}, u32[]{:S(2)}) %all-to-all-start.3) | async-done | bytes 786464 | tf_op jit(solution)/shard_map/all_to_all | solution.py:438
  209.5 1.4 collective-permute-start.10
  213.7 15.9 %shard_map.104 = (bf16[64,1408]{1,0:T(8,128)(2,1)}, bf16[64,1408]{1,0:T(8,128)(2,1)}) custom-call(s32[4]{0:T(128)} %pad_add_fusion.info, bf16[512,768]{1,0:T(8,128)(2,1)} %bitcast.80, bf16[512,768]{1,0:T(8,128)(2,1)} %copy-done.3, bf16[512,1408]{1,0:T(8,128)(2,1)} %convolution_convert_fusion.text, bf16[1408,1408]{1,0:T(8,128)(2,1)} %fusion.1.reorder, ...), custom_call_target="tpu_custom_call" | custom-call | tf_op jit(solution)/shard_map/pallas_call | solution.py:285
  231.3 1.6 add_convert_fusion
  (117 shorter events, 21.9 us)
Async XLA Ops:
  6.5 12.2 %copy-start.10 = (bf16[11,1,3,704]{3,2,1,0:T(4,128)(2,1)S(1)}, bf16[11,1,3,704]{3,2,1,0:T(4,128)(2,1)}, u32[]{:S(2)}) copy-start(bf16[11,1,3,704]{3,2,1,0:T(4,128)(2,1)} %param.18) | copy-start | bytes 139396
  6.5 12.3 %copy-start.11 = (bf16[704,11]{0,1:T(8,128)(2,1)S(1)}, bf16[704,11]{0,1:T(8,128)(2,1)}, u32[]{:S(2)}) copy-start(bf16[704,11]{0,1:T(8,128)(2,1)} %param.19) | copy-start | bytes 46468
  6.5 13.2 %copy-start.4 = (bf16[256,1408]{1,0:T(8,128)(2,1)S(1)}, bf16[256,1408]{1,0:T(8,128)(2,1)}, u32[]{:S(2)}) copy-start(bf16[256,1408]{1,0:T(8,128)(2,1)} %param.10) | copy-start | bytes 2162692
  9.7 20.9 %all-to-all-start = ((bf16[4,22,1760]{2,1,0:T(8,128)(2,1)}), bf16[4,22,1760]{2,1,0:T(8,128)(2,1)S(1)}, u32[]{:S(2)}, u32[]{:S(2)}) async-start(bf16[4,22,1760]{2,1,0:T(8,128)(2,1)} %broadcast_in_dim.15), calls=%async_computation | async-start | bytes 688128 | tf_op jit(solution)/shard_map/all_to_all | solution.py:57
  18.7 85.8 %all-gather.3.cloned.1.call-start = ((), (), s32[]{:S(2)}) async-start(), calls=%async_computation.4 | async-start | bytes 7659520 | tf_op jit(solution)/shard_map/all_gather | solution.py:385
  18.9 11.3 %collective-permute-start = (bf16[2,11,1408]{2,1,0:T(8,128)(2,1)S(1)}, bf16[2,11,1408]{2,1,0:T(8,128)(2,1)S(1)}, u32[]{:S(2)}, u32[]{:S(2)}) collective-permute-start(bf16[2,11,1408]{2,1,0:T(8,128)(2,1)S(1)} %pad_maximum_fusion.5), channel_id=1, source_target_pairs={{0,128},{128,0},{1,129},{129,1},{2,130},{130,2},{3,131},{131,3},{4... | collective-permute-start | bytes 185864 | tf_op jit(solution)/shard_map/ppermute | solution.py:342
  19.9 0.7 copy-start.12
  24.5 3.9 %copy-start.6 = (bf16[128,1408]{1,0:T(8,128)(2,1)S(1)}, bf16[128,1408]{1,0:T(8,128)(2,1)}, u32[]{:S(2)}) copy-start(bf16[128,1408]{1,0:T(8,128)(2,1)} %param.15) | copy-start | bytes 1081348
  29.3 0.9 copy-start.9
  31.7 180.1 %all-gather.5.cloned.1.call-start = ((), (), s32[]{:S(2)}) async-start(), calls=%async_computation.5 | async-start | bytes 8425472 | tf_op jit(solution)/shard_map/all_gather | solution.py:408
  31.7 34.6 %collective-permute-start.7 = (bf16[112,1408]{1,0:T(8,128)(2,1)S(1)}, bf16[112,1408]{1,0:T(8,128)(2,1)S(1)}, u32[]{:S(2)}, u32[]{:S(2)}) collective-permute-start(bf16[112,1408]{1,0:T(8,128)(2,1)S(1)} %maximum_maximum_fusion), channel_id=1, source_target_pairs={{0,2},{2,4},{4,6},{6,0},{1,3},{3,5},{5,7},{7,1},{8,10},{10,12},{12... | collective-permute-start | bytes 946184 | tf_op jit(solution)/shard_map/ppermute | solution.py:403
  34.2 32.1 %collective-permute-start.6 = (bf16[112,1408]{1,0:T(8,128)(2,1)S(1)}, bf16[112,1408]{1,0:T(8,128)(2,1)S(1)}, u32[]{:S(2)}, u32[]{:S(2)}) collective-permute-start(bf16[112,1408]{1,0:T(8,128)(2,1)S(1)} %maximum_maximum_fusion), channel_id=1, source_target_pairs={{0,4},{2,6},{4,0},{6,2},{1,5},{3,7},{5,1},{7,3},{8,12},{10,14},{12... | collective-permute-start | bytes 946184 | tf_op jit(solution)/shard_map/ppermute | solution.py:403
  37.4 28.8 %collective-permute-start.5 = (bf16[112,1408]{1,0:T(8,128)(2,1)S(1)}, bf16[112,1408]{1,0:T(8,128)(2,1)S(1)}, u32[]{:S(2)}, u32[]{:S(2)}) collective-permute-start(bf16[112,1408]{1,0:T(8,128)(2,1)S(1)} %maximum_maximum_fusion), channel_id=1, source_target_pairs={{0,6},{2,0},{4,2},{6,4},{1,7},{3,1},{5,3},{7,5},{8,14},{10,8},{12,... | collective-permute-start | bytes 946184 | tf_op jit(solution)/shard_map/ppermute | solution.py:403
  66.5 1.9 copy-start.13
  67.5 18.6 %collective-permute-start.1 = (bf16[272,1408]{1,0:T(8,128)(2,1)S(1)}, bf16[272,1408]{1,0:T(8,128)(2,1)S(1)}, u32[]{:S(2)}, u32[]{:S(2)}) collective-permute-start(bf16[272,1408]{1,0:T(8,128)(2,1)S(1)} %fusion.9), channel_id=1, source_target_pairs={{0,128},{128,0},{1,129},{129,1},{2,130},{130,2},{3,131},{131,3},{4... | collective-permute-start | bytes 2297864 | tf_op jit(solution)/shard_map/ppermute | solution.py:421
  112.7 6.1 %collective-permute-start.2 = (bf16[256,384]{1,0:T(8,128)(2,1)}, bf16[256,384]{1,0:T(8,128)(2,1)S(1)}, u32[]{:S(2)}, u32[]{:S(2)}) collective-permute-start(bf16[256,384]{1,0:T(8,128)(2,1)} %get-tuple-element.23), channel_id=1, source_target_pairs={{0,128},{128,0},{1,129},{129,1},{2,130},{130,2},{3,131},{131,3},{4... | collective-permute-start | bytes 589832 | tf_op jit(solution)/shard_map/ppermute | solution.py:426
  123.9 3.2 %collective-permute-start.3 = (bf16[128,1408]{1,0:T(8,128)(2,1)}, bf16[128,1408]{1,0:T(8,128)(2,1)S(1)}, u32[]{:S(2)}, u32[]{:S(2)}) collective-permute-start(bf16[128,1408]{1,0:T(8,128)(2,1)} %get-tuple-element.25), channel_id=1, source_target_pairs={{0,1},{1,0},{2,3},{3,2},{4,5},{5,4},{6,7},{7,6},{8,9},{9,8},{10,11... | collective-permute-start | bytes 1081352 | tf_op jit(solution)/shard_map/ppermute | solution.py:33
  127.1 0.8 copy-start.7
  132.3 18.6 %all-to-all-start.1 = ((bf16[4,128,384]{2,1,0:T(8,128)(2,1)}), bf16[4,128,384]{2,1,0:T(8,128)(2,1)S(1)}, u32[]{:S(2)}, u32[]{:S(2)}) async-start(bf16[4,128,384]{2,1,0:T(8,128)(2,1)} %shard_map.102), calls=%async_computation.1 | async-start | bytes 786432 | tf_op jit(solution)/shard_map/all_to_all | solution.py:429
  139.1 23.7 %collective-permute-start.8 = (bf16[3,64,1408]{2,1,0:T(8,128)(2,1)S(1)}, bf16[3,64,1408]{2,1,0:T(8,128)(2,1)S(1)}, u32[]{:S(2)}, u32[]{:S(2)}) collective-permute-start(bf16[3,64,1408]{2,1,0:T(8,128)(2,1)S(1)} %pad_maximum_fusion.1), channel_id=1, source_target_pairs={{0,8},{8,16},{16,24},{24,32},{32,40},{40,48},{48,56},{56,64},{64,7... | collective-permute-start | bytes 1622024 | tf_op jit(solution)/shard_map/ppermute | solution.py:413
  150.9 3.1 %copy-start.2 = (bf16[4,128,384]{2,1,0:T(8,128)(2,1)}, bf16[4,128,384]{2,1,0:T(8,128)(2,1)S(1)}, u32[]{:S(2)}) copy-start(bf16[4,128,384]{2,1,0:T(8,128)(2,1)S(1)} %all-to-all-done.1.mine) | copy-start | bytes 1179652
  150.9 3.1 %collective-permute-start.4 = (bf16[4,128,384]{2,1,0:T(8,128)(2,1)S(1)}, bf16[4,128,384]{2,1,0:T(8,128)(2,1)S(1)}, u32[]{:S(2)}, u32[]{:S(2)}) collective-permute-start(bf16[4,128,384]{2,1,0:T(8,128)(2,1)S(1)} %all-to-all-done.1.mine), channel_id=1, source_target_pairs={{0,1},{1,0},{2,3},{3,2},{4,5},{5,4},{6,7},{7,6},{8,9},{9,8},{10,11... | collective-permute-start | bytes 1179656 | tf_op jit(solution)/shard_map/ppermute | solution.py:33
  154.0 0.8 copy-start.5
  159.3 14.8 %all-to-all-start.2 = ((bf16[4,64,704]{2,1,0:T(8,128)(2,1)}), bf16[4,64,704]{2,1,0:T(8,128)(2,1)S(1)}, u32[]{:S(2)}, u32[]{:S(2)}) async-start(bf16[4,64,704]{2,1,0:T(8,128)(2,1)} %bitcast.82), calls=%async_computation.2 | async-start | bytes 786432 | tf_op jit(solution)/shard_map/all_to_all | solution.py:432
  162.9 22.4 %collective-permute-start.9 = (bf16[3,64,1408]{2,1,0:T(8,128)(2,1)S(1)}, bf16[3,64,1408]{2,1,0:T(8,128)(2,1)S(1)}, u32[]{:S(2)}, u32[]{:S(2)}) collective-permute-start(bf16[3,64,1408]{2,1,0:T(8,128)(2,1)S(1)} %broadcast_select_fusion), channel_id=1, source_target_pairs={{0,1},{1,0},{2,3},{3,2},{4,5},{5,4},{6,7},{7,6},{8,9},{9,8},{10,11... | collective-permute-start | bytes 1622024 | tf_op jit(solution)/shard_map/ppermute | solution.py:33
  175.5 33.9 %all-to-all-start.3 = ((bf16[64,8,768]{2,1,0:T(8,128)(2,1)}), bf16[64,8,768]{2,1,0:T(8,128)(2,1)S(1)}, u32[]{:S(2)}, u32[]{:S(2)}) async-start(bf16[64,8,768]{2,1,0:T(8,128)(2,1)} %fusion.8), calls=%async_computation.3 | async-start | bytes 1572864 | tf_op jit(solution)/shard_map/all_to_all | solution.py:438
  185.3 2.1 copy-start
  187.4 23.5 %copy-start.14 = (s32[1,2]{1,0:T(1,128)S(1)}, s32[1,2]{1,0:T(1,128)}, u32[]{:S(2)}) copy-start(s32[1,2]{1,0:T(1,128)} %param.17) | copy-start | bytes 28
  209.5 3.3 %copy-start.1 = (bf16[64,8,768]{2,1,0:T(8,128)(2,1)}, bf16[64,8,768]{2,1,0:T(8,128)(2,1)S(1)}, u32[]{:S(2)}) copy-start(bf16[64,8,768]{2,1,0:T(8,128)(2,1)S(1)} %all-to-all-done.3) | copy-start | bytes 2359300
  209.5 3.3 %collective-permute-start.10 = (bf16[512,768]{1,0:T(8,128)(2,1)S(1)}, bf16[512,768]{1,0:T(8,128)(2,1)S(1)}, u32[]{:S(2)}, u32[]{:S(2)}) collective-permute-start(bf16[512,768]{1,0:T(8,128)(2,1)S(1)} %bitcast.79), channel_id=1, source_target_pairs={{0,1},{1,0},{2,3},{3,2},{4,5},{5,4},{6,7},{7,6},{8,9},{9,8},{10,11... | collective-permute-start | bytes 2359304 | tf_op jit(solution)/shard_map/ppermute | solution.py:33
  212.8 0.9 copy-start.3
  229.6 1.7 collective-permute-start.11
  (1 other events, 0.7 us)
Sparse Core Ops, SparseCore 0:
  31.8 72.6 all-gather.2
  107.0 83.5 all-gather.4

commit v8 on v7

--- a/solution.py
+++ b/solution.py
@@ -129,61 +129,59 @@
     give[...] = whole[pl.ds(pl.multiple_of((1 - sub) * rows, 16), rows), :]
 
 
-def vision_block(at, part, info, own, other, weights_hbm, own_out, other_out, weights, heads, sem):
+def vision_block(at, part, info, values, weights_hbm, out, weights, heads, sem):
     base = at - at % 128
     load = pltpu.make_async_copy(weights_hbm.at[:, base : base + weights.shape[1]], weights, sem)
     load.start()
-    rows = own.shape[0]
-    images = info.shape[0] // 2
+    rows = values.shape[0]
+
+    def image_of(row):
+        token = lax.rem(row, rows // 4)
+        image = jnp.zeros(row.shape, jnp.int32)
+        for step in range(info.shape[0]):
+            image = image + jnp.where(token >= info[step], 1, 0)
+        return image
+
+    asking = image_of(lax.broadcasted_iota(jnp.int32, (rows, 1), 0))
+    asked = image_of(lax.broadcasted_iota(jnp.int32, (1, rows), 1))
+    allowed = jnp.where(asking == asked, 1.0, 0.0)
+    heads[...] = jnp.zeros(heads.shape, F32)
     load.wait()
-    for side, (values, out) in enumerate(((own, own_out), (other, other_out))):
-
-        def image_of(row):
-            token = lax.rem(row, rows // 4)
-            image = jnp.zeros(row.shape, jnp.int32)
-            for step in range(images):
-                image = image + jnp.where(token >= info[side * images + step], 1, 0)
-            return image
-
-        asking = image_of(lax.broadcasted_iota(jnp.int32, (rows, 1), 0))
-        asked = image_of(lax.broadcasted_iota(jnp.int32, (1, rows), 1))
-        allowed = jnp.where(asking == asked, 1.0, 0.0)
-        triple = []
-        for member in range(3):
-            begin = at - base + member * part
-            end = begin + part
-            low = begin - begin % 128
-            high = end + -end % 128
-            triple.append((dot(values[...], weights[:, low:high]), begin - low))
-        heads[...] = jnp.zeros(heads.shape, F32)
-        for head in range(part // HD):
-            query, key, value = (
-                array[:, shift + head * HD : shift + (head + 1) * HD].astype(BF)
-                for array, shift in triple
-            )
-            raw = jnp.exp(contract_last(query, key) * (1.0 / math.sqrt(HD))) * allowed
-            share = (raw * (1.0 / jnp.sum(raw, axis=1, keepdims=True))).astype(BF)
-            heads[:, head * HD : (head + 1) * HD] = dot(share, value)
-        out[...] = heads[...].astype(BF)
-
-
-def run_vision_block(at, part, info, own, other, weights):
-    rows, width = own.shape
+    triple = []
+    for member in range(3):
+        begin = at - base + member * part
+        end = begin + part
+        low = begin - begin % 128
+        high = end + -end % 128
+        triple.append((dot(values[...], weights[:, low:high]), begin - low))
+    for head in range(part // HD):
+        query, key, value = (
+            array[:, shift + head * HD : shift + (head + 1) * HD].astype(BF)
+            for array, shift in triple
+        )
+        raw = jnp.exp(contract_last(query, key) * (1.0 / math.sqrt(HD))) * allowed
+        share = (raw * (1.0 / jnp.sum(raw, axis=1, keepdims=True))).astype(BF)
+        heads[:, head * HD : (head + 1) * HD] = dot(share, value)
+    out[...] = heads[...].astype(BF)
+
+
+def run_vision_block(at, part, info, values, weights):
+    rows, width = values.shape
     vmem = pl.BlockSpec(memory_space=pltpu.VMEM)
     end = at + 3 * part
     return pl.pallas_call(
         functools.partial(vision_block, at, part),
-        out_shape=[jax.ShapeDtypeStruct((rows, part + pad_to(part)), BF)] * 2,
-        in_specs=[pl.BlockSpec(memory_space=pltpu.SMEM), vmem, vmem]
+        out_shape=jax.ShapeDtypeStruct((rows, part + pad_to(part)), BF),
+        in_specs=[pl.BlockSpec(memory_space=pltpu.SMEM), vmem]
         + [pl.BlockSpec(memory_space=pl.ANY)],
-        out_specs=[vmem] * 2,
+        out_specs=vmem,
         scratch_shapes=[
             pltpu.VMEM((width, end + pad_to(end) - (at - at % 128)), BF),
             pltpu.VMEM((rows, part + pad_to(part)), F32),
             pltpu.SemaphoreType.DMA,
         ],
         compiler_params=pltpu.CompilerParams(vmem_limit_bytes=56 << 20),
-    )(info, own, other, weights)
+    )(info, values, weights)
 
 
 def vision_output(at, part, info, own, other, weights_hbm, keep, give, weights, heads, whole, sem):
@@ -419,10 +417,9 @@
     place_info = jnp.stack([sub, group]).astype(jnp.int32)
     pair = [(0, 1), (1, 0)]
     paired = lax.ppermute(marked, "grp", pair)
-    both_ends = jnp.concatenate([ends, paired[rows_v, : ends.shape[0]].astype(jnp.int32)])
-    heads, heads_away = run_vision_block(
-        at_in, part, both_ends, marked[:rows_v], paired[:rows_v], full_v
-    )
+    paired_ends = paired[rows_v, : ends.shape[0]].astype(jnp.int32)
+    heads_away = run_vision_block(at_in, part, paired_ends, paired[:rows_v], full_v)
+    heads = run_vision_block(at_in, part, ends, marked[:rows_v], full_v)
     heads_back = lax.ppermute(heads_away, "grp", pair)
     keep, give = run_vision_output(at_out, part, place_info, heads, heads_back, full_v)
     merged = run_merger_rows(lines, own_patches, keep, swap_sub(give), spread)

time: 241 us -> 240 us (level)
  waiting for transfers between devices: 104 us -> 100 us
  Pallas kernels: 37.5 us -> 41 us
    ppermute x1, waiting for transfers between devices: 4.68 us -> 0.01 us  [shards(): heads_back = lax.ppermute(heads_away, 'grp', pair)]
    pallas_call x1 -> x2, Pallas kernels: 8.14 us -> 11.5 us  [run_vision_block(): pl.pallas_call(functools.partial(vision_block, at, part), out_shape=jax.S...]
    unnamed x31 -> x33, local copies, waits for them, and re-layouts: 5.58 us -> 5.49 us
  transfers between devices with their start and end apart: 18 -> 18, of which waited for: 11 -> 10; matrix products, arithmetic and copies ran while one was open for 9% -> 9% of each run, Pallas kernels for 9% -> 10%
where the time goes in v8:
time: 240 us; the launch traced here: 239 us
  waiting for transfers between devices  100 us (42%)
  starting transfers between devices  51.1 us (21%)
  Pallas kernels  41 us (17%)
  other arithmetic  15.4 us (6%)
  between operations  13.9 us (6%)
  local copies, waits for them, and re-layouts  12.4 us (5%)
  matrix products  5.32 us (2%)
    ppermute x3, waiting for transfers between devices, shards(): lax.ppermute(mine, 'zh', [(i, (i + s) % lines) for i in range(lines)])  25.5 us
    all_to_all x1, waiting for transfers between devices, shards(): lax.all_to_all(sent.reshape(pieces, slots, half + pad_to(half)), TOK, spl...  17.9 us
    all_gather x1, waiting for transfers between devices, shards(): full_v = lax.all_gather(line_v, PLANE, axis=0, tiled=True)  17.1 us
    ppermute x1, waiting for transfers between devices, shards(): paired = lax.ppermute(marked, 'grp', pair)  16.6 us
    pallas_call x1, Pallas kernels, run_decoder_block(): pl.pallas_call(functools.partial(decoder_block, half, cap), out_shape=[ja...  16 us
    pallas_call x2, Pallas kernels, run_vision_block(): pl.pallas_call(functools.partial(vision_block, at, part), out_shape=jax.S...  11.5 us
    all_to_all x1, waiting for transfers between devices, shards(): lax.all_to_all(partial, 'zh', split_axis=0, concat_axis=0, tiled=True)  10.7 us
    all_to_all x1, starting transfers between devices, shards(): lax.all_to_all(sent.reshape(pieces, slots, half + pad_to(half)), TOK, spl...  9.22 us
  transfers between devices with their start and end apart: 18, of which 10 were waited for; matrix products, arithmetic and copies ran while one was open for 9% of the time, Pallas kernels for 10%

profile of v8, /device:TPU:1, one launch (start us, length us, event | category | flops | bytes accessed | tf_op | source)
XLA Modules:
  0.0 239.3 jit_solution(12685672225348102739)
XLA Ops:
  6.5 1.2 reshape.352
  9.7 9.0 %all-to-all-start = ((bf16[4,22,1760]{2,1,0:T(8,128)(2,1)}), bf16[4,22,1760]{2,1,0:T(8,128)(2,1)S(1)}, u32[]{:S(2)}, u32[]{:S(2)}) async-start(bf16[4,22,1760]{2,1,0:T(8,128)(2,1)} %broadcast_in_dim.15), calls=%async_computation | async-start | bytes 688128 | tf_op jit(solution)/shard_map/all_to_all | solution.py:57
  21.0 3.6 %fusion.1.reorder = bf16[1408,1408]{1,0:T(8,128)(2,1)} fusion(s32[1408]{0:T(1024)S(1)} %fusion.40), kind=kLoop, calls=%fused_computation.3 | loop fusion | flops 3964928 | bytes 3970560 | tf_op jit(solution)/shard_map/convert_element_type | solution.py:369
  24.6 3.9 %fusion.spread = bf16[1408,1536]{1,0:T(8,128)(2,1)} fusion(s32[1536]{0:T(1024)S(1)} %fusion.41), kind=kLoop, calls=%fused_computation.1 | loop fusion | flops 4325376 | bytes 4331520 | tf_op jit(solution)/shard_map/convert_element_type | solution.py:359
  31.7 2.4 %collective-permute-start.7 = (bf16[112,1408]{1,0:T(8,128)(2,1)S(1)}, bf16[112,1408]{1,0:T(8,128)(2,1)S(1)}, u32[]{:S(2)}, u32[]{:S(2)}) collective-permute-start(bf16[112,1408]{1,0:T(8,128)(2,1)S(1)} %maximum_maximum_fusion), channel_id=1, source_target_pairs={{0,2},{2,4},{4,6},{6,0},{1,3},{3,5},{5,7},{7,1},{8,10},{10,12},{12... | collective-permute-start | bytes 946184 | tf_op jit(solution)/shard_map/ppermute | solution.py:401
  34.2 3.3 %collective-permute-start.6 = (bf16[112,1408]{1,0:T(8,128)(2,1)S(1)}, bf16[112,1408]{1,0:T(8,128)(2,1)S(1)}, u32[]{:S(2)}, u32[]{:S(2)}) collective-permute-start(bf16[112,1408]{1,0:T(8,128)(2,1)S(1)} %maximum_maximum_fusion), channel_id=1, source_target_pairs={{0,4},{2,6},{4,0},{6,2},{1,5},{3,7},{5,1},{7,3},{8,12},{10,14},{12... | collective-permute-start | bytes 946184 | tf_op jit(solution)/shard_map/ppermute | solution.py:401
  37.5 3.3 %collective-permute-start.5 = (bf16[112,1408]{1,0:T(8,128)(2,1)S(1)}, bf16[112,1408]{1,0:T(8,128)(2,1)S(1)}, u32[]{:S(2)}, u32[]{:S(2)}) collective-permute-start(bf16[112,1408]{1,0:T(8,128)(2,1)S(1)} %maximum_maximum_fusion), channel_id=1, source_target_pairs={{0,6},{2,0},{4,2},{6,4},{1,7},{3,1},{5,3},{7,5},{8,14},{10,8},{12,... | collective-permute-start | bytes 946184 | tf_op jit(solution)/shard_map/ppermute | solution.py:401
  40.8 25.5 %collective-permute-done.5 = bf16[112,1408]{1,0:T(8,128)(2,1)S(1)} collective-permute-done((bf16[112,1408]{1,0:T(8,128)(2,1)S(1)}, bf16[112,1408]{1,0:T(8,128)(2,1)S(1)}, u32[]{:S(2)}, u32[]{:S(2)}) %collective-permute-start.5) | collective-permute-done | bytes 315424 | tf_op jit(solution)/shard_map/ppermute | solution.py:401
  69.3 16.6 %collective-permute-done.1 = bf16[272,1408]{1,0:T(8,128)(2,1)S(1)} collective-permute-done((bf16[272,1408]{1,0:T(8,128)(2,1)S(1)}, bf16[272,1408]{1,0:T(8,128)(2,1)S(1)}, u32[]{:S(2)}, u32[]{:S(2)}) %collective-permute-start.1) | collective-permute-done | bytes 765984 | tf_op jit(solution)/shard_map/ppermute | solution.py:419
  87.4 17.1 %all-gather.3.cloned.1.call-done.weights_hbm = bf16[1408,2560]{1,0:T(8,128)(2,1)} async-done(((bf16[88,2560]{1,0:T(8,128)(2,1)}), bf16[1408,2560]{1,0:T(8,128)(2,1)}) %all-gather.3.cloned.1.call-update) | async-done | bytes 7208976 | tf_op jit(solution)/shard_map/all_gather | solution.py:383
  104.5 5.8 %shard_map.101 = bf16[256,384]{1,0:T(8,128)(2,1)} custom-call(s32[4]{0:T(128)} %fusion.75.info, bf16[256,1408]{1,0:T(8,128)(2,1)} %slice.89.values, bf16[1408,2560]{1,0:T(8,128)(2,1)} %all-gather.3.cloned.1.call-done.weights_hbm), custom_call_target="tpu_custom_call" | custom-call | tf_op jit(solution)/shard_map/pallas_call | solution.py:172
  110.3 1.5 collective-permute-start.2
  111.9 5.8 %shard_map.100.own = bf16[256,384]{1,0:T(8,128)(2,1)} custom-call(s32[4]{0:T(128)} %bitcast.87, bf16[256,1408]{1,0:T(8,128)(2,1)} %slice.70.values, bf16[1408,2560]{1,0:T(8,128)(2,1)} %all-gather.3.cloned.1.call-done.weights_hbm), custom_call_target="tpu_custom_call" | custom-call | tf_op jit(solution)/shard_map/pallas_call | solution.py:172
  118.3 4.5 %shard_map.102 = (bf16[128,1408]{1,0:T(8,128)(2,1)}, bf16[128,1408]{1,0:T(8,128)(2,1)}) custom-call(s32[2]{0:T(128)} %pad_add_fusion.1.info, bf16[256,384]{1,0:T(8,128)(2,1)} %shard_map.100.own, bf16[256,384]{1,0:T(8,128)(2,1)} %copy-done.8, bf16[1408,2560]{1,0:T(8,128)(2,1)} %all-gather.3.cloned.1.call-done.weights_hbm), custom_call_target="tpu_custom_call" | custom-call | tf_op jit(solution)/shard_map/pallas_call | solution.py:209
  123.9 1.5 collective-permute-done.3.other
  126.2 4.4 %shard_map.103 = bf16[4,128,384]{2,1,0:T(8,128)(2,1)} custom-call(bf16[128,1408]{1,0:T(8,128)(2,1)} %bitcast.83, bf16[128,1408]{1,0:T(8,128)(2,1)} %get-tuple-element.20.keep, bf16[128,1408]{1,0:T(8,128)(2,1)} %copy-done.7, bf16[1408,1536]{1,0:T(8,128)(2,1)} %fusion.spread), custom_call_target="tpu_custom_call" | custom-call | tf_op jit(solution)/shard_map/pallas_call | solution.py:236
  130.6 6.2 %all-to-all-start.1 = ((bf16[4,128,384]{2,1,0:T(8,128)(2,1)}), bf16[4,128,384]{2,1,0:T(8,128)(2,1)S(1)}, u32[]{:S(2)}, u32[]{:S(2)}) async-start(bf16[4,128,384]{2,1,0:T(8,128)(2,1)} %shard_map.103), calls=%async_computation.1 | async-start | bytes 786432 | tf_op jit(solution)/shard_map/all_to_all | solution.py:426
  136.9 3.1 %collective-permute-start.8 = (bf16[3,64,1408]{2,1,0:T(8,128)(2,1)S(1)}, bf16[3,64,1408]{2,1,0:T(8,128)(2,1)S(1)}, u32[]{:S(2)}, u32[]{:S(2)}) collective-permute-start(bf16[3,64,1408]{2,1,0:T(8,128)(2,1)S(1)} %pad_maximum_fusion.1), channel_id=1, source_target_pairs={{0,8},{8,16},{16,24},{24,32},{32,40},{40,48},{48,56},{56,64},{64,7... | collective-permute-start | bytes 1622024 | tf_op jit(solution)/shard_map/ppermute | solution.py:411
  140.0 7.6 %all-to-all-done.1.mine = bf16[4,128,384]{2,1,0:T(8,128)(2,1)S(1)} async-done(((bf16[4,128,384]{2,1,0:T(8,128)(2,1)}), bf16[4,128,384]{2,1,0:T(8,128)(2,1)S(1)}, u32[]{:S(2)}, u32[]{:S(2)}) %all-to-all-start.1) | async-done | bytes 393248 | tf_op jit(solution)/shard_map/all_to_all | solution.py:426
  147.7 4.3 %collective-permute-start.4 = (bf16[4,128,384]{2,1,0:T(8,128)(2,1)S(1)}, bf16[4,128,384]{2,1,0:T(8,128)(2,1)S(1)}, u32[]{:S(2)}, u32[]{:S(2)}) collective-permute-start(bf16[4,128,384]{2,1,0:T(8,128)(2,1)S(1)} %all-to-all-done.1.mine), channel_id=1, source_target_pairs={{0,1},{1,0},{2,3},{3,2},{4,5},{5,4},{6,7},{7,6},{8,9},{9,8},{10,11... | collective-permute-start | bytes 1179656 | tf_op jit(solution)/shard_map/ppermute | solution.py:33
  154.1 4.5 %shard_map.104 = bf16[256,704]{1,0:T(8,128)(2,1)} custom-call(s32[2]{0:T(128)} %pad_add_fusion.1.info, bf16[4,128,384]{2,1,0:T(8,128)(2,1)} %copy-done.2, bf16[4,128,384]{2,1,0:T(8,128)(2,1)} %copy-done.5, bf16[1408,2560]{1,0:T(8,128)(2,1)} %all-gather.3.cloned.1.call-done.weights_hbm), custom_call_target="tpu_custom_call" | custom-call | tf_op jit(solution)/shard_map/pallas_call | solution.py:265
  158.6 3.5 %all-to-all-start.2 = ((bf16[4,64,704]{2,1,0:T(8,128)(2,1)}), bf16[4,64,704]{2,1,0:T(8,128)(2,1)S(1)}, u32[]{:S(2)}, u32[]{:S(2)}) async-start(bf16[4,64,704]{2,1,0:T(8,128)(2,1)} %bitcast.82), calls=%async_computation.2 | async-start | bytes 786432 | tf_op jit(solution)/shard_map/all_to_all | solution.py:429
  162.8 10.7 %all-to-all-done.2 = bf16[4,64,704]{2,1,0:T(8,128)(2,1)S(1)} async-done(((bf16[4,64,704]{2,1,0:T(8,128)(2,1)}), bf16[4,64,704]{2,1,0:T(8,128)(2,1)S(1)}, u32[]{:S(2)}, u32[]{:S(2)}) %all-to-all-start.2) | async-done | bytes 360480 | tf_op jit(solution)/shard_map/all_to_all | solution.py:429
  173.5 1.4 fusion.8
  174.8 9.2 %all-to-all-start.3 = ((bf16[64,8,768]{2,1,0:T(8,128)(2,1)}), bf16[64,8,768]{2,1,0:T(8,128)(2,1)S(1)}, u32[]{:S(2)}, u32[]{:S(2)}) async-start(bf16[64,8,768]{2,1,0:T(8,128)(2,1)} %fusion.8), calls=%async_computation.3 | async-start | bytes 1572864 | tf_op jit(solution)/shard_map/all_to_all | solution.py:435
  184.4 1.8 copy-done
  186.2 4.0 %convolution_convert_fusion.text = bf16[512,1408]{1,0:T(8,128)(2,1)} fusion(bf16[1408,1408]{1,0:T(8,128)(2,1)S(1)} %copy-done, bf16[128,1408]{1,0:T(8,128)(2,1)S(1)} %copy-done.6, bf16[384,1408]{1,0:T(8,128)(2,1)S(1)} %bitcast.84), kind=kOutput, calls=%fused_computation.4 | convolution fusion | flops 2033647616 | bytes 6848512 | tf_op jit(solution)/shard_map/dot_general | solution.py:37
  190.2 17.9 %all-to-all-done.3 = bf16[64,8,768]{2,1,0:T(8,128)(2,1)S(1)} async-done(((bf16[64,8,768]{2,1,0:T(8,128)(2,1)}), bf16[64,8,768]{2,1,0:T(8,128)(2,1)S(1)}, u32[]{:S(2)}, u32[]{:S(2)}) %all-to-all-start.3) | async-done | bytes 786464 | tf_op jit(solution)/shard_map/all_to_all | solution.py:435
  208.1 2.2 collective-permute-start.10
  213.1 16.0 %shard_map.105 = (bf16[64,1408]{1,0:T(8,128)(2,1)}, bf16[64,1408]{1,0:T(8,128)(2,1)}) custom-call(s32[4]{0:T(128)} %pad_add_fusion.info, bf16[512,768]{1,0:T(8,128)(2,1)} %bitcast.80, bf16[512,768]{1,0:T(8,128)(2,1)} %copy-done.3, bf16[512,1408]{1,0:T(8,128)(2,1)} %convolution_convert_fusion.text, bf16[1408,1408]{1,0:T(8,128)(2,1)} %fusion.1.reorder, ...), custom_call_target="tpu_custom_call" | custom-call | tf_op jit(solution)/shard_map/pallas_call | solution.py:283
  229.5 1.3 collective-permute-done.11
  230.8 1.6 add_convert_fusion
  (119 shorter events, 20.7 us)
Async XLA Ops:
  6.5 12.2 %copy-start.10 = (bf16[11,1,3,704]{3,2,1,0:T(4,128)(2,1)S(1)}, bf16[11,1,3,704]{3,2,1,0:T(4,128)(2,1)}, u32[]{:S(2)}) copy-start(bf16[11,1,3,704]{3,2,1,0:T(4,128)(2,1)} %param.18) | copy-start | bytes 139396
  6.5 12.3 %copy-start.11 = (bf16[704,11]{0,1:T(8,128)(2,1)S(1)}, bf16[704,11]{0,1:T(8,128)(2,1)}, u32[]{:S(2)}) copy-start(bf16[704,11]{0,1:T(8,128)(2,1)} %param.19) | copy-start | bytes 46468
  6.5 13.2 %copy-start.4 = (bf16[256,1408]{1,0:T(8,128)(2,1)S(1)}, bf16[256,1408]{1,0:T(8,128)(2,1)}, u32[]{:S(2)}) copy-start(bf16[256,1408]{1,0:T(8,128)(2,1)} %param.10) | copy-start | bytes 2162692
  9.7 20.9 %all-to-all-start = ((bf16[4,22,1760]{2,1,0:T(8,128)(2,1)}), bf16[4,22,1760]{2,1,0:T(8,128)(2,1)S(1)}, u32[]{:S(2)}, u32[]{:S(2)}) async-start(bf16[4,22,1760]{2,1,0:T(8,128)(2,1)} %broadcast_in_dim.15), calls=%async_computation | async-start | bytes 688128 | tf_op jit(solution)/shard_map/all_to_all | solution.py:57
  18.7 85.8 %all-gather.3.cloned.1.call-start = ((), (), s32[]{:S(2)}) async-start(), calls=%async_computation.4 | async-start | bytes 7659520 | tf_op jit(solution)/shard_map/all_gather | solution.py:383
  18.9 11.4 %collective-permute-start = (bf16[2,11,1408]{2,1,0:T(8,128)(2,1)S(1)}, bf16[2,11,1408]{2,1,0:T(8,128)(2,1)S(1)}, u32[]{:S(2)}, u32[]{:S(2)}) collective-permute-start(bf16[2,11,1408]{2,1,0:T(8,128)(2,1)S(1)} %pad_maximum_fusion.5), channel_id=1, source_target_pairs={{0,128},{128,0},{1,129},{129,1},{2,130},{130,2},{3,131},{131,3},{4... | collective-permute-start | bytes 185864 | tf_op jit(solution)/shard_map/ppermute | solution.py:340
  20.8 3.8 %copy-start.12 = (s32[4,1]{0,1:T(1,128)}, s32[4,1]{0,1:T(1,128)S(1)}, u32[]{:S(2)}) copy-start(s32[4,1]{0,1:T(1,128)S(1)} %reduce-window.15) | copy-start | bytes 52
  24.6 3.9 %copy-start.6 = (bf16[128,1408]{1,0:T(8,128)(2,1)S(1)}, bf16[128,1408]{1,0:T(8,128)(2,1)}, u32[]{:S(2)}) copy-start(bf16[128,1408]{1,0:T(8,128)(2,1)} %param.15) | copy-start | bytes 1081348
  29.3 0.9 copy-start.9
  31.7 179.5 %all-gather.5.cloned.1.call-start = ((), (), s32[]{:S(2)}) async-start(), calls=%async_computation.5 | async-start | bytes 8425472 | tf_op jit(solution)/shard_map/all_gather | solution.py:406
  31.7 34.6 %collective-permute-start.7 = (bf16[112,1408]{1,0:T(8,128)(2,1)S(1)}, bf16[112,1408]{1,0:T(8,128)(2,1)S(1)}, u32[]{:S(2)}, u32[]{:S(2)}) collective-permute-start(bf16[112,1408]{1,0:T(8,128)(2,1)S(1)} %maximum_maximum_fusion), channel_id=1, source_target_pairs={{0,2},{2,4},{4,6},{6,0},{1,3},{3,5},{5,7},{7,1},{8,10},{10,12},{12... | collective-permute-start | bytes 946184 | tf_op jit(solution)/shard_map/ppermute | solution.py:401
  34.2 32.1 %collective-permute-start.6 = (bf16[112,1408]{1,0:T(8,128)(2,1)S(1)}, bf16[112,1408]{1,0:T(8,128)(2,1)S(1)}, u32[]{:S(2)}, u32[]{:S(2)}) collective-permute-start(bf16[112,1408]{1,0:T(8,128)(2,1)S(1)} %maximum_maximum_fusion), channel_id=1, source_target_pairs={{0,4},{2,6},{4,0},{6,2},{1,5},{3,7},{5,1},{7,3},{8,12},{10,14},{12... | collective-permute-start | bytes 946184 | tf_op jit(solution)/shard_map/ppermute | solution.py:401
  37.5 28.8 %collective-permute-start.5 = (bf16[112,1408]{1,0:T(8,128)(2,1)S(1)}, bf16[112,1408]{1,0:T(8,128)(2,1)S(1)}, u32[]{:S(2)}, u32[]{:S(2)}) collective-permute-start(bf16[112,1408]{1,0:T(8,128)(2,1)S(1)} %maximum_maximum_fusion), channel_id=1, source_target_pairs={{0,6},{2,0},{4,2},{6,4},{1,7},{3,1},{5,3},{7,5},{8,14},{10,8},{12,... | collective-permute-start | bytes 946184 | tf_op jit(solution)/shard_map/ppermute | solution.py:401
  66.5 1.8 copy-start.14
  67.6 18.4 %collective-permute-start.1 = (bf16[272,1408]{1,0:T(8,128)(2,1)S(1)}, bf16[272,1408]{1,0:T(8,128)(2,1)S(1)}, u32[]{:S(2)}, u32[]{:S(2)}) collective-permute-start(bf16[272,1408]{1,0:T(8,128)(2,1)S(1)} %fusion.9), channel_id=1, source_target_pairs={{0,128},{128,0},{1,129},{129,1},{2,130},{130,2},{3,131},{131,3},{4... | collective-permute-start | bytes 2297864 | tf_op jit(solution)/shard_map/ppermute | solution.py:419
  110.3 7.3 %collective-permute-start.2 = (bf16[256,384]{1,0:T(8,128)(2,1)}, bf16[256,384]{1,0:T(8,128)(2,1)S(1)}, u32[]{:S(2)}, u32[]{:S(2)}) collective-permute-start(bf16[256,384]{1,0:T(8,128)(2,1)} %shard_map.101), channel_id=1, source_target_pairs={{0,128},{128,0},{1,129},{129,1},{2,130},{130,2},{3,131},{131,3},{4... | collective-permute-start | bytes 589832 | tf_op jit(solution)/shard_map/ppermute | solution.py:423
  122.8 2.6 %collective-permute-start.3 = (bf16[128,1408]{1,0:T(8,128)(2,1)}, bf16[128,1408]{1,0:T(8,128)(2,1)S(1)}, u32[]{:S(2)}, u32[]{:S(2)}) collective-permute-start(bf16[128,1408]{1,0:T(8,128)(2,1)} %get-tuple-element.21), channel_id=1, source_target_pairs={{0,1},{1,0},{2,3},{3,2},{4,5},{5,4},{6,7},{7,6},{8,9},{9,8},{10,11... | collective-permute-start | bytes 1081352 | tf_op jit(solution)/shard_map/ppermute | solution.py:33
  125.4 0.7 copy-start.7
  130.6 17.1 %all-to-all-start.1 = ((bf16[4,128,384]{2,1,0:T(8,128)(2,1)}), bf16[4,128,384]{2,1,0:T(8,128)(2,1)S(1)}, u32[]{:S(2)}, u32[]{:S(2)}) async-start(bf16[4,128,384]{2,1,0:T(8,128)(2,1)} %shard_map.103), calls=%async_computation.1 | async-start | bytes 786432 | tf_op jit(solution)/shard_map/all_to_all | solution.py:426
  136.9 25.2 %collective-permute-start.8 = (bf16[3,64,1408]{2,1,0:T(8,128)(2,1)S(1)}, bf16[3,64,1408]{2,1,0:T(8,128)(2,1)S(1)}, u32[]{:S(2)}, u32[]{:S(2)}) collective-permute-start(bf16[3,64,1408]{2,1,0:T(8,128)(2,1)S(1)} %pad_maximum_fusion.1), channel_id=1, source_target_pairs={{0,8},{8,16},{16,24},{24,32},{32,40},{40,48},{48,56},{56,64},{64,7... | collective-permute-start | bytes 1622024 | tf_op jit(solution)/shard_map/ppermute | solution.py:411
  147.7 5.7 %copy-start.2 = (bf16[4,128,384]{2,1,0:T(8,128)(2,1)}, bf16[4,128,384]{2,1,0:T(8,128)(2,1)S(1)}, u32[]{:S(2)}) copy-start(bf16[4,128,384]{2,1,0:T(8,128)(2,1)S(1)} %all-to-all-done.1.mine) | copy-start | bytes 1179652
  147.7 5.7 %collective-permute-start.4 = (bf16[4,128,384]{2,1,0:T(8,128)(2,1)S(1)}, bf16[4,128,384]{2,1,0:T(8,128)(2,1)S(1)}, u32[]{:S(2)}, u32[]{:S(2)}) collective-permute-start(bf16[4,128,384]{2,1,0:T(8,128)(2,1)S(1)} %all-to-all-done.1.mine), channel_id=1, source_target_pairs={{0,1},{1,0},{2,3},{3,2},{4,5},{5,4},{6,7},{7,6},{8,9},{9,8},{10,11... | collective-permute-start | bytes 1179656 | tf_op jit(solution)/shard_map/ppermute | solution.py:33
  153.4 0.7 copy-start.5
  158.6 14.8 %all-to-all-start.2 = ((bf16[4,64,704]{2,1,0:T(8,128)(2,1)}), bf16[4,64,704]{2,1,0:T(8,128)(2,1)S(1)}, u32[]{:S(2)}, u32[]{:S(2)}) async-start(bf16[4,64,704]{2,1,0:T(8,128)(2,1)} %bitcast.82), calls=%async_computation.2 | async-start | bytes 786432 | tf_op jit(solution)/shard_map/all_to_all | solution.py:429
  162.3 21.8 %collective-permute-start.9 = (bf16[3,64,1408]{2,1,0:T(8,128)(2,1)S(1)}, bf16[3,64,1408]{2,1,0:T(8,128)(2,1)S(1)}, u32[]{:S(2)}, u32[]{:S(2)}) collective-permute-start(bf16[3,64,1408]{2,1,0:T(8,128)(2,1)S(1)} %broadcast_select_fusion), channel_id=1, source_target_pairs={{0,1},{1,0},{2,3},{3,2},{4,5},{5,4},{6,7},{7,6},{8,9},{9,8},{10,11... | collective-permute-start | bytes 1622024 | tf_op jit(solution)/shard_map/ppermute | solution.py:33
  174.8 33.2 %all-to-all-start.3 = ((bf16[64,8,768]{2,1,0:T(8,128)(2,1)}), bf16[64,8,768]{2,1,0:T(8,128)(2,1)S(1)}, u32[]{:S(2)}, u32[]{:S(2)}) async-start(bf16[64,8,768]{2,1,0:T(8,128)(2,1)} %fusion.8), calls=%async_computation.3 | async-start | bytes 1572864 | tf_op jit(solution)/shard_map/all_to_all | solution.py:435
  184.1 2.1 copy-start
  186.2 24.1 %copy-start.15 = (s32[1,2]{1,0:T(1,128)S(1)}, s32[1,2]{1,0:T(1,128)}, u32[]{:S(2)}) copy-start(s32[1,2]{1,0:T(1,128)} %param.17) | copy-start | bytes 28
  208.1 4.1 %copy-start.1 = (bf16[64,8,768]{2,1,0:T(8,128)(2,1)}, bf16[64,8,768]{2,1,0:T(8,128)(2,1)S(1)}, u32[]{:S(2)}) copy-start(bf16[64,8,768]{2,1,0:T(8,128)(2,1)S(1)} %all-to-all-done.3) | copy-start | bytes 2359300
  208.1 4.1 %collective-permute-start.10 = (bf16[512,768]{1,0:T(8,128)(2,1)S(1)}, bf16[512,768]{1,0:T(8,128)(2,1)S(1)}, u32[]{:S(2)}, u32[]{:S(2)}) collective-permute-start(bf16[512,768]{1,0:T(8,128)(2,1)S(1)} %bitcast.79), channel_id=1, source_target_pairs={{0,1},{1,0},{2,3},{3,2},{4,5},{5,4},{6,7},{7,6},{8,9},{9,8},{10,11... | collective-permute-start | bytes 2359304 | tf_op jit(solution)/shard_map/ppermute | solution.py:33
  212.2 0.9 copy-start.3
  229.1 1.7 collective-permute-start.11
  (2 other events, 1.4 us)
Sparse Core Ops, SparseCore 0:
  31.8 72.6 all-gather.2
  107.0 80.4 all-gather.4

commit v9 on v8

--- a/solution.py
+++ b/solution.py
@@ -222,24 +222,33 @@
     )(info, own, other, weights)
 
 
-def merger_rows(patches, keep, other, spread, out):
+def merger_rows(piece, patches, keep, other, out, ordered):
     hidden = patches[...].astype(F32) + (keep[...].astype(F32) + other[...].astype(F32))
-    ready = dot(layer_norm(hidden).astype(BF), spread[...]).astype(BF)
-    columns = out.shape[2]
-    for place in range(out.shape[0]):
-        out[place] = ready[:, place * columns : (place + 1) * columns]
-
-
-def run_merger_rows(lines, patches, keep, other, spread):
-    rows = patches.shape[0]
+    ready = layer_norm(hidden)
+    lines = out.shape[0]
+    count = ready.shape[1] // (lines * piece)
+    ordered[...] = jnp.zeros(ordered.shape, F32)
+    for place in range(lines):
+        for part in range(count):
+            source = (part * lines + place) * piece
+            ordered[place, :, part * piece : (part + 1) * piece] = ready[
+                :, source : source + piece
+            ]
+    out[...] = ordered[...].astype(BF)
+
+
+def run_merger_rows(lines, piece, patches, keep, other):
+    rows, width = patches.shape
+    shape = (lines, rows, width // lines + pad_to(width // lines))
     vmem = pl.BlockSpec(memory_space=pltpu.VMEM)
     return pl.pallas_call(
-        merger_rows,
-        out_shape=jax.ShapeDtypeStruct((lines, rows, spread.shape[1] // lines), BF),
-        in_specs=[vmem] * 4,
+        functools.partial(merger_rows, piece),
+        out_shape=jax.ShapeDtypeStruct(shape, BF),
+        in_specs=[vmem] * 3,
         out_specs=vmem,
+        scratch_shapes=[pltpu.VMEM(shape, F32)],
         compiler_params=pltpu.CompilerParams(vmem_limit_bytes=56 << 20),
-    )(patches, keep, other, spread)
+    )(patches, keep, other)
 
 
 def merger_dot(depth, info, mine, theirs, weights_hbm, out, weights, sem):
@@ -351,12 +360,6 @@
     mark = jnp.pad(ends.astype(BF)[None], ((0, 15), (0, width - ends.shape[0])))
     marked = jnp.concatenate([normed, mark], axis=0)
     depth = 4 * mrows
-    spread_at = jnp.arange(lines * (depth + pad_to(depth)), dtype=jnp.int32)
-    inner = spread_at % (depth + pad_to(depth))
-    source = inner // mrows * (lines * mrows) + inner % mrows
-    source = source + spread_at // (depth + pad_to(depth)) * mrows
-    source = jnp.where(inner < depth, source, width)
-    spread = (jnp.arange(width, dtype=jnp.int32)[:, None] == source[None, :]).astype(BF)
     me = lax.axis_index("zh")
     order = jnp.arange(width, dtype=jnp.int32)
     fan = 2 * drows
@@ -377,8 +380,8 @@
         ],
         axis=0,
     )
-    line_v, marked, reorder, mine, spread, own_patches = lax.optimization_barrier(
-        (line_v, marked, reorder, mine, spread, own_patches)
+    line_v, marked, reorder, mine, own_patches = lax.optimization_barrier(
+        (line_v, marked, reorder, mine, own_patches)
     )
     full_v = lax.all_gather(line_v, PLANE, axis=0, tiled=True)
 
@@ -422,7 +425,7 @@
     heads = run_vision_block(at_in, part, ends, marked[:rows_v], full_v)
     heads_back = lax.ppermute(heads_away, "grp", pair)
     keep, give = run_vision_output(at_out, part, place_info, heads, heads_back, full_v)
-    merged = run_merger_rows(lines, own_patches, keep, swap_sub(give), spread)
+    merged = run_merger_rows(lines, mrows, own_patches, keep, swap_sub(give))
     merged = lax.all_to_all(merged, "zh", split_axis=0, concat_axis=0, tiled=True)
     partial = run_merger_dot(half, depth, place_info, merged, swap_sub(merged), full_v)
     partial = partial.reshape(lines, tokens, half)

time: 240 us -> 237 us (0.988)
  other arithmetic: 15.4 us -> 11.4 us
  waiting for transfers between devices: 100 us -> 103 us
    convert_element_type x1 -> x0, other arithmetic: 3.9 us -> none  [shards(): (jnp.arange(width, dtype=jnp.int32)[:, None] == source[None, :]).astype(BF)]
  transfers between devices with their start and end apart: 18 -> 18, of which waited for: 10 -> 11; matrix products, arithmetic and copies ran while one was open for 9% -> 8% of each run, Pallas kernels for 10% -> 10%
where the time goes in v9:
time: 237 us; the launch traced here: 236 us
  waiting for transfers between devices  103 us (43%)
  starting transfers between devices  51.5 us (22%)
  Pallas kernels  39.2 us (17%)
  between operations  13.8 us (6%)
  local copies, waits for them, and re-layouts  12.4 us (5%)
  other arithmetic  11.4 us (5%)
  matrix products  5.32 us (2%)
    ppermute x3, waiting for transfers between devices, shards(): lax.ppermute(mine, 'zh', [(i, (i + s) % lines) for i in range(lines)])  25.4 us
    all_gather x1, waiting for transfers between devices, shards(): full_v = lax.all_gather(line_v, PLANE, axis=0, tiled=True)  18.7 us
    all_to_all x1, waiting for transfers between devices, shards(): lax.all_to_all(sent.reshape(pieces, slots, half + pad_to(half)), TOK, spl...  17.8 us
    ppermute x1, waiting for transfers between devices, shards(): paired = lax.ppermute(marked, 'grp', pair)  16.1 us
    pallas_call x1, Pallas kernels, run_decoder_block(): pl.pallas_call(functools.partial(decoder_block, half, cap), out_shape=[ja...  15.9 us
    pallas_call x2, Pallas kernels, run_vision_block(): pl.pallas_call(functools.partial(vision_block, at, part), out_shape=jax.S...  11.5 us
    all_to_all x1, starting transfers between devices, shards(): lax.all_to_all(sent.reshape(pieces, slots, half + pad_to(half)), TOK, spl...  11.3 us
    all_to_all x1, waiting for transfers between devices, shards(): lax.all_to_all(partial, 'zh', split_axis=0, concat_axis=0, tiled=True)  9.95 us
  transfers between devices with their start and end apart: 18, of which 11 were waited for; matrix products, arithmetic and copies ran while one was open for 8% of the time, Pallas kernels for 10%

profile of v9, /device:TPU:1, one launch (start us, length us, event | category | flops | bytes accessed | tf_op | source)
XLA Modules:
  0.0 236.4 jit_solution(4355185871895543687)
XLA Ops:
  6.5 1.2 reshape.317
  9.7 9.0 %all-to-all-start = ((bf16[4,22,1760]{2,1,0:T(8,128)(2,1)}), bf16[4,22,1760]{2,1,0:T(8,128)(2,1)S(1)}, u32[]{:S(2)}, u32[]{:S(2)}) async-start(bf16[4,22,1760]{2,1,0:T(8,128)(2,1)} %broadcast_in_dim.11), calls=%async_computation | async-start | bytes 688128 | tf_op jit(solution)/shard_map/all_to_all | solution.py:57
  20.9 3.6 %fusion.reorder = bf16[1408,1408]{1,0:T(8,128)(2,1)} fusion(s32[1408]{0:T(1024)S(1)} %fusion.31), kind=kLoop, calls=%fused_computation.1 | loop fusion | flops 3964928 | bytes 3970560 | tf_op jit(solution)/shard_map/convert_element_type | solution.py:372
  26.4 2.1 collective-permute-done
  29.9 1.5 collective-permute-start.7
  31.4 4.4 %collective-permute-start.6 = (bf16[112,1408]{1,0:T(8,128)(2,1)S(1)}, bf16[112,1408]{1,0:T(8,128)(2,1)S(1)}, u32[]{:S(2)}, u32[]{:S(2)}) collective-permute-start(bf16[112,1408]{1,0:T(8,128)(2,1)S(1)} %maximum_maximum_fusion), channel_id=1, source_target_pairs={{0,4},{2,6},{4,0},{6,2},{1,5},{3,7},{5,1},{7,3},{8,12},{10,14},{12... | collective-permute-start | bytes 946184 | tf_op jit(solution)/shard_map/ppermute | solution.py:404
  35.8 2.5 %collective-permute-start.5 = (bf16[112,1408]{1,0:T(8,128)(2,1)S(1)}, bf16[112,1408]{1,0:T(8,128)(2,1)S(1)}, u32[]{:S(2)}, u32[]{:S(2)}) collective-permute-start(bf16[112,1408]{1,0:T(8,128)(2,1)S(1)} %maximum_maximum_fusion), channel_id=1, source_target_pairs={{0,6},{2,0},{4,2},{6,4},{1,7},{3,1},{5,3},{7,5},{8,14},{10,8},{12,... | collective-permute-start | bytes 946184 | tf_op jit(solution)/shard_map/ppermute | solution.py:404
  38.3 25.4 %collective-permute-done.5 = bf16[112,1408]{1,0:T(8,128)(2,1)S(1)} collective-permute-done((bf16[112,1408]{1,0:T(8,128)(2,1)S(1)}, bf16[112,1408]{1,0:T(8,128)(2,1)S(1)}, u32[]{:S(2)}, u32[]{:S(2)}) %collective-permute-start.5) | collective-permute-done | bytes 315424 | tf_op jit(solution)/shard_map/ppermute | solution.py:404
  66.7 16.1 %collective-permute-done.1 = bf16[272,1408]{1,0:T(8,128)(2,1)S(1)} collective-permute-done((bf16[272,1408]{1,0:T(8,128)(2,1)S(1)}, bf16[272,1408]{1,0:T(8,128)(2,1)S(1)}, u32[]{:S(2)}, u32[]{:S(2)}) %collective-permute-start.1) | collective-permute-done | bytes 765984 | tf_op jit(solution)/shard_map/ppermute | solution.py:422
  84.2 18.7 %all-gather.3.cloned.1.call-done.weights_hbm = bf16[1408,2560]{1,0:T(8,128)(2,1)} async-done(((bf16[88,2560]{1,0:T(8,128)(2,1)}), bf16[1408,2560]{1,0:T(8,128)(2,1)}) %all-gather.3.cloned.1.call-update) | async-done | bytes 7208976 | tf_op jit(solution)/shard_map/all_gather | solution.py:386
  102.8 5.8 %shard_map.101 = bf16[256,384]{1,0:T(8,128)(2,1)} custom-call(s32[4]{0:T(128)} %fusion.53.info, bf16[256,1408]{1,0:T(8,128)(2,1)} %slice.89.values, bf16[1408,2560]{1,0:T(8,128)(2,1)} %all-gather.3.cloned.1.call-done.weights_hbm), custom_call_target="tpu_custom_call" | custom-call | tf_op jit(solution)/shard_map/pallas_call | solution.py:172
  108.6 1.5 collective-permute-start.2
  110.1 5.8 %shard_map.100.own = bf16[256,384]{1,0:T(8,128)(2,1)} custom-call(s32[4]{0:T(128)} %bitcast.87, bf16[256,1408]{1,0:T(8,128)(2,1)} %slice.70.values, bf16[1408,2560]{1,0:T(8,128)(2,1)} %all-gather.3.cloned.1.call-done.weights_hbm), custom_call_target="tpu_custom_call" | custom-call | tf_op jit(solution)/shard_map/pallas_call | solution.py:172
  116.6 4.5 %shard_map.102 = (bf16[128,1408]{1,0:T(8,128)(2,1)}, bf16[128,1408]{1,0:T(8,128)(2,1)}) custom-call(s32[2]{0:T(128)} %pad_add_fusion.1.info, bf16[256,384]{1,0:T(8,128)(2,1)} %shard_map.100.own, bf16[256,384]{1,0:T(8,128)(2,1)} %copy-done.8, bf16[1408,2560]{1,0:T(8,128)(2,1)} %all-gather.3.cloned.1.call-done.weights_hbm), custom_call_target="tpu_custom_call" | custom-call | tf_op jit(solution)/shard_map/pallas_call | solution.py:209
  122.2 1.5 collective-permute-done.3.other
  124.5 2.8 %shard_map.103 = bf16[4,128,384]{2,1,0:T(8,128)(2,1)} custom-call(bf16[128,1408]{1,0:T(8,128)(2,1)} %bitcast.83, bf16[128,1408]{1,0:T(8,128)(2,1)} %get-tuple-element.19.keep, bf16[128,1408]{1,0:T(8,128)(2,1)} %copy-done.7), custom_call_target="tpu_custom_call" | custom-call | tf_op jit(solution)/shard_map/pallas_call | solution.py:244
  127.3 6.2 %all-to-all-start.1 = ((bf16[4,128,384]{2,1,0:T(8,128)(2,1)}), bf16[4,128,384]{2,1,0:T(8,128)(2,1)S(1)}, u32[]{:S(2)}, u32[]{:S(2)}) async-start(bf16[4,128,384]{2,1,0:T(8,128)(2,1)} %shard_map.103), calls=%async_computation.1 | async-start | bytes 786432 | tf_op jit(solution)/shard_map/all_to_all | solution.py:429
  133.6 3.1 %collective-permute-start.8 = (bf16[3,64,1408]{2,1,0:T(8,128)(2,1)S(1)}, bf16[3,64,1408]{2,1,0:T(8,128)(2,1)S(1)}, u32[]{:S(2)}, u32[]{:S(2)}) collective-permute-start(bf16[3,64,1408]{2,1,0:T(8,128)(2,1)S(1)} %pad_maximum_fusion.1), channel_id=1, source_target_pairs={{0,8},{8,16},{16,24},{24,32},{32,40},{40,48},{48,56},{56,64},{64,7... | collective-permute-start | bytes 1622024 | tf_op jit(solution)/shard_map/ppermute | solution.py:414
  136.7 7.9 %all-to-all-done.1.mine = bf16[4,128,384]{2,1,0:T(8,128)(2,1)S(1)} async-done(((bf16[4,128,384]{2,1,0:T(8,128)(2,1)}), bf16[4,128,384]{2,1,0:T(8,128)(2,1)S(1)}, u32[]{:S(2)}, u32[]{:S(2)}) %all-to-all-start.1) | async-done | bytes 393248 | tf_op jit(solution)/shard_map/all_to_all | solution.py:429
  144.6 3.0 %collective-permute-start.4 = (bf16[4,128,384]{2,1,0:T(8,128)(2,1)S(1)}, bf16[4,128,384]{2,1,0:T(8,128)(2,1)S(1)}, u32[]{:S(2)}, u32[]{:S(2)}) collective-permute-start(bf16[4,128,384]{2,1,0:T(8,128)(2,1)S(1)} %all-to-all-done.1.mine), channel_id=1, source_target_pairs={{0,1},{1,0},{2,3},{3,2},{4,5},{5,4},{6,7},{7,6},{8,9},{9,8},{10,11... | collective-permute-start | bytes 1179656 | tf_op jit(solution)/shard_map/ppermute | solution.py:33
  149.7 4.5 %shard_map.104 = bf16[256,704]{1,0:T(8,128)(2,1)} custom-call(s32[2]{0:T(128)} %pad_add_fusion.1.info, bf16[4,128,384]{2,1,0:T(8,128)(2,1)} %copy-done.2, bf16[4,128,384]{2,1,0:T(8,128)(2,1)} %copy-done.5, bf16[1408,2560]{1,0:T(8,128)(2,1)} %all-gather.3.cloned.1.call-done.weights_hbm), custom_call_target="tpu_custom_call" | custom-call | tf_op jit(solution)/shard_map/pallas_call | solution.py:274
  154.2 3.5 %all-to-all-start.2 = ((bf16[4,64,704]{2,1,0:T(8,128)(2,1)}), bf16[4,64,704]{2,1,0:T(8,128)(2,1)S(1)}, u32[]{:S(2)}, u32[]{:S(2)}) async-start(bf16[4,64,704]{2,1,0:T(8,128)(2,1)} %bitcast.82), calls=%async_computation.2 | async-start | bytes 786432 | tf_op jit(solution)/shard_map/all_to_all | solution.py:432
  158.3 10.0 %all-to-all-done.2 = bf16[4,64,704]{2,1,0:T(8,128)(2,1)S(1)} async-done(((bf16[4,64,704]{2,1,0:T(8,128)(2,1)}), bf16[4,64,704]{2,1,0:T(8,128)(2,1)S(1)}, u32[]{:S(2)}, u32[]{:S(2)}) %all-to-all-start.2) | async-done | bytes 360480 | tf_op jit(solution)/shard_map/all_to_all | solution.py:432
  168.3 1.4 fusion.7
  169.7 11.3 %all-to-all-start.3 = ((bf16[64,8,768]{2,1,0:T(8,128)(2,1)}), bf16[64,8,768]{2,1,0:T(8,128)(2,1)S(1)}, u32[]{:S(2)}, u32[]{:S(2)}) async-start(bf16[64,8,768]{2,1,0:T(8,128)(2,1)} %fusion.7), calls=%async_computation.3 | async-start | bytes 1572864 | tf_op jit(solution)/shard_map/all_to_all | solution.py:438
  181.3 1.8 copy-done
  183.2 4.0 %convolution_convert_fusion.text = bf16[512,1408]{1,0:T(8,128)(2,1)} fusion(bf16[1408,1408]{1,0:T(8,128)(2,1)S(1)} %copy-done, bf16[128,1408]{1,0:T(8,128)(2,1)S(1)} %copy-done.6, bf16[384,1408]{1,0:T(8,128)(2,1)S(1)} %bitcast.84), kind=kOutput, calls=%fused_computation.2 | convolution fusion | flops 2033647616 | bytes 6848512 | tf_op jit(solution)/shard_map/dot_general | solution.py:37
  187.1 17.8 %all-to-all-done.3 = bf16[64,8,768]{2,1,0:T(8,128)(2,1)S(1)} async-done(((bf16[64,8,768]{2,1,0:T(8,128)(2,1)}), bf16[64,8,768]{2,1,0:T(8,128)(2,1)S(1)}, u32[]{:S(2)}, u32[]{:S(2)}) %all-to-all-start.3) | async-done | bytes 786464 | tf_op jit(solution)/shard_map/all_to_all | solution.py:438
  204.9 2.5 %collective-permute-start.10 = (bf16[512,768]{1,0:T(8,128)(2,1)S(1)}, bf16[512,768]{1,0:T(8,128)(2,1)S(1)}, u32[]{:S(2)}, u32[]{:S(2)}) collective-permute-start(bf16[512,768]{1,0:T(8,128)(2,1)S(1)} %bitcast.79), channel_id=1, source_target_pairs={{0,1},{1,0},{2,3},{3,2},{4,5},{5,4},{6,7},{7,6},{8,9},{9,8},{10,11... | collective-permute-start | bytes 2359304 | tf_op jit(solution)/shard_map/ppermute | solution.py:33
  210.2 15.9 %shard_map.105 = (bf16[64,1408]{1,0:T(8,128)(2,1)}, bf16[64,1408]{1,0:T(8,128)(2,1)}) custom-call(s32[4]{0:T(128)} %pad_add_fusion.info, bf16[512,768]{1,0:T(8,128)(2,1)} %bitcast.80, bf16[512,768]{1,0:T(8,128)(2,1)} %copy-done.3, bf16[512,1408]{1,0:T(8,128)(2,1)} %convolution_convert_fusion.text, bf16[1408,1408]{1,0:T(8,128)(2,1)} %fusion.reorder, ...), custom_call_target="tpu_custom_call" | custom-call | tf_op jit(solution)/shard_map/pallas_call | solution.py:292
  226.6 1.3 collective-permute-done.11
  227.9 1.6 add_convert_fusion
  (117 shorter events, 20.6 us)
Async XLA Ops:
  6.5 12.2 %copy-start.10 = (bf16[11,1,3,704]{3,2,1,0:T(4,128)(2,1)S(1)}, bf16[11,1,3,704]{3,2,1,0:T(4,128)(2,1)}, u32[]{:S(2)}) copy-start(bf16[11,1,3,704]{3,2,1,0:T(4,128)(2,1)} %param.18) | copy-start | bytes 139396
  6.5 12.3 %copy-start.11 = (bf16[704,11]{0,1:T(8,128)(2,1)S(1)}, bf16[704,11]{0,1:T(8,128)(2,1)}, u32[]{:S(2)}) copy-start(bf16[704,11]{0,1:T(8,128)(2,1)} %param.19) | copy-start | bytes 46468
  6.5 13.2 %copy-start.4 = (bf16[256,1408]{1,0:T(8,128)(2,1)S(1)}, bf16[256,1408]{1,0:T(8,128)(2,1)}, u32[]{:S(2)}) copy-start(bf16[256,1408]{1,0:T(8,128)(2,1)} %param.10) | copy-start | bytes 2162692
  9.7 19.1 %all-to-all-start = ((bf16[4,22,1760]{2,1,0:T(8,128)(2,1)}), bf16[4,22,1760]{2,1,0:T(8,128)(2,1)S(1)}, u32[]{:S(2)}, u32[]{:S(2)}) async-start(bf16[4,22,1760]{2,1,0:T(8,128)(2,1)} %broadcast_in_dim.11), calls=%async_computation | async-start | bytes 688128 | tf_op jit(solution)/shard_map/all_to_all | solution.py:57
  18.7 84.1 %all-gather.3.cloned.1.call-start = ((), (), s32[]{:S(2)}) async-start(), calls=%async_computation.4 | async-start | bytes 7659520 | tf_op jit(solution)/shard_map/all_gather | solution.py:386
  19.0 9.5 %collective-permute-start = (bf16[2,11,1408]{2,1,0:T(8,128)(2,1)S(1)}, bf16[2,11,1408]{2,1,0:T(8,128)(2,1)S(1)}, u32[]{:S(2)}, u32[]{:S(2)}) collective-permute-start(bf16[2,11,1408]{2,1,0:T(8,128)(2,1)S(1)} %pad_maximum_fusion.5), channel_id=1, source_target_pairs={{0,128},{128,0},{1,129},{129,1},{2,130},{130,2},{3,131},{131,3},{4... | collective-permute-start | bytes 185864 | tf_op jit(solution)/shard_map/ppermute | solution.py:349
  20.8 3.7 %copy-start.12 = (s32[4,1]{0,1:T(1,128)}, s32[4,1]{0,1:T(1,128)S(1)}, u32[]{:S(2)}) copy-start(s32[4,1]{0,1:T(1,128)S(1)} %reduce-window.15) | copy-start | bytes 52
  20.9 3.6 %copy-start.6 = (bf16[128,1408]{1,0:T(8,128)(2,1)S(1)}, bf16[128,1408]{1,0:T(8,128)(2,1)}, u32[]{:S(2)}) copy-start(bf16[128,1408]{1,0:T(8,128)(2,1)} %param.15) | copy-start | bytes 1081348
  25.3 0.9 copy-start.9
  29.9 178.4 %all-gather.5.cloned.1.call-start = ((), (), s32[]{:S(2)}) async-start(), calls=%async_computation.5 | async-start | bytes 8425472 | tf_op jit(solution)/shard_map/all_gather | solution.py:409
  29.9 33.8 %collective-permute-start.7 = (bf16[112,1408]{1,0:T(8,128)(2,1)S(1)}, bf16[112,1408]{1,0:T(8,128)(2,1)S(1)}, u32[]{:S(2)}, u32[]{:S(2)}) collective-permute-start(bf16[112,1408]{1,0:T(8,128)(2,1)S(1)} %maximum_maximum_fusion), channel_id=1, source_target_pairs={{0,2},{2,4},{4,6},{6,0},{1,3},{3,5},{5,7},{7,1},{8,10},{10,12},{12... | collective-permute-start | bytes 946184 | tf_op jit(solution)/shard_map/ppermute | solution.py:404
  31.4 32.3 %collective-permute-start.6 = (bf16[112,1408]{1,0:T(8,128)(2,1)S(1)}, bf16[112,1408]{1,0:T(8,128)(2,1)S(1)}, u32[]{:S(2)}, u32[]{:S(2)}) collective-permute-start(bf16[112,1408]{1,0:T(8,128)(2,1)S(1)} %maximum_maximum_fusion), channel_id=1, source_target_pairs={{0,4},{2,6},{4,0},{6,2},{1,5},{3,7},{5,1},{7,3},{8,12},{10,14},{12... | collective-permute-start | bytes 946184 | tf_op jit(solution)/shard_map/ppermute | solution.py:404
  35.8 27.8 %collective-permute-start.5 = (bf16[112,1408]{1,0:T(8,128)(2,1)S(1)}, bf16[112,1408]{1,0:T(8,128)(2,1)S(1)}, u32[]{:S(2)}, u32[]{:S(2)}) collective-permute-start(bf16[112,1408]{1,0:T(8,128)(2,1)S(1)} %maximum_maximum_fusion), channel_id=1, source_target_pairs={{0,6},{2,0},{4,2},{6,4},{1,7},{3,1},{5,3},{7,5},{8,14},{10,8},{12,... | collective-permute-start | bytes 946184 | tf_op jit(solution)/shard_map/ppermute | solution.py:404
  63.9 1.7 copy-start.14
  64.9 17.8 %collective-permute-start.1 = (bf16[272,1408]{1,0:T(8,128)(2,1)S(1)}, bf16[272,1408]{1,0:T(8,128)(2,1)S(1)}, u32[]{:S(2)}, u32[]{:S(2)}) collective-permute-start(bf16[272,1408]{1,0:T(8,128)(2,1)S(1)} %fusion.8), channel_id=1, source_target_pairs={{0,128},{128,0},{1,129},{129,1},{2,130},{130,2},{3,131},{131,3},{4... | collective-permute-start | bytes 2297864 | tf_op jit(solution)/shard_map/ppermute | solution.py:422
  108.6 7.3 %collective-permute-start.2 = (bf16[256,384]{1,0:T(8,128)(2,1)}, bf16[256,384]{1,0:T(8,128)(2,1)S(1)}, u32[]{:S(2)}, u32[]{:S(2)}) collective-permute-start(bf16[256,384]{1,0:T(8,128)(2,1)} %shard_map.101), channel_id=1, source_target_pairs={{0,128},{128,0},{1,129},{129,1},{2,130},{130,2},{3,131},{131,3},{4... | collective-permute-start | bytes 589832 | tf_op jit(solution)/shard_map/ppermute | solution.py:426
  121.1 2.6 %collective-permute-start.3 = (bf16[128,1408]{1,0:T(8,128)(2,1)}, bf16[128,1408]{1,0:T(8,128)(2,1)S(1)}, u32[]{:S(2)}, u32[]{:S(2)}) collective-permute-start(bf16[128,1408]{1,0:T(8,128)(2,1)} %get-tuple-element.20), channel_id=1, source_target_pairs={{0,1},{1,0},{2,3},{3,2},{4,5},{5,4},{6,7},{7,6},{8,9},{9,8},{10,11... | collective-permute-start | bytes 1081352 | tf_op jit(solution)/shard_map/ppermute | solution.py:33
  123.7 0.7 copy-start.7
  127.3 17.3 %all-to-all-start.1 = ((bf16[4,128,384]{2,1,0:T(8,128)(2,1)}), bf16[4,128,384]{2,1,0:T(8,128)(2,1)S(1)}, u32[]{:S(2)}, u32[]{:S(2)}) async-start(bf16[4,128,384]{2,1,0:T(8,128)(2,1)} %shard_map.103), calls=%async_computation.1 | async-start | bytes 786432 | tf_op jit(solution)/shard_map/all_to_all | solution.py:429
  133.6 24.1 %collective-permute-start.8 = (bf16[3,64,1408]{2,1,0:T(8,128)(2,1)S(1)}, bf16[3,64,1408]{2,1,0:T(8,128)(2,1)S(1)}, u32[]{:S(2)}, u32[]{:S(2)}) collective-permute-start(bf16[3,64,1408]{2,1,0:T(8,128)(2,1)S(1)} %pad_maximum_fusion.1), channel_id=1, source_target_pairs={{0,8},{8,16},{16,24},{24,32},{32,40},{40,48},{48,56},{56,64},{64,7... | collective-permute-start | bytes 1622024 | tf_op jit(solution)/shard_map/ppermute | solution.py:414
  144.6 4.4 %copy-start.2 = (bf16[4,128,384]{2,1,0:T(8,128)(2,1)}, bf16[4,128,384]{2,1,0:T(8,128)(2,1)S(1)}, u32[]{:S(2)}) copy-start(bf16[4,128,384]{2,1,0:T(8,128)(2,1)S(1)} %all-to-all-done.1.mine) | copy-start | bytes 1179652
  144.6 4.4 %collective-permute-start.4 = (bf16[4,128,384]{2,1,0:T(8,128)(2,1)S(1)}, bf16[4,128,384]{2,1,0:T(8,128)(2,1)S(1)}, u32[]{:S(2)}, u32[]{:S(2)}) collective-permute-start(bf16[4,128,384]{2,1,0:T(8,128)(2,1)S(1)} %all-to-all-done.1.mine), channel_id=1, source_target_pairs={{0,1},{1,0},{2,3},{3,2},{4,5},{5,4},{6,7},{7,6},{8,9},{9,8},{10,11... | collective-permute-start | bytes 1179656 | tf_op jit(solution)/shard_map/ppermute | solution.py:33
  148.9 0.7 copy-start.5
  154.2 14.1 %all-to-all-start.2 = ((bf16[4,64,704]{2,1,0:T(8,128)(2,1)}), bf16[4,64,704]{2,1,0:T(8,128)(2,1)S(1)}, u32[]{:S(2)}, u32[]{:S(2)}) async-start(bf16[4,64,704]{2,1,0:T(8,128)(2,1)} %bitcast.82), calls=%async_computation.2 | async-start | bytes 786432 | tf_op jit(solution)/shard_map/all_to_all | solution.py:432
  157.8 23.2 %collective-permute-start.9 = (bf16[3,64,1408]{2,1,0:T(8,128)(2,1)S(1)}, bf16[3,64,1408]{2,1,0:T(8,128)(2,1)S(1)}, u32[]{:S(2)}, u32[]{:S(2)}) collective-permute-start(bf16[3,64,1408]{2,1,0:T(8,128)(2,1)S(1)} %broadcast_select_fusion), channel_id=1, source_target_pairs={{0,1},{1,0},{2,3},{3,2},{4,5},{5,4},{6,7},{7,6},{8,9},{9,8},{10,11... | collective-permute-start | bytes 1622024 | tf_op jit(solution)/shard_map/ppermute | solution.py:33
  169.7 35.3 %all-to-all-start.3 = ((bf16[64,8,768]{2,1,0:T(8,128)(2,1)}), bf16[64,8,768]{2,1,0:T(8,128)(2,1)S(1)}, u32[]{:S(2)}, u32[]{:S(2)}) async-start(bf16[64,8,768]{2,1,0:T(8,128)(2,1)} %fusion.7), calls=%async_computation.3 | async-start | bytes 1572864 | tf_op jit(solution)/shard_map/all_to_all | solution.py:438
  181.0 2.1 copy-start
  183.2 24.3 %copy-start.15 = (s32[1,2]{1,0:T(1,128)S(1)}, s32[1,2]{1,0:T(1,128)}, u32[]{:S(2)}) copy-start(s32[1,2]{1,0:T(1,128)} %param.17) | copy-start | bytes 28
  204.9 4.4 %copy-start.1 = (bf16[64,8,768]{2,1,0:T(8,128)(2,1)}, bf16[64,8,768]{2,1,0:T(8,128)(2,1)S(1)}, u32[]{:S(2)}) copy-start(bf16[64,8,768]{2,1,0:T(8,128)(2,1)S(1)} %all-to-all-done.3) | copy-start | bytes 2359300
  204.9 4.4 %collective-permute-start.10 = (bf16[512,768]{1,0:T(8,128)(2,1)S(1)}, bf16[512,768]{1,0:T(8,128)(2,1)S(1)}, u32[]{:S(2)}, u32[]{:S(2)}) collective-permute-start(bf16[512,768]{1,0:T(8,128)(2,1)S(1)} %bitcast.79), channel_id=1, source_target_pairs={{0,1},{1,0},{2,3},{3,2},{4,5},{5,4},{6,7},{7,6},{8,9},{9,8},{10,11... | collective-permute-start | bytes 2359304 | tf_op jit(solution)/shard_map/ppermute | solution.py:33
  209.4 0.9 copy-start.3
  226.2 1.7 collective-permute-start.11
  (2 other events, 1.3 us)
Sparse Core Ops, SparseCore 0:
  30.0 72.7 all-gather.2
  105.3 78.8 all-gather.4

commit v10 on v9

--- a/solution.py
+++ b/solution.py
@@ -131,8 +131,17 @@
 
 def vision_block(at, part, info, values, weights_hbm, out, weights, heads, sem):
     base = at - at % 128
-    load = pltpu.make_async_copy(weights_hbm.at[:, base : base + weights.shape[1]], weights, sem)
-    load.start()
+    cut = at - base + 2 * part
+    cut = cut + -cut % 128
+    span = weights.shape[1]
+    early = pltpu.make_async_copy(
+        weights_hbm.at[:, base : base + cut], weights.at[:, :cut], sem.at[0]
+    )
+    late = pltpu.make_async_copy(
+        weights_hbm.at[:, base + cut : base + span], weights.at[:, cut:], sem.at[1]
+    )
+    early.start()
+    late.start()
     rows = values.shape[0]
 
     def image_of(row):
@@ -146,9 +155,11 @@
     asked = image_of(lax.broadcasted_iota(jnp.int32, (1, rows), 1))
     allowed = jnp.where(asking == asked, 1.0, 0.0)
     heads[...] = jnp.zeros(heads.shape, F32)
-    load.wait()
+    early.wait()
     triple = []
     for member in range(3):
+        if member == 2:
+            late.wait()
         begin = at - base + member * part
         end = begin + part
         low = begin - begin % 128
@@ -178,7 +189,7 @@
         scratch_shapes=[
             pltpu.VMEM((width, end + pad_to(end) - (at - at % 128)), BF),
             pltpu.VMEM((rows, part + pad_to(part)), F32),
-            pltpu.SemaphoreType.DMA,
+            pltpu.SemaphoreType.DMA((2,)),
         ],
         compiler_params=pltpu.CompilerParams(vmem_limit_bytes=56 << 20),
     )(info, values, weights)

time: 237 us -> 235 us (level)
  waiting for transfers between devices: 103 us -> 98.5 us
    all_to_all x1, waiting for transfers between devices: 17.8 us -> 13.9 us  [shards(): lax.all_to_all(sent.reshape(pieces, slots, half + pad_to(half)), TOK, spl...]
    ppermute x5, starting transfers between devices: 7.54 us -> 11.4 us  [swap_sub(): return lax.ppermute(value, 'sub', [(0, 1), (1, 0)])]
where the time goes in v10:
time: 235 us; the launch traced here: 234 us
  waiting for transfers between devices  98.5 us (42%)
  starting transfers between devices  53 us (23%)
  Pallas kernels  39.6 us (17%)
  between operations  13.8 us (6%)
  local copies, waits for them, and re-layouts  12.4 us (5%)
  other arithmetic  11.4 us (5%)
  matrix products  5.32 us (2%)
    ppermute x3, waiting for transfers between devices, shards(): lax.ppermute(mine, 'zh', [(i, (i + s) % lines) for i in range(lines)])  25.4 us
    all_gather x1, waiting for transfers between devices, shards(): full_v = lax.all_gather(line_v, PLANE, axis=0, tiled=True)  18.7 us
    ppermute x1, waiting for transfers between devices, shards(): paired = lax.ppermute(marked, 'grp', pair)  16.1 us
    pallas_call x1, Pallas kernels, run_decoder_block(): pl.pallas_call(functools.partial(decoder_block, half, cap), out_shape=[ja...  15.9 us
    all_to_all x1, waiting for transfers between devices, shards(): lax.all_to_all(sent.reshape(pieces, slots, half + pad_to(half)), TOK, spl...  13.9 us
    pallas_call x2, Pallas kernels, run_vision_block(): pl.pallas_call(functools.partial(vision_block, at, part), out_shape=jax.S...  11.8 us
    ppermute x5, starting transfers between devices, swap_sub(): return lax.ppermute(value, 'sub', [(0, 1), (1, 0)])  11.4 us
    all_to_all x1, waiting for transfers between devices, shards(): lax.all_to_all(partial, 'zh', split_axis=0, concat_axis=0, tiled=True)  9.96 us
  transfers between devices with their start and end apart: 18, of which 11 were waited for; matrix products, arithmetic and copies ran while one was open for 8% of the time, Pallas kernels for 10%

profile of v10, /device:TPU:1, one launch (start us, length us, event | category | flops | bytes accessed | tf_op | source)
XLA Modules:
  0.0 234.1 jit_solution(14848388074689352807)
XLA Ops:
  6.5 1.2 reshape.317
  9.7 9.0 %all-to-all-start = ((bf16[4,22,1760]{2,1,0:T(8,128)(2,1)}), bf16[4,22,1760]{2,1,0:T(8,128)(2,1)S(1)}, u32[]{:S(2)}, u32[]{:S(2)}) async-start(bf16[4,22,1760]{2,1,0:T(8,128)(2,1)} %broadcast_in_dim.11), calls=%async_computation | async-start | bytes 688128 | tf_op jit(solution)/shard_map/all_to_all | solution.py:57
  20.9 3.6 %fusion.reorder = bf16[1408,1408]{1,0:T(8,128)(2,1)} fusion(s32[1408]{0:T(1024)S(1)} %fusion.31), kind=kLoop, calls=%fused_computation.1 | loop fusion | flops 3964928 | bytes 3970560 | tf_op jit(solution)/shard_map/convert_element_type | solution.py:383
  26.4 2.1 collective-permute-done
  29.9 1.5 collective-permute-start.7
  31.4 4.4 %collective-permute-start.6 = (bf16[112,1408]{1,0:T(8,128)(2,1)S(1)}, bf16[112,1408]{1,0:T(8,128)(2,1)S(1)}, u32[]{:S(2)}, u32[]{:S(2)}) collective-permute-start(bf16[112,1408]{1,0:T(8,128)(2,1)S(1)} %maximum_maximum_fusion), channel_id=1, source_target_pairs={{0,4},{2,6},{4,0},{6,2},{1,5},{3,7},{5,1},{7,3},{8,12},{10,14},{12... | collective-permute-start | bytes 946184 | tf_op jit(solution)/shard_map/ppermute | solution.py:415
  35.8 2.5 %collective-permute-start.5 = (bf16[112,1408]{1,0:T(8,128)(2,1)S(1)}, bf16[112,1408]{1,0:T(8,128)(2,1)S(1)}, u32[]{:S(2)}, u32[]{:S(2)}) collective-permute-start(bf16[112,1408]{1,0:T(8,128)(2,1)S(1)} %maximum_maximum_fusion), channel_id=1, source_target_pairs={{0,6},{2,0},{4,2},{6,4},{1,7},{3,1},{5,3},{7,5},{8,14},{10,8},{12,... | collective-permute-start | bytes 946184 | tf_op jit(solution)/shard_map/ppermute | solution.py:415
  38.3 25.4 %collective-permute-done.5 = bf16[112,1408]{1,0:T(8,128)(2,1)S(1)} collective-permute-done((bf16[112,1408]{1,0:T(8,128)(2,1)S(1)}, bf16[112,1408]{1,0:T(8,128)(2,1)S(1)}, u32[]{:S(2)}, u32[]{:S(2)}) %collective-permute-start.5) | collective-permute-done | bytes 315424 | tf_op jit(solution)/shard_map/ppermute | solution.py:415
  66.7 16.1 %collective-permute-done.1 = bf16[272,1408]{1,0:T(8,128)(2,1)S(1)} collective-permute-done((bf16[272,1408]{1,0:T(8,128)(2,1)S(1)}, bf16[272,1408]{1,0:T(8,128)(2,1)S(1)}, u32[]{:S(2)}, u32[]{:S(2)}) %collective-permute-start.1) | collective-permute-done | bytes 765984 | tf_op jit(solution)/shard_map/ppermute | solution.py:433
  84.2 18.7 %all-gather.3.cloned.1.call-done.weights_hbm = bf16[1408,2560]{1,0:T(8,128)(2,1)} async-done(((bf16[88,2560]{1,0:T(8,128)(2,1)}), bf16[1408,2560]{1,0:T(8,128)(2,1)}) %all-gather.3.cloned.1.call-update) | async-done | bytes 7208976 | tf_op jit(solution)/shard_map/all_gather | solution.py:397
  102.8 5.9 %shard_map.101 = bf16[256,384]{1,0:T(8,128)(2,1)} custom-call(s32[4]{0:T(128)} %fusion.53.info, bf16[256,1408]{1,0:T(8,128)(2,1)} %slice.89.values, bf16[1408,2560]{1,0:T(8,128)(2,1)} %all-gather.3.cloned.1.call-done.weights_hbm), custom_call_target="tpu_custom_call" | custom-call | tf_op jit(solution)/shard_map/pallas_call | solution.py:183
  108.8 1.5 collective-permute-start.2
  110.3 5.9 %shard_map.100.own = bf16[256,384]{1,0:T(8,128)(2,1)} custom-call(s32[4]{0:T(128)} %bitcast.87, bf16[256,1408]{1,0:T(8,128)(2,1)} %slice.70.values, bf16[1408,2560]{1,0:T(8,128)(2,1)} %all-gather.3.cloned.1.call-done.weights_hbm), custom_call_target="tpu_custom_call" | custom-call | tf_op jit(solution)/shard_map/pallas_call | solution.py:183
  116.9 4.6 %shard_map.102 = (bf16[128,1408]{1,0:T(8,128)(2,1)}, bf16[128,1408]{1,0:T(8,128)(2,1)}) custom-call(s32[2]{0:T(128)} %pad_add_fusion.1.info, bf16[256,384]{1,0:T(8,128)(2,1)} %shard_map.100.own, bf16[256,384]{1,0:T(8,128)(2,1)} %copy-done.8, bf16[1408,2560]{1,0:T(8,128)(2,1)} %all-gather.3.cloned.1.call-done.weights_hbm), custom_call_target="tpu_custom_call" | custom-call | tf_op jit(solution)/shard_map/pallas_call | solution.py:220
  122.6 1.5 collective-permute-done.3.other
  124.8 2.8 %shard_map.103 = bf16[4,128,384]{2,1,0:T(8,128)(2,1)} custom-call(bf16[128,1408]{1,0:T(8,128)(2,1)} %bitcast.83, bf16[128,1408]{1,0:T(8,128)(2,1)} %get-tuple-element.19.keep, bf16[128,1408]{1,0:T(8,128)(2,1)} %copy-done.7), custom_call_target="tpu_custom_call" | custom-call | tf_op jit(solution)/shard_map/pallas_call | solution.py:255
  127.7 6.0 %all-to-all-start.1 = ((bf16[4,128,384]{2,1,0:T(8,128)(2,1)}), bf16[4,128,384]{2,1,0:T(8,128)(2,1)S(1)}, u32[]{:S(2)}, u32[]{:S(2)}) async-start(bf16[4,128,384]{2,1,0:T(8,128)(2,1)} %shard_map.103), calls=%async_computation.1 | async-start | bytes 786432 | tf_op jit(solution)/shard_map/all_to_all | solution.py:440
  133.8 3.1 %collective-permute-start.8 = (bf16[3,64,1408]{2,1,0:T(8,128)(2,1)S(1)}, bf16[3,64,1408]{2,1,0:T(8,128)(2,1)S(1)}, u32[]{:S(2)}, u32[]{:S(2)}) collective-permute-start(bf16[3,64,1408]{2,1,0:T(8,128)(2,1)S(1)} %pad_maximum_fusion.1), channel_id=1, source_target_pairs={{0,8},{8,16},{16,24},{24,32},{32,40},{40,48},{48,56},{56,64},{64,7... | collective-permute-start | bytes 1622024 | tf_op jit(solution)/shard_map/ppermute | solution.py:425
  136.9 7.6 %all-to-all-done.1.mine = bf16[4,128,384]{2,1,0:T(8,128)(2,1)S(1)} async-done(((bf16[4,128,384]{2,1,0:T(8,128)(2,1)}), bf16[4,128,384]{2,1,0:T(8,128)(2,1)S(1)}, u32[]{:S(2)}, u32[]{:S(2)}) %all-to-all-start.1) | async-done | bytes 393248 | tf_op jit(solution)/shard_map/all_to_all | solution.py:440
  144.5 3.4 %collective-permute-start.4 = (bf16[4,128,384]{2,1,0:T(8,128)(2,1)S(1)}, bf16[4,128,384]{2,1,0:T(8,128)(2,1)S(1)}, u32[]{:S(2)}, u32[]{:S(2)}) collective-permute-start(bf16[4,128,384]{2,1,0:T(8,128)(2,1)S(1)} %all-to-all-done.1.mine), channel_id=1, source_target_pairs={{0,1},{1,0},{2,3},{3,2},{4,5},{5,4},{6,7},{7,6},{8,9},{9,8},{10,11... | collective-permute-start | bytes 1179656 | tf_op jit(solution)/shard_map/ppermute | solution.py:33
  150.0 4.5 %shard_map.104 = bf16[256,704]{1,0:T(8,128)(2,1)} custom-call(s32[2]{0:T(128)} %pad_add_fusion.1.info, bf16[4,128,384]{2,1,0:T(8,128)(2,1)} %copy-done.2, bf16[4,128,384]{2,1,0:T(8,128)(2,1)} %copy-done.5, bf16[1408,2560]{1,0:T(8,128)(2,1)} %all-gather.3.cloned.1.call-done.weights_hbm), custom_call_target="tpu_custom_call" | custom-call | tf_op jit(solution)/shard_map/pallas_call | solution.py:285
  154.5 3.5 %all-to-all-start.2 = ((bf16[4,64,704]{2,1,0:T(8,128)(2,1)}), bf16[4,64,704]{2,1,0:T(8,128)(2,1)S(1)}, u32[]{:S(2)}, u32[]{:S(2)}) async-start(bf16[4,64,704]{2,1,0:T(8,128)(2,1)} %bitcast.82), calls=%async_computation.2 | async-start | bytes 786432 | tf_op jit(solution)/shard_map/all_to_all | solution.py:443
  158.6 10.0 %all-to-all-done.2 = bf16[4,64,704]{2,1,0:T(8,128)(2,1)S(1)} async-done(((bf16[4,64,704]{2,1,0:T(8,128)(2,1)}), bf16[4,64,704]{2,1,0:T(8,128)(2,1)S(1)}, u32[]{:S(2)}, u32[]{:S(2)}) %all-to-all-start.2) | async-done | bytes 360480 | tf_op jit(solution)/shard_map/all_to_all | solution.py:443
  168.7 1.4 fusion.7
  170.0 9.2 %all-to-all-start.3 = ((bf16[64,8,768]{2,1,0:T(8,128)(2,1)}), bf16[64,8,768]{2,1,0:T(8,128)(2,1)S(1)}, u32[]{:S(2)}, u32[]{:S(2)}) async-start(bf16[64,8,768]{2,1,0:T(8,128)(2,1)} %fusion.7), calls=%async_computation.3 | async-start | bytes 1572864 | tf_op jit(solution)/shard_map/all_to_all | solution.py:449
  179.5 1.8 copy-done
  181.3 4.0 %convolution_convert_fusion.text = bf16[512,1408]{1,0:T(8,128)(2,1)} fusion(bf16[1408,1408]{1,0:T(8,128)(2,1)S(1)} %copy-done, bf16[128,1408]{1,0:T(8,128)(2,1)S(1)} %copy-done.6, bf16[384,1408]{1,0:T(8,128)(2,1)S(1)} %bitcast.84), kind=kOutput, calls=%fused_computation.2 | convolution fusion | flops 2033647616 | bytes 6848512 | tf_op jit(solution)/shard_map/dot_general | solution.py:37
  185.3 13.9 %all-to-all-done.3 = bf16[64,8,768]{2,1,0:T(8,128)(2,1)S(1)} async-done(((bf16[64,8,768]{2,1,0:T(8,128)(2,1)}), bf16[64,8,768]{2,1,0:T(8,128)(2,1)S(1)}, u32[]{:S(2)}, u32[]{:S(2)}) %all-to-all-start.3) | async-done | bytes 786464 | tf_op jit(solution)/shard_map/all_to_all | solution.py:449
  199.2 6.0 %collective-permute-start.10 = (bf16[512,768]{1,0:T(8,128)(2,1)S(1)}, bf16[512,768]{1,0:T(8,128)(2,1)S(1)}, u32[]{:S(2)}, u32[]{:S(2)}) collective-permute-start(bf16[512,768]{1,0:T(8,128)(2,1)S(1)} %bitcast.79), channel_id=1, source_target_pairs={{0,1},{1,0},{2,3},{3,2},{4,5},{5,4},{6,7},{7,6},{8,9},{9,8},{10,11... | collective-permute-start | bytes 2359304 | tf_op jit(solution)/shard_map/ppermute | solution.py:33
  207.9 15.9 %shard_map.105 = (bf16[64,1408]{1,0:T(8,128)(2,1)}, bf16[64,1408]{1,0:T(8,128)(2,1)}) custom-call(s32[4]{0:T(128)} %pad_add_fusion.info, bf16[512,768]{1,0:T(8,128)(2,1)} %bitcast.80, bf16[512,768]{1,0:T(8,128)(2,1)} %copy-done.3, bf16[512,1408]{1,0:T(8,128)(2,1)} %convolution_convert_fusion.text, bf16[1408,1408]{1,0:T(8,128)(2,1)} %fusion.reorder, ...), custom_call_target="tpu_custom_call" | custom-call | tf_op jit(solution)/shard_map/pallas_call | solution.py:303
  224.3 1.3 collective-permute-done.11
  225.6 1.6 add_convert_fusion
  (117 shorter events, 20.5 us)
Async XLA Ops:
  6.5 12.2 %copy-start.10 = (bf16[11,1,3,704]{3,2,1,0:T(4,128)(2,1)S(1)}, bf16[11,1,3,704]{3,2,1,0:T(4,128)(2,1)}, u32[]{:S(2)}) copy-start(bf16[11,1,3,704]{3,2,1,0:T(4,128)(2,1)} %param.18) | copy-start | bytes 139396
  6.5 12.3 %copy-start.11 = (bf16[704,11]{0,1:T(8,128)(2,1)S(1)}, bf16[704,11]{0,1:T(8,128)(2,1)}, u32[]{:S(2)}) copy-start(bf16[704,11]{0,1:T(8,128)(2,1)} %param.19) | copy-start | bytes 46468
  6.5 13.2 %copy-start.4 = (bf16[256,1408]{1,0:T(8,128)(2,1)S(1)}, bf16[256,1408]{1,0:T(8,128)(2,1)}, u32[]{:S(2)}) copy-start(bf16[256,1408]{1,0:T(8,128)(2,1)} %param.10) | copy-start | bytes 2162692
  9.7 19.1 %all-to-all-start = ((bf16[4,22,1760]{2,1,0:T(8,128)(2,1)}), bf16[4,22,1760]{2,1,0:T(8,128)(2,1)S(1)}, u32[]{:S(2)}, u32[]{:S(2)}) async-start(bf16[4,22,1760]{2,1,0:T(8,128)(2,1)} %broadcast_in_dim.11), calls=%async_computation | async-start | bytes 688128 | tf_op jit(solution)/shard_map/all_to_all | solution.py:57
  18.7 84.1 %all-gather.3.cloned.1.call-start = ((), (), s32[]{:S(2)}) async-start(), calls=%async_computation.4 | async-start | bytes 7659520 | tf_op jit(solution)/shard_map/all_gather | solution.py:397
  19.0 9.5 %collective-permute-start = (bf16[2,11,1408]{2,1,0:T(8,128)(2,1)S(1)}, bf16[2,11,1408]{2,1,0:T(8,128)(2,1)S(1)}, u32[]{:S(2)}, u32[]{:S(2)}) collective-permute-start(bf16[2,11,1408]{2,1,0:T(8,128)(2,1)S(1)} %pad_maximum_fusion.5), channel_id=1, source_target_pairs={{0,128},{128,0},{1,129},{129,1},{2,130},{130,2},{3,131},{131,3},{4... | collective-permute-start | bytes 185864 | tf_op jit(solution)/shard_map/ppermute | solution.py:360
  20.8 3.7 %copy-start.12 = (s32[4,1]{0,1:T(1,128)}, s32[4,1]{0,1:T(1,128)S(1)}, u32[]{:S(2)}) copy-start(s32[4,1]{0,1:T(1,128)S(1)} %reduce-window.15) | copy-start | bytes 52
  20.9 3.6 %copy-start.6 = (bf16[128,1408]{1,0:T(8,128)(2,1)S(1)}, bf16[128,1408]{1,0:T(8,128)(2,1)}, u32[]{:S(2)}) copy-start(bf16[128,1408]{1,0:T(8,128)(2,1)} %param.15) | copy-start | bytes 1081348
  25.3 0.9 copy-start.9
  29.9 176.1 %all-gather.5.cloned.1.call-start = ((), (), s32[]{:S(2)}) async-start(), calls=%async_computation.5 | async-start | bytes 8425472 | tf_op jit(solution)/shard_map/all_gather | solution.py:420
  29.9 33.8 %collective-permute-start.7 = (bf16[112,1408]{1,0:T(8,128)(2,1)S(1)}, bf16[112,1408]{1,0:T(8,128)(2,1)S(1)}, u32[]{:S(2)}, u32[]{:S(2)}) collective-permute-start(bf16[112,1408]{1,0:T(8,128)(2,1)S(1)} %maximum_maximum_fusion), channel_id=1, source_target_pairs={{0,2},{2,4},{4,6},{6,0},{1,3},{3,5},{5,7},{7,1},{8,10},{10,12},{12... | collective-permute-start | bytes 946184 | tf_op jit(solution)/shard_map/ppermute | solution.py:415
  31.4 32.3 %collective-permute-start.6 = (bf16[112,1408]{1,0:T(8,128)(2,1)S(1)}, bf16[112,1408]{1,0:T(8,128)(2,1)S(1)}, u32[]{:S(2)}, u32[]{:S(2)}) collective-permute-start(bf16[112,1408]{1,0:T(8,128)(2,1)S(1)} %maximum_maximum_fusion), channel_id=1, source_target_pairs={{0,4},{2,6},{4,0},{6,2},{1,5},{3,7},{5,1},{7,3},{8,12},{10,14},{12... | collective-permute-start | bytes 946184 | tf_op jit(solution)/shard_map/ppermute | solution.py:415
  35.8 27.8 %collective-permute-start.5 = (bf16[112,1408]{1,0:T(8,128)(2,1)S(1)}, bf16[112,1408]{1,0:T(8,128)(2,1)S(1)}, u32[]{:S(2)}, u32[]{:S(2)}) collective-permute-start(bf16[112,1408]{1,0:T(8,128)(2,1)S(1)} %maximum_maximum_fusion), channel_id=1, source_target_pairs={{0,6},{2,0},{4,2},{6,4},{1,7},{3,1},{5,3},{7,5},{8,14},{10,8},{12,... | collective-permute-start | bytes 946184 | tf_op jit(solution)/shard_map/ppermute | solution.py:415
  63.9 1.7 copy-start.14
  64.9 17.8 %collective-permute-start.1 = (bf16[272,1408]{1,0:T(8,128)(2,1)S(1)}, bf16[272,1408]{1,0:T(8,128)(2,1)S(1)}, u32[]{:S(2)}, u32[]{:S(2)}) collective-permute-start(bf16[272,1408]{1,0:T(8,128)(2,1)S(1)} %fusion.8), channel_id=1, source_target_pairs={{0,128},{128,0},{1,129},{129,1},{2,130},{130,2},{3,131},{131,3},{4... | collective-permute-start | bytes 2297864 | tf_op jit(solution)/shard_map/ppermute | solution.py:433
  108.8 7.5 %collective-permute-start.2 = (bf16[256,384]{1,0:T(8,128)(2,1)}, bf16[256,384]{1,0:T(8,128)(2,1)S(1)}, u32[]{:S(2)}, u32[]{:S(2)}) collective-permute-start(bf16[256,384]{1,0:T(8,128)(2,1)} %shard_map.101), channel_id=1, source_target_pairs={{0,128},{128,0},{1,129},{129,1},{2,130},{130,2},{3,131},{131,3},{4... | collective-permute-start | bytes 589832 | tf_op jit(solution)/shard_map/ppermute | solution.py:437
  121.6 2.5 %collective-permute-start.3 = (bf16[128,1408]{1,0:T(8,128)(2,1)}, bf16[128,1408]{1,0:T(8,128)(2,1)S(1)}, u32[]{:S(2)}, u32[]{:S(2)}) collective-permute-start(bf16[128,1408]{1,0:T(8,128)(2,1)} %get-tuple-element.20), channel_id=1, source_target_pairs={{0,1},{1,0},{2,3},{3,2},{4,5},{5,4},{6,7},{7,6},{8,9},{9,8},{10,11... | collective-permute-start | bytes 1081352 | tf_op jit(solution)/shard_map/ppermute | solution.py:33
  124.1 0.7 copy-start.7
  127.7 16.8 %all-to-all-start.1 = ((bf16[4,128,384]{2,1,0:T(8,128)(2,1)}), bf16[4,128,384]{2,1,0:T(8,128)(2,1)S(1)}, u32[]{:S(2)}, u32[]{:S(2)}) async-start(bf16[4,128,384]{2,1,0:T(8,128)(2,1)} %shard_map.103), calls=%async_computation.1 | async-start | bytes 786432 | tf_op jit(solution)/shard_map/all_to_all | solution.py:440
  133.8 24.2 %collective-permute-start.8 = (bf16[3,64,1408]{2,1,0:T(8,128)(2,1)S(1)}, bf16[3,64,1408]{2,1,0:T(8,128)(2,1)S(1)}, u32[]{:S(2)}, u32[]{:S(2)}) collective-permute-start(bf16[3,64,1408]{2,1,0:T(8,128)(2,1)S(1)} %pad_maximum_fusion.1), channel_id=1, source_target_pairs={{0,8},{8,16},{16,24},{24,32},{32,40},{40,48},{48,56},{56,64},{64,7... | collective-permute-start | bytes 1622024 | tf_op jit(solution)/shard_map/ppermute | solution.py:425
  144.5 4.8 %copy-start.2 = (bf16[4,128,384]{2,1,0:T(8,128)(2,1)}, bf16[4,128,384]{2,1,0:T(8,128)(2,1)S(1)}, u32[]{:S(2)}) copy-start(bf16[4,128,384]{2,1,0:T(8,128)(2,1)S(1)} %all-to-all-done.1.mine) | copy-start | bytes 1179652
  144.5 4.8 %collective-permute-start.4 = (bf16[4,128,384]{2,1,0:T(8,128)(2,1)S(1)}, bf16[4,128,384]{2,1,0:T(8,128)(2,1)S(1)}, u32[]{:S(2)}, u32[]{:S(2)}) collective-permute-start(bf16[4,128,384]{2,1,0:T(8,128)(2,1)S(1)} %all-to-all-done.1.mine), channel_id=1, source_target_pairs={{0,1},{1,0},{2,3},{3,2},{4,5},{5,4},{6,7},{7,6},{8,9},{9,8},{10,11... | collective-permute-start | bytes 1179656 | tf_op jit(solution)/shard_map/ppermute | solution.py:33
  149.3 0.7 copy-start.5
  154.5 14.1 %all-to-all-start.2 = ((bf16[4,64,704]{2,1,0:T(8,128)(2,1)}), bf16[4,64,704]{2,1,0:T(8,128)(2,1)S(1)}, u32[]{:S(2)}, u32[]{:S(2)}) async-start(bf16[4,64,704]{2,1,0:T(8,128)(2,1)} %bitcast.82), calls=%async_computation.2 | async-start | bytes 786432 | tf_op jit(solution)/shard_map/all_to_all | solution.py:443
  158.1 21.1 %collective-permute-start.9 = (bf16[3,64,1408]{2,1,0:T(8,128)(2,1)S(1)}, bf16[3,64,1408]{2,1,0:T(8,128)(2,1)S(1)}, u32[]{:S(2)}, u32[]{:S(2)}) collective-permute-start(bf16[3,64,1408]{2,1,0:T(8,128)(2,1)S(1)} %broadcast_select_fusion), channel_id=1, source_target_pairs={{0,1},{1,0},{2,3},{3,2},{4,5},{5,4},{6,7},{7,6},{8,9},{9,8},{10,11... | collective-permute-start | bytes 1622024 | tf_op jit(solution)/shard_map/ppermute | solution.py:33
  170.0 29.2 %all-to-all-start.3 = ((bf16[64,8,768]{2,1,0:T(8,128)(2,1)}), bf16[64,8,768]{2,1,0:T(8,128)(2,1)S(1)}, u32[]{:S(2)}, u32[]{:S(2)}) async-start(bf16[64,8,768]{2,1,0:T(8,128)(2,1)} %fusion.7), calls=%async_computation.3 | async-start | bytes 1572864 | tf_op jit(solution)/shard_map/all_to_all | solution.py:449
  179.2 2.1 copy-start
  181.3 23.8 %copy-start.15 = (s32[1,2]{1,0:T(1,128)S(1)}, s32[1,2]{1,0:T(1,128)}, u32[]{:S(2)}) copy-start(s32[1,2]{1,0:T(1,128)} %param.17) | copy-start | bytes 28
  199.2 7.9 %copy-start.1 = (bf16[64,8,768]{2,1,0:T(8,128)(2,1)}, bf16[64,8,768]{2,1,0:T(8,128)(2,1)S(1)}, u32[]{:S(2)}) copy-start(bf16[64,8,768]{2,1,0:T(8,128)(2,1)S(1)} %all-to-all-done.3) | copy-start | bytes 2359300
  199.2 7.9 %collective-permute-start.10 = (bf16[512,768]{1,0:T(8,128)(2,1)S(1)}, bf16[512,768]{1,0:T(8,128)(2,1)S(1)}, u32[]{:S(2)}, u32[]{:S(2)}) collective-permute-start(bf16[512,768]{1,0:T(8,128)(2,1)S(1)} %bitcast.79), channel_id=1, source_target_pairs={{0,1},{1,0},{2,3},{3,2},{4,5},{5,4},{6,7},{7,6},{8,9},{9,8},{10,11... | collective-permute-start | bytes 2359304 | tf_op jit(solution)/shard_map/ppermute | solution.py:33
  207.1 0.9 copy-start.3
  223.9 1.7 collective-permute-start.11
  (2 other events, 1.3 us)
Sparse Core Ops, SparseCore 0:
  30.0 72.7 all-gather.2
  105.3 81.2 all-gather.4
